TPU v7x, 32 devices: a whole 2x2x4 slice. The times are simulated.
32 devices in a mesh: depth: 4 (over y, core), tile: 8 (over z, x).
Axes of the slice: x: 2, y: 2, z: 4, core: 2. Of those that a mesh axis runs over, the one named last changes fastest.
Arguments:
- density: float32 [16, 128, 2048], P('depth', 'tile'), may hold values from -6 to 6
- bins: int32 [16, 128, 2048], P('depth', 'tile'), may hold values from 0 to 255
- counts: int32 [4, 8], P('depth', 'tile'), may hold values from 0 to 4
- colors: bfloat16 [3, 256], replicated, may hold values from 0.049804688 to 1
- opacities: bfloat16 [256], replicated, may hold values from 0.0049743652 to 0.19921875
Outputs:
- image: float32 [4, 128, 2048], P(None, 'tile', 'depth')
Inputs may be any that keep to these rules, and one draw needn't show every extreme that they name: counts of brick (s, t) is the number of its leading slices that are occupied; its other slices are transparent.
All inputs are finite; a program needn't handle non-finite values.
Results may differ from a plain program's by a relative error of at most 0.0003.
Values sent between devices are 32-bit elements; how exact they have to be, the bound alone decides.
No kernel may reach another device: no remote copies, remote signals or barrier semaphores. Data moves between devices by JAX's collectives and lax.ppermute only.
A program may use at most 64 MiB of HBM per device.

v0:
```python
import jax
import jax.numpy as jnp
from jax import lax
from jax.sharding import PartitionSpec as P


def with_halo(block, sides, width):
    for axis, dim in sides:
        count = lax.axis_size(axis)
        forward = [(i, i + 1) for i in range(count - 1)]
        backward = [(target, source) for source, target in forward]
        low = lax.ppermute(
            lax.slice_in_dim(block, block.shape[dim] - width, None, axis=dim), axis, forward
        )
        high = lax.ppermute(lax.slice_in_dim(block, 0, width, axis=dim), axis, backward)
        block = jnp.concatenate([low, block, high], axis=dim)
    return block


def from_partner(x, axis, stride):
    return lax.ppermute(x, axis, [(i, i ^ 1 << stride) for i in range(lax.axis_size(axis))])


def lighting(padded):
    grad_depth = (padded[2:, 1:-1] - padded[:-2, 1:-1]) * 0.5
    grad_row = (padded[1:-1, 2:] - padded[1:-1, :-2]) * 0.5
    center = padded[1:-1, 1:-1]
    zero_col = jnp.zeros_like(center[:, :, :1])
    grad_col = (
        jnp.concatenate([center[:, :, 1:], zero_col], 2)
        - jnp.concatenate([zero_col, center[:, :, :-1]], 2)
    ) * 0.5
    magnitude = jnp.sqrt(grad_depth * grad_depth + grad_row * grad_row + grad_col * grad_col)
    facing = jnp.abs(0.64 * grad_depth + 0.6 * grad_row + 0.48 * grad_col)
    return 0.3 + 0.7 * facing / jnp.maximum(magnitude, 1.0)


def lookup_slice(transfer, slice_bins):
    flat_bins = slice_bins.reshape(2, -1)
    levels = lax.broadcasted_iota(jnp.int32, (transfer.shape[1], 1), 0)
    halves = []
    for portion in range(2):
        onehot = (flat_bins[portion][None, :] == levels).astype(jnp.bfloat16)
        halves.append(jnp.dot(transfer, onehot, preferred_element_type=jnp.float32))
    return jnp.concatenate(halves, 1).reshape((4,) + slice_bins.shape)


def over(front, back):
    return front + (1.0 - front[3:4]) * back


def on_device(density, bins, counts, colors, opacities):
    slices, rows, cols = density.shape
    transfer = jnp.concatenate([colors, opacities[None]], 0)
    padded = with_halo(density, (("depth", 0), ("tile", 1)), 1)
    shade = lighting(padded)
    count = counts[0, 0]
    looked = lax.map(lambda slice_bins: lookup_slice(transfer, slice_bins), bins)
    occupied = (jnp.arange(slices) < count).astype(jnp.float32)
    alpha = looked[:, 3] * occupied[:, None, None]
    shaded = looked[:, :3] * shade[:, None]
    passing = jnp.cumprod(1.0 - alpha, axis=0)
    before = jnp.concatenate([jnp.ones_like(passing[:1]), passing[:-1]], 0)
    weight = before * alpha
    colored = jnp.sum(weight[:, None] * shaded, axis=0)
    remaining = passing[-1]
    partial_image = jnp.concatenate([colored, (1.0 - remaining)[None]], 0)
    slab_count = lax.axis_size("depth")
    piece_cols = cols // slab_count
    current = partial_image.reshape(4, rows, slab_count, piece_cols)
    position = lax.axis_index("depth")
    rounds = slab_count.bit_length() - 1
    for level in range(rounds):
        pieces_left = current.shape[2]
        paired = current.reshape(4, rows, pieces_left // 2, 2, piece_cols)
        first_half = paired[:, :, :, 0]
        second_half = paired[:, :, :, 1]
        is_behind = position >> level & 1 == 1
        kept = jnp.where(is_behind, second_half, first_half)
        outgoing = jnp.where(is_behind, first_half, second_half)
        received = from_partner(outgoing, "depth", level)
        current = jnp.where(is_behind, over(received, kept), over(kept, received))
    return current.reshape(4, rows, piece_cols)


def solution(mesh):
    return jax.shard_map(
        on_device,
        mesh=mesh,
        in_specs=(P("depth", "tile", None), P("depth", "tile", None), P("depth", "tile"), P(), P()),
        out_specs=P(None, "tile", "depth"),
        check_vma=False,
    )
```

profile of v0, /device:TPU:0, one launch (start us, length us, event | category | flops | bytes accessed | tf_op | source)
XLA Modules:
  0.0 61.9 jit_solution(13355619172865646441)
XLA Ops:
  0.0 1.7 %fusion.17 = (f32[1,16,2048]{2,1,0:T(8,128)S(1)}, f32[1,16,2048]{2,1,0:T(8,128)}) fusion(f32[4,16,2048]{2,1,0:T(8,128)} %param.7), kind=kLoop, calls=%fused_computation.58 | loop fusion | bytes 524288 | tf_op jit(solution)/shard_map/slice | solution.py:15
  1.7 2.4 %collective-permute-start.1 = (f32[1,16,2048]{2,1,0:T(8,128)}, f32[1,16,2048]{2,1,0:T(8,128)S(1)}, u32[]{:S(2)}, u32[]{:S(2)}) collective-permute-start(f32[1,16,2048]{2,1,0:T(8,128)} %get-tuple-element.44), channel_id=1, source_target_pairs={{0,8},{8,16},{16,24},{1,9},{9,17},{17,25},{2,10},{10,18},{18,26},{... | collective-permute-start | bytes 393224 | tf_op jit(solution)/shard_map/ppermute | solution.py:12
  4.0 1.3 %collective-permute-start = (f32[1,16,2048]{2,1,0:T(8,128)S(1)}, f32[1,16,2048]{2,1,0:T(8,128)S(1)}, u32[]{:S(2)}, u32[]{:S(2)}) collective-permute-start(f32[1,16,2048]{2,1,0:T(8,128)S(1)} %get-tuple-element.43), channel_id=1, source_target_pairs={{8,0},{16,8},{24,16},{9,1},{17,9},{25,17},{10,2},{18,10},{26,18},{... | collective-permute-start | bytes 393224 | tf_op jit(solution)/shard_map/ppermute | solution.py:15
  5.3 2.2 %fusion.18 = (f32[4,16,2047]{2,1,0:T(8,128)S(1)}, f32[4,16,2047]{2,1,0:T(8,128)}) fusion(f32[4,16,2048]{2,1,0:T(8,128)} %param.7), kind=kLoop, calls=%fused_computation.59 | loop fusion | bytes 2096128 | tf_op jit(solution)/shard_map/slice | solution.py:30
  7.5 26.1 %while.10 = (s32[]{:T(128)}, f32[4,4,16,2048]{3,2,1,0:T(8,128)S(1)}, s32[4,16,2048]{2,1,0:T(8,128)}, bf16[4,256]{1,0:T(4,128)(2,1)S(1)}, s32[]{:T(128)}, /*index=5*/s32[]{:T(128)}, s32[]{}) while((s32[]{:T(128)}, f32[4,4,16,2048]{3,2,1,0:T(8,128)S(1)}, s32[4,16,2048]{2,1,0:T(8,128)}, bf16[4,256]{1,0:T(4,128)(2,1)S(1)}, s32[]{:T(128)}, ...), condition=%wide.region_1.2_spmd, body=%wide.region_0.1_spmd.sunk | while | flops 75628544 | bytes 3281005 | solution.py:58
  7.5 0.9 %dynamic-slice_bitcast_fusion.3 = (s32[1,16,8,128]{3,2,1,0:T(8,128)S(1)}, s32[1,16,8,128]{3,2,1,0:T(8,128)S(1)}) fusion(s32[4,16,2048]{2,1,0:T(8,128)} %get-tuple-element.92, s32[]{:T(128)S(6)} %copy.47, s32[]{:T(128)S(6)} %add.69), kind=kLoop, calls=%fused_computation.9.clone.1 | loop fusion | bytes 262152 | tf_op jit(solution)/shard_map/while
  8.5 2.6 %convolution_bitcast_fusion.4 = f32[4,16384]{1,0:T(4,128)S(1)} fusion(bf16[4,256]{1,0:T(4,128)(2,1)S(1)} %get-tuple-element.93, s32[16384]{0:T(1024)S(1)} %bitcast.94), kind=kOutput, calls=%fused_computation.clone.1 | convolution fusion | flops 37748736 | bytes 329728 | tf_op jit(solution)/shard_map/while/body/eval_jaxpr/dot_general | solution.py:44
  11.0 2.6 %convolution_bitcast_fusion.5 = f32[4,16384]{1,0:T(4,128)S(1)} fusion(bf16[4,256]{1,0:T(4,128)(2,1)S(1)} %get-tuple-element.93, s32[16384]{0:T(1024)S(1)} %bitcast.95), kind=kOutput, calls=%fused_computation.1.clone.1 | convolution fusion | flops 37748736 | bytes 329728 | tf_op jit(solution)/shard_map/while/body/eval_jaxpr/dot_general | solution.py:44
  15.0 2.6 %convolution_bitcast_fusion.4 = f32[4,16384]{1,0:T(4,128)S(1)} fusion(bf16[4,256]{1,0:T(4,128)(2,1)S(1)} %get-tuple-element.93, s32[16384]{0:T(1024)S(1)} %bitcast.94), kind=kOutput, calls=%fused_computation.clone.1 | convolution fusion | flops 37748736 | bytes 329728 | tf_op jit(solution)/shard_map/while/body/eval_jaxpr/dot_general | solution.py:44
  17.5 2.6 %convolution_bitcast_fusion.5 = f32[4,16384]{1,0:T(4,128)S(1)} fusion(bf16[4,256]{1,0:T(4,128)(2,1)S(1)} %get-tuple-element.93, s32[16384]{0:T(1024)S(1)} %bitcast.95), kind=kOutput, calls=%fused_computation.1.clone.1 | convolution fusion | flops 37748736 | bytes 329728 | tf_op jit(solution)/shard_map/while/body/eval_jaxpr/dot_general | solution.py:44
  21.5 2.6 %convolution_bitcast_fusion.4 = f32[4,16384]{1,0:T(4,128)S(1)} fusion(bf16[4,256]{1,0:T(4,128)(2,1)S(1)} %get-tuple-element.93, s32[16384]{0:T(1024)S(1)} %bitcast.94), kind=kOutput, calls=%fused_computation.clone.1 | convolution fusion | flops 37748736 | bytes 329728 | tf_op jit(solution)/shard_map/while/body/eval_jaxpr/dot_general | solution.py:44
  24.1 2.6 %convolution_bitcast_fusion.5 = f32[4,16384]{1,0:T(4,128)S(1)} fusion(bf16[4,256]{1,0:T(4,128)(2,1)S(1)} %get-tuple-element.93, s32[16384]{0:T(1024)S(1)} %bitcast.95), kind=kOutput, calls=%fused_computation.1.clone.1 | convolution fusion | flops 37748736 | bytes 329728 | tf_op jit(solution)/shard_map/while/body/eval_jaxpr/dot_general | solution.py:44
  28.0 2.6 %convolution_bitcast_fusion.4 = f32[4,16384]{1,0:T(4,128)S(1)} fusion(bf16[4,256]{1,0:T(4,128)(2,1)S(1)} %get-tuple-element.93, s32[16384]{0:T(1024)S(1)} %bitcast.94), kind=kOutput, calls=%fused_computation.clone.1 | convolution fusion | flops 37748736 | bytes 329728 | tf_op jit(solution)/shard_map/while/body/eval_jaxpr/dot_general | solution.py:44
  30.6 2.6 %convolution_bitcast_fusion.5 = f32[4,16384]{1,0:T(4,128)S(1)} fusion(bf16[4,256]{1,0:T(4,128)(2,1)S(1)} %get-tuple-element.93, s32[16384]{0:T(1024)S(1)} %bitcast.95), kind=kOutput, calls=%fused_computation.1.clone.1 | convolution fusion | flops 37748736 | bytes 329728 | tf_op jit(solution)/shard_map/while/body/eval_jaxpr/dot_general | solution.py:44
  34.5 0.9 %pad_multiply_fusion = f32[4,16,2048]{2,1,0:T(8,128)} fusion(f32[3,16,2048]{2,1,0:T(8,128)S(1)} %slice.102, f32[4,4,16,2048]{3,2,1,0:T(8,128)S(1)} %get-tuple-element.27, f32[4]{0:T(128)S(1)} %compare_convert_fusion), kind=kLoop, calls=%fused_computation.19 | loop fusion | flops 262144 | bytes 1441808 | tf_op jit(solution)/shard_map/mul | solution.py:64
  36.3 4.8 %collective-permute-start.3 = (f32[6,1,2048]{2,1,0:T(1,128)}, f32[6,1,2048]{2,1,0:T(1,128)}, u32[]{:S(2)}, u32[]{:S(2)}) collective-permute-start(f32[6,1,2048]{2,1,0:T(1,128)} %get-tuple-element.39), channel_id=1, source_target_pairs={{0,1},{1,2},{2,3},{3,4},{4,5},{5,6},{6,7},{8,9},{9,10},{10,11},{11... | collective-permute-start | bytes 147464 | tf_op jit(solution)/shard_map/ppermute | solution.py:12
  41.2 1.3 %collective-permute-start.2 = (f32[6,1,2048]{2,1,0:T(1,128)}, f32[6,1,2048]{2,1,0:T(1,128)}, u32[]{:S(2)}, u32[]{:S(2)}) collective-permute-start(f32[6,1,2048]{2,1,0:T(1,128)} %get-tuple-element.38), channel_id=1, source_target_pairs={{1,0},{2,1},{3,2},{4,3},{5,4},{6,5},{7,6},{9,8},{10,9},{11,10},{12... | collective-permute-start | bytes 147464 | tf_op jit(solution)/shard_map/ppermute | solution.py:15
  43.1 1.0 %concatenate.49 = f32[1,16,2,2,512]{4,3,2,1,0:T(2,128)S(1)} reshape(f32[1,16,2048]{2,1,0:T(8,128)} %slice_subtract_fusion) | data formatting | bytes 262144 | tf_op jit(solution)/shard_map/concatenate | solution.py:67
  44.2 3.3 %collective-permute-done.2 = f32[6,1,2048]{2,1,0:T(1,128)} collective-permute-done((f32[6,1,2048]{2,1,0:T(1,128)}, f32[6,1,2048]{2,1,0:T(1,128)}, u32[]{:S(2)}, u32[]{:S(2)}) %collective-permute-start.2) | collective-permute-done | bytes 49184 | tf_op jit(solution)/shard_map/ppermute | solution.py:15
  47.5 2.0 %divide_add_fusion = f32[4,16,2048]{2,1,0:T(8,128)S(1)} fusion(f32[4,16,2047]{2,1,0:T(8,128)} %get-tuple-element.46, f32[4,16,2047]{2,1,0:T(8,128)S(1)} %get-tuple-element.45, f32[6,16,2048]{2,1,0:T(8,128)} %copy-done.2, f32[6,1,2048]{2,1,0:T(1,128)} %collective-permute-done.3, f32[6,1,2048]{2,1,0:T(1,128)} %collective-permute-done.2, ...), kind=kLoop, calls=%fused_computation.18 | loop fusion | flops 3276800 | bytes 3243520 | tf_op jit(solution)/shard_map/add | solution.py:35
  50.9 1.1 %collective-permute-start.4 = (f32[4,16,2,512]{3,2,1,0:T(2,128)S(1)}, f32[4,16,2,512]{3,2,1,0:T(2,128)S(1)}, u32[]{:S(2)}, u32[]{:S(2)}) collective-permute-start(f32[4,16,2,512]{3,2,1,0:T(2,128)S(1)} %fusion.6), channel_id=1, source_target_pairs={{0,8},{8,0},{16,24},{24,16},{1,9},{9,1},{17,25},{25,17},{2,10},{10... | collective-permute-start | bytes 786440 | tf_op jit(solution)/shard_map/ppermute | solution.py:21
  52.0 1.1 %collective-permute-done.4 = f32[4,16,2,512]{3,2,1,0:T(2,128)S(1)} collective-permute-done((f32[4,16,2,512]{3,2,1,0:T(2,128)S(1)}, f32[4,16,2,512]{3,2,1,0:T(2,128)S(1)}, u32[]{:S(2)}, u32[]{:S(2)}) %collective-permute-start.4) | collective-permute-done | bytes 262176 | tf_op jit(solution)/shard_map/ppermute | solution.py:21
  53.6 3.5 %collective-permute-start.5 = (f32[4,16,1,512]{3,2,1,0:T(1,128)S(1)}, f32[4,16,1,512]{3,2,1,0:T(1,128)S(1)}, u32[]{:S(2)}, u32[]{:S(2)}) collective-permute-start(f32[4,16,1,512]{3,2,1,0:T(1,128)S(1)} %fusion.12), channel_id=1, source_target_pairs={{0,16},{8,24},{16,0},{24,8},{1,17},{9,25},{17,1},{25,9},{2,18},{10... | collective-permute-start | bytes 393224 | tf_op jit(solution)/shard_map/ppermute | solution.py:21
  57.2 3.8 %collective-permute-done.5 = f32[4,16,1,512]{3,2,1,0:T(1,128)S(1)} collective-permute-done((f32[4,16,1,512]{3,2,1,0:T(1,128)S(1)}, f32[4,16,1,512]{3,2,1,0:T(1,128)S(1)}, u32[]{:S(2)}, u32[]{:S(2)}) %collective-permute-start.5) | collective-permute-done | bytes 131104 | tf_op jit(solution)/shard_map/ppermute | solution.py:21
  (61 shorter events, 9.3 us)
Async XLA Ops:
  0.0 7.5 %copy-start.4 = (bf16[256]{0:T(256)(128)(2,1)S(1)}, bf16[256]{0:T(256)(128)(2,1)}, u32[]{:S(2)}) copy-start(bf16[256]{0:T(256)(128)(2,1)} %param.11) | copy-start | bytes 1540
  0.0 7.5 %copy-start.3 = (bf16[3,256]{1,0:T(4,128)(2,1)S(1)}, bf16[3,256]{1,0:T(4,128)(2,1)}, u32[]{:S(2)}) copy-start(bf16[3,256]{1,0:T(4,128)(2,1)} %param.10) | copy-start | bytes 4612
  1.7 33.8 %collective-permute-start.1 = (f32[1,16,2048]{2,1,0:T(8,128)}, f32[1,16,2048]{2,1,0:T(8,128)S(1)}, u32[]{:S(2)}, u32[]{:S(2)}) collective-permute-start(f32[1,16,2048]{2,1,0:T(8,128)} %get-tuple-element.44), channel_id=1, source_target_pairs={{0,8},{8,16},{16,24},{1,9},{9,17},{17,25},{2,10},{10,18},{18,26},{... | collective-permute-start | bytes 393224 | tf_op jit(solution)/shard_map/ppermute | solution.py:12
  4.0 31.5 %collective-permute-start = (f32[1,16,2048]{2,1,0:T(8,128)S(1)}, f32[1,16,2048]{2,1,0:T(8,128)S(1)}, u32[]{:S(2)}, u32[]{:S(2)}) collective-permute-start(f32[1,16,2048]{2,1,0:T(8,128)S(1)} %get-tuple-element.43), channel_id=1, source_target_pairs={{8,0},{16,8},{24,16},{9,1},{17,9},{25,17},{10,2},{18,10},{26,18},{... | collective-permute-start | bytes 393224 | tf_op jit(solution)/shard_map/ppermute | solution.py:15
  33.6 1.8 %copy-start = (f32[4,16,2048]{2,1,0:T(8,128)S(1)}, f32[4,16,2048]{2,1,0:T(8,128)}, u32[]{:S(2)}) copy-start(f32[4,16,2048]{2,1,0:T(8,128)} %param.7) | copy-start | bytes 1572868
  35.5 7.6 %copy-start.2 = (f32[6,16,2048]{2,1,0:T(8,128)}, f32[6,16,2048]{2,1,0:T(8,128)S(1)}, u32[]{:S(2)}) copy-start(f32[6,16,2048]{2,1,0:T(8,128)S(1)} %constant_dynamic-update-slice_fusion) | copy-start | bytes 2359300
  36.3 7.8 %collective-permute-start.3 = (f32[6,1,2048]{2,1,0:T(1,128)}, f32[6,1,2048]{2,1,0:T(1,128)}, u32[]{:S(2)}, u32[]{:S(2)}) collective-permute-start(f32[6,1,2048]{2,1,0:T(1,128)} %get-tuple-element.39), channel_id=1, source_target_pairs={{0,1},{1,2},{2,3},{3,4},{4,5},{5,6},{6,7},{8,9},{9,10},{10,11},{11... | collective-permute-start | bytes 147464 | tf_op jit(solution)/shard_map/ppermute | solution.py:12
  41.2 6.3 %collective-permute-start.2 = (f32[6,1,2048]{2,1,0:T(1,128)}, f32[6,1,2048]{2,1,0:T(1,128)}, u32[]{:S(2)}, u32[]{:S(2)}) collective-permute-start(f32[6,1,2048]{2,1,0:T(1,128)} %get-tuple-element.38), channel_id=1, source_target_pairs={{1,0},{2,1},{3,2},{4,3},{5,4},{6,5},{7,6},{9,8},{10,9},{11,10},{12... | collective-permute-start | bytes 147464 | tf_op jit(solution)/shard_map/ppermute | solution.py:15
  44.2 5.3 %copy-start.1 = (f32[4,16,2048]{2,1,0:T(8,128)S(1)}, f32[4,16,2048]{2,1,0:T(8,128)}, u32[]{:S(2)}) copy-start(f32[4,16,2048]{2,1,0:T(8,128)} %pad_multiply_fusion) | copy-start | bytes 1572868
  50.9 2.2 %collective-permute-start.4 = (f32[4,16,2,512]{3,2,1,0:T(2,128)S(1)}, f32[4,16,2,512]{3,2,1,0:T(2,128)S(1)}, u32[]{:S(2)}, u32[]{:S(2)}) collective-permute-start(f32[4,16,2,512]{3,2,1,0:T(2,128)S(1)} %fusion.6), channel_id=1, source_target_pairs={{0,8},{8,0},{16,24},{24,16},{1,9},{9,1},{17,25},{25,17},{2,10},{10... | collective-permute-start | bytes 786440 | tf_op jit(solution)/shard_map/ppermute | solution.py:21
  53.6 7.3 %collective-permute-start.5 = (f32[4,16,1,512]{3,2,1,0:T(1,128)S(1)}, f32[4,16,1,512]{3,2,1,0:T(1,128)S(1)}, u32[]{:S(2)}, u32[]{:S(2)}) collective-permute-start(f32[4,16,1,512]{3,2,1,0:T(1,128)S(1)} %fusion.12), channel_id=1, source_target_pairs={{0,16},{8,24},{16,0},{24,8},{1,17},{9,25},{17,1},{25,9},{2,18},{10... | collective-permute-start | bytes 393224 | tf_op jit(solution)/shard_map/ppermute | solution.py:21
where the time goes:
time: 62.4 us; the launch traced here: 61.9 us
  matrix products  20.4 us (33%)
  starting transfers between devices  14.3 us (23%)
  local copies, waits for them, and re-layouts  11.9 us (19%)
  waiting for transfers between devices  8.11 us (13%)
  other arithmetic  6.08 us (10%)
  between operations  0.98 us (2%)
    dot_general x8, matrix products, lookup_slice(): halves.append(jnp.dot(transfer, onehot, preferred_element_type=jnp.float32))  20.4 us
    ppermute x2, starting transfers between devices, with_halo(): lax.ppermute(lax.slice_in_dim(block, block.shape[dim] - width, None, axis...  7.19 us
    ppermute x2, waiting for transfers between devices, from_partner(): lax.ppermute(x, axis, [(i, i ^ 1 << stride) for i in range(lax.axis_size(...  4.81 us
    ppermute x2, starting transfers between devices, from_partner(): lax.ppermute(x, axis, [(i, i ^ 1 << stride) for i in range(lax.axis_size(...  4.55 us
    while x12, local copies, waits for them, and re-layouts  3.66 us
    ppermute x2, waiting for transfers between devices, with_halo(): lax.ppermute(lax.slice_in_dim(block, 0, width, axis=dim), axis, backward)  3.29 us
    ppermute x2, starting transfers between devices, with_halo(): lax.ppermute(lax.slice_in_dim(block, 0, width, axis=dim), axis, backward)  2.57 us
    slice x2, local copies, waits for them, and re-layouts, with_halo(): lax.slice_in_dim(block, 0, width, axis=dim)  2.47 us
  transfers between devices with their start and end apart: 6, of which 3 were waited for; matrix products, arithmetic and copies ran while one was open for 50% of the time, Pallas kernels for 0%

commit v1 on v0

v1 whole, which is shorter than its diff:
```python
import functools

import jax
import jax.numpy as jnp
from jax import lax
from jax.experimental import pallas as pl
from jax.experimental.pallas import tpu as pltpu
from jax.sharding import PartitionSpec as P

LANES = 128
SUBLANES = 8
COLOR_ONE = 4096.0
OPACITY_ONE = 32768.0
VMEM_LIMIT = 12 * 2**20


def vmem():
    return pl.BlockSpec(memory_space=pltpu.VMEM)


def smem():
    return pl.BlockSpec(memory_space=pltpu.SMEM)


def params():
    return pltpu.CompilerParams(vmem_limit_bytes=VMEM_LIMIT)


def cost(flops, nbytes):
    return pl.CostEstimate(flops=flops, bytes_accessed=nbytes, transcendentals=0)


def f32(*shape):
    return jax.ShapeDtypeStruct(shape, jnp.float32)


def faces_kernel(density, depth_even, depth_odd, row_even, row_odd):
    slices, rows, _ = density.shape
    depth_low = lax.axis_index("depth") & 1 == 0
    tile_low = lax.axis_index("tile") & 1 == 0
    first, last = density[0], density[slices - 1]
    depth_even[...] = jnp.where(depth_low, last, first)
    depth_odd[...] = jnp.where(depth_low, first, last)
    for k in range(slices):
        top, bottom = density[k, 0:1], density[k, rows - 1 : rows]
        row_even[k : k + 1] = jnp.where(tile_low, bottom, top)
        row_odd[k : k + 1] = jnp.where(tile_low, top, bottom)


def trade(x, axis, first):
    count = lax.axis_size(axis)
    pairs = [(i, i + 1) for i in range(first, count - 1, 2)]
    return lax.ppermute(x, axis, pairs + [(b, a) for a, b in pairs])


def whole_number(x, one):
    return (x.astype(jnp.float32) * one).astype(jnp.int32)


def weights_kernel(count, bins, colors, opacities, weighted, passed):
    slices, rows, cols = bins.shape
    color = whole_number(colors[...], COLOR_ONE)
    opacity = whole_number(opacities[...], OPACITY_ONE)
    words = [color[0:1] | (color[1:2] << 16), color[2:3] | (opacity << 16)]
    tables = [
        [jnp.broadcast_to(word[:, i : i + LANES], (SUBLANES, LANES)) for word in words]
        for i in range(0, word_count(colors), LANES)
    ]
    opacity_unit = [
        jnp.where(k < count[0, 0], 1.0 / OPACITY_ONE, 0.0).astype(jnp.float32)
        for k in range(slices)
    ]
    for r in range(0, rows, SUBLANES):
        for c in range(0, cols, LANES):
            at = (slice(r, r + SUBLANES), slice(c, c + LANES))
            before = jnp.full((SUBLANES, LANES), 1.0 / COLOR_ONE, jnp.float32)
            for k in range(slices):
                index = bins[(k, *at)]
                lane = index & (LANES - 1)
                found = [lane_lookup(tables[0][j], lane) for j in range(2)]
                for part in range(1, len(tables)):
                    here = index >= part * LANES
                    found = [
                        jnp.where(here, lane_lookup(tables[part][j], lane), found[j])
                        for j in range(2)
                    ]
                alpha = (found[1] >> 16).astype(jnp.float32) * opacity_unit[k]
                weight = before * alpha
                weighted[(0, k, *at)] = weight * (found[0] & 0xFFFF).astype(jnp.float32)
                weighted[(1, k, *at)] = weight * (found[0] >> 16).astype(jnp.float32)
                weighted[(2, k, *at)] = weight * (found[1] & 0xFFFF).astype(jnp.float32)
                before = before - weight
            passed[at] = before * COLOR_ONE


def word_count(colors):
    return colors.shape[1]


def lane_lookup(table, lane):
    return jnp.take_along_axis(table, lane, axis=1, mode="promise_in_bounds")


def shade_kernel(keeps, density, depth_even, depth_odd, row_even, row_odd, weighted, passed, image):
    slices, rows, cols = density.shape
    half, _, _, piece = image.shape
    me = lax.axis_index("depth")
    mine = me & 1
    depth_is_low = mine == 0
    tile_is_low = lax.axis_index("tile") & 1 == 0
    lane = lax.broadcasted_iota(jnp.int32, (SUBLANES, LANES), 1)
    sub = lax.broadcasted_iota(jnp.int32, (SUBLANES, LANES), 0)
    at_left, at_right = lane == 0, lane == LANES - 1
    at_top, at_bottom = sub == 0, sub == SUBLANES - 1
    groups = rows // SUBLANES

    for i in range(half):
        number = 2 * i + (mine if keeps else 1 - mine)
        for p in range(0, piece, LANES):
            start = pl.multiple_of(number * piece + p, LANES)
            left = pl.multiple_of(jnp.maximum(start - LANES, 0), LANES)
            right = pl.multiple_of(jnp.minimum(start + LANES, cols - LANES), LANES)
            has_left = jnp.where(start > 0, 1.0, 0.0).astype(jnp.float32)
            has_right = jnp.where(start + LANES < cols, 1.0, 0.0).astype(jnp.float32)
            here = pl.ds(start, LANES)
            even_rows, odd_rows = row_even[:, here], row_odd[:, here]
            above_rows = jnp.where(tile_is_low, odd_rows, even_rows)
            below_rows = jnp.where(tile_is_low, even_rows, odd_rows)
            for g in range(groups):
                at = (slice(g * SUBLANES, (g + 1) * SUBLANES), here)
                even_face, odd_face = depth_even[at], depth_odd[at]
                column = [jnp.where(depth_is_low, odd_face, even_face)]
                column += [density[(k, *at)] for k in range(slices)]
                column += [jnp.where(depth_is_low, even_face, odd_face)]
                sums = [jnp.zeros((SUBLANES, LANES), jnp.float32) for _ in range(3)]
                for k in range(slices):
                    v = column[k + 1]
                    band = slice(g * SUBLANES, (g + 1) * SUBLANES)
                    lv = density[k, band, pl.ds(left, LANES)] * has_left
                    rv = density[k, band, pl.ds(right, LANES)] * has_right
                    plus = jnp.where(at_right, pltpu.roll(rv, LANES - 1, 1), pltpu.roll(v, LANES - 1, 1))
                    minus = jnp.where(at_left, pltpu.roll(lv, 1, 1), pltpu.roll(v, 1, 1))
                    by_col = plus - minus
                    if g == 0:
                        edge = jnp.broadcast_to(above_rows[k : k + 1], (SUBLANES, LANES))
                    else:
                        edge = pltpu.roll(density[k, (g - 1) * SUBLANES : g * SUBLANES, here], 1, 0)
                    up = jnp.where(at_top, edge, pltpu.roll(v, 1, 0))
                    if g == groups - 1:
                        edge = jnp.broadcast_to(below_rows[k : k + 1], (SUBLANES, LANES))
                    else:
                        edge = pltpu.roll(density[k, (g + 1) * SUBLANES : (g + 2) * SUBLANES, here], SUBLANES - 1, 0)
                    down = jnp.where(at_bottom, edge, pltpu.roll(v, SUBLANES - 1, 0))
                    by_row = down - up
                    by_depth = column[k + 2] - column[k]
                    square = by_depth * by_depth + by_row * by_row + by_col * by_col
                    facing = jnp.abs(0.448 * by_depth + 0.42 * by_row + 0.336 * by_col)
                    shade = 0.3 + facing * lax.rsqrt(jnp.maximum(square, 4.0))
                    for channel in range(3):
                        sums[channel] = sums[channel] + weighted[(channel, k, *at)] * shade
                out = (slice(g * SUBLANES, (g + 1) * SUBLANES), slice(p, p + LANES))
                for channel in range(3):
                    image[(i, channel, *out)] = sums[channel]
                image[(i, 3, *out)] = 1.0 - passed[at]


def merge_kernel(level, last, kept, received, *outs):
    pieces = kept.shape[0]
    me = lax.axis_index("depth")
    behind = (me >> level) & 1 == 1

    def merged(piece):
        a, b = kept[piece], received[piece]
        front = jnp.where(behind, b, a)
        back = jnp.where(behind, a, b)
        return front + (1.0 - front[3:4]) * back

    if last:
        outs[0][...] = merged(0)
        return
    bit = (me >> (level + 1)) & 1
    for i in range(pieces // 2):
        outs[0][i] = merged(2 * i + bit)
        outs[1][i] = merged(2 * i + 1 - bit)


def on_device(density, bins, counts, colors, opacities):
    slices, rows, cols = density.shape
    slab_count = lax.axis_size("depth")
    half, piece = slab_count // 2, cols // slab_count
    pixels = rows * cols
    faces = pl.pallas_call(
        faces_kernel,
        out_shape=[f32(rows, cols), f32(rows, cols), f32(slices, cols), f32(slices, cols)],
        in_specs=[vmem()],
        out_specs=[vmem()] * 4,
        compiler_params=params(),
        name="faces",
    )(density)
    traded = [
        trade(faces[0], "depth", 0),
        trade(faces[1], "depth", 1),
        trade(faces[2], "tile", 0),
        trade(faces[3], "tile", 1),
    ]
    weighted, passed = pl.pallas_call(
        weights_kernel,
        out_shape=[f32(3, slices, rows, cols), f32(rows, cols)],
        in_specs=[smem(), vmem(), vmem(), vmem()],
        out_specs=[vmem(), vmem()],
        compiler_params=params(),
        cost_estimate=cost(64 * slices * pixels, 16 * slices * pixels),
        name="weights",
    )(counts, bins, colors, opacities[None])

    def shaded(keeps):
        return pl.pallas_call(
            functools.partial(shade_kernel, keeps),
            out_shape=f32(half, 4, rows, piece),
            in_specs=[vmem()] * 7,
            out_specs=vmem(),
            compiler_params=params(),
            cost_estimate=cost(20 * slices * pixels, 8 * slices * pixels),
            name="shade_kept" if keeps else "shade_sent",
        )(density, *traded, weighted, passed)

    outgoing = shaded(False)
    levels = slab_count.bit_length() - 1
    kept = shaded(True)
    for level in range(levels):
        partner = [(i, i ^ 1 << level) for i in range(slab_count)]
        received = lax.ppermute(outgoing, "depth", partner)
        last = level == levels - 1
        left = kept.shape[0] // 2
        shapes = [f32(4, rows, piece)] if last else [f32(left, 4, rows, piece)] * 2
        merged = pl.pallas_call(
            functools.partial(merge_kernel, level, last),
            out_shape=shapes,
            in_specs=[vmem()] * 2,
            out_specs=[vmem()] * len(shapes),
            compiler_params=params(),
            name="merge",
        )(kept, received)
        if last:
            return merged[0]
        kept, outgoing = merged


def solution(mesh):
    return jax.shard_map(
        on_device,
        mesh=mesh,
        in_specs=(P("depth", "tile", None), P("depth", "tile", None), P("depth", "tile"), P(), P()),
        out_specs=P(None, "tile", "depth"),
        check_vma=False,
    )
```

time: 62.4 us -> 22.8 us (0.37)
  the two profiles are of different devices: /device:TPU:0 before, /device:TPU:2 now
where the time goes in v1:
time: 22.8 us; the launch traced here: 22.5 us
  starting transfers between devices  9.59 us (42%)
  waiting for transfers between devices  5.16 us (23%)
  local copies, waits for them, and re-layouts  4.46 us (20%)
  Pallas kernels  2.54 us (11%)
  between operations  0.75 us (3%)
    ppermute x4, starting transfers between devices, trade(): return lax.ppermute(x, axis, pairs + [(b, a) for a, b in pairs])  5.73 us
    ppermute x2, waiting for transfers between devices, on_device(): received = lax.ppermute(outgoing, 'depth', partner)  5.15 us
    ppermute x2, starting transfers between devices, on_device(): received = lax.ppermute(outgoing, 'depth', partner)  3.86 us
    unnamed x8, local copies, waits for them, and re-layouts  3.8 us
    pallas_call x1, Pallas kernels, on_device(): pl.pallas_call(weights_kernel, out_shape=[f32(3, slices, rows, cols), f32...  1.03 us
    pallas_call x2, Pallas kernels, shaded(): pl.pallas_call(functools.partial(shade_kernel, keeps), out_shape=f32(half...  0.74 us
    pallas_call x2, Pallas kernels, on_device(): pl.pallas_call(functools.partial(merge_kernel, level, last), out_shape=sh...  0.73 us
    broadcast_in_dim x1, local copies, waits for them, and re-layouts, on_device(): opacities[None]  0.66 us
  transfers between devices with their start and end apart: 6, of which 2 were waited for; matrix products, arithmetic and copies ran while one was open for 3% of the time, Pallas kernels for 6%

profile of v1, /device:TPU:2, one launch (start us, length us, event | category | flops | bytes accessed | tf_op | source)
XLA Modules:
  0.0 22.5 jit_solution(14930407141340967735)
XLA Ops:
  0.0 0.0 copy-start
  0.0 1.0 %copy-done = f32[4,16,2048]{2,1,0:T(8,128)S(1)} copy-done((f32[4,16,2048]{2,1,0:T(8,128)S(1)}, f32[4,16,2048]{2,1,0:T(8,128)}, u32[]{:S(2)}) %copy-start) | copy-done | bytes 524312
  1.1 0.1 collective-permute-start
  1.2 0.7 %collective-permute-start.1 = (f32[16,2048]{1,0:T(8,128)S(1)}, f32[16,2048]{1,0:T(8,128)S(1)}, u32[]{:S(2)}, u32[]{:S(2)}) collective-permute-start(f32[16,2048]{1,0:T(8,128)S(1)} %get-tuple-element.14), channel_id=1, source_target_pairs={{8,16},{16,8},{9,17},{17,9},{10,18},{18,10},{11,19},{19,11},{12,20... | collective-permute-start | bytes 393224 | tf_op jit(solution)/shard_map/ppermute | solution.py:53
  1.8 0.1 collective-permute-start.2
  1.9 4.9 %collective-permute-start.3 = (f32[4,2048]{1,0:T(4,128)S(1)}, f32[4,2048]{1,0:T(4,128)S(1)}, u32[]{:S(2)}, u32[]{:S(2)}) collective-permute-start(f32[4,2048]{1,0:T(4,128)S(1)} %get-tuple-element.16), channel_id=1, source_target_pairs={{1,2},{3,4},{5,6},{2,1},{4,3},{6,5},{9,10},{11,12},{13,14},{10,9},... | collective-permute-start | bytes 98312 | tf_op jit(solution)/shard_map/ppermute | solution.py:53
  7.5 0.7 %broadcast_in_dim.3.opacities = bf16[1,256]{1,0:T(2,128)(2,1)S(1)} reshape(bf16[256]{0:T(256)(128)(2,1)} %param.9) | data formatting | bytes 1024 | tf_op jit(solution)/shard_map/broadcast_in_dim | solution.py:214
  8.2 0.0 copy-start.2
  8.2 1.0 %copy-done.2 = s32[4,16,2048]{2,1,0:T(8,128)S(1)} copy-done((s32[4,16,2048]{2,1,0:T(8,128)S(1)}, s32[4,16,2048]{2,1,0:T(8,128)}, u32[]{:S(2)}) %copy-start.2) | copy-done | bytes 524312
  9.2 0.7 %copy-done.3 = bf16[3,256]{1,0:T(4,128)(2,1)S(1)} copy-done((bf16[3,256]{1,0:T(4,128)(2,1)S(1)}, bf16[3,256]{1,0:T(4,128)(2,1)}, u32[]{:S(2)}) %copy-start.3) | copy-done | bytes 1560
  9.9 1.0 %weights.1 = (f32[3,4,16,2048]{3,2,1,0:T(8,128)S(1)}, f32[16,2048]{1,0:T(8,128)S(1)}) custom-call(s32[1,1]{1,0:T(1,128)S(6)} %copy.6.count, s32[4,16,2048]{2,1,0:T(8,128)S(1)} %copy-done.2, bf16[3,256]{1,0:T(4,128)(2,1)S(1)} %copy-done.3, bf16[1,256]{1,0:T(2,128)(2,1)S(1)} %broadcast_in_dim.3.opacities), custom_call_target="tpu_custom_call" | custom-call | flops 8388608 | bytes 2097152 | tf_op jit(solution)/shard_map/weights/pallas_call | solution.py:206
  10.9 0.0 collective-permute-done.2.row_even
  10.9 0.0 collective-permute-done.3.row_odd
  10.9 0.0 collective-permute-done.depth_even
  10.9 0.0 collective-permute-done.1.depth_odd
  11.0 0.0 copy-start.1
  11.0 1.0 %copy-done.1 = f32[4,16,2048]{2,1,0:T(8,128)S(1)} copy-done((f32[4,16,2048]{2,1,0:T(8,128)S(1)}, f32[4,16,2048]{2,1,0:T(8,128)}, u32[]{:S(2)}) %copy-start.1) | copy-done | bytes 524312
  12.0 0.4 %shade_sent.1 = f32[2,4,16,512]{3,2,1,0:T(8,128)S(1)} custom-call(f32[4,16,2048]{2,1,0:T(8,128)S(1)} %copy-done.1, f32[16,2048]{1,0:T(8,128)S(1)} %collective-permute-done.depth_even, f32[16,2048]{1,0:T(8,128)S(1)} %collective-permute-done.1.depth_odd, f32[4,2048]{1,0:T(4,128)S(1)} %collective-permute-done.2.row_even, ...), custom_call_target="tpu_custom_call" | custom-call | flops 2621440 | bytes 1048576 | tf_op jit(solution)/shard_map/shade_sent/pallas_call | solution.py:217
  12.4 2.4 %collective-permute-start.4 = (f32[2,4,16,512]{3,2,1,0:T(8,128)S(1)}, f32[2,4,16,512]{3,2,1,0:T(8,128)S(1)}, u32[]{:S(2)}, u32[]{:S(2)}) collective-permute-start(f32[2,4,16,512]{3,2,1,0:T(8,128)S(1)} %shade_sent.1), channel_id=1, source_target_pairs={{0,8},{8,0},{16,24},{24,16},{1,9},{9,1},{17,25},{25,17},{2,10},{10... | collective-permute-start | bytes 786440 | tf_op jit(solution)/shard_map/ppermute | solution.py:232
  14.8 0.4 %shade_kept.1.kept = f32[2,4,16,512]{3,2,1,0:T(8,128)S(1)} custom-call(f32[4,16,2048]{2,1,0:T(8,128)S(1)} %copy-done.1, f32[16,2048]{1,0:T(8,128)S(1)} %collective-permute-done.depth_even, f32[16,2048]{1,0:T(8,128)S(1)} %collective-permute-done.1.depth_odd, f32[4,2048]{1,0:T(4,128)S(1)} %collective-permute-done.2.row_even, ...), custom_call_target="tpu_custom_call" | custom-call | flops 2621440 | bytes 1048576 | tf_op jit(solution)/shard_map/shade_kept/pallas_call | solution.py:217
  15.1 0.8 %collective-permute-done.4.received = f32[2,4,16,512]{3,2,1,0:T(8,128)S(1)} collective-permute-done((f32[2,4,16,512]{3,2,1,0:T(8,128)S(1)}, f32[2,4,16,512]{3,2,1,0:T(8,128)S(1)}, u32[]{:S(2)}, u32[]{:S(2)}) %collective-permute-start.4) | collective-permute-done | bytes 262176 | tf_op jit(solution)/shard_map/ppermute | solution.py:232
  16.0 1.5 %collective-permute-start.5 = (f32[1,4,16,512]{3,2,1,0:T(8,128)S(1)}, f32[1,4,16,512]{3,2,1,0:T(8,128)S(1)}, u32[]{:S(2)}, u32[]{:S(2)}) collective-permute-start(f32[1,4,16,512]{3,2,1,0:T(8,128)S(1)} %get-tuple-element.20), channel_id=1, source_target_pairs={{0,16},{8,24},{16,0},{24,8},{1,17},{9,25},{17,1},{25,9},{2,18},{10... | collective-permute-start | bytes 393224 | tf_op jit(solution)/shard_map/ppermute | solution.py:232
  17.5 4.4 %collective-permute-done.5.received = f32[1,4,16,512]{3,2,1,0:T(8,128)S(1)} collective-permute-done((f32[1,4,16,512]{3,2,1,0:T(8,128)S(1)}, f32[1,4,16,512]{3,2,1,0:T(8,128)S(1)}, u32[]{:S(2)}, u32[]{:S(2)}) %collective-permute-start.5) | collective-permute-done | bytes 131104 | tf_op jit(solution)/shard_map/ppermute | solution.py:232
  21.8 0.7 %merge.3 = f32[4,16,512]{2,1,0:T(8,128)} custom-call(f32[1,4,16,512]{3,2,1,0:T(8,128)S(1)} %get-tuple-element.19.kept, f32[1,4,16,512]{3,2,1,0:T(8,128)S(1)} %collective-permute-done.5.received), custom_call_target="tpu_custom_call" | custom-call | tf_op jit(solution)/shard_map/merge/pallas_call | solution.py:236
  (3 shorter events, 0.1 us)
Async XLA Ops:
  0.0 1.0 %copy-start = (f32[4,16,2048]{2,1,0:T(8,128)S(1)}, f32[4,16,2048]{2,1,0:T(8,128)}, u32[]{:S(2)}) copy-start(f32[4,16,2048]{2,1,0:T(8,128)} %density.5) | copy-start | bytes 1572868
  1.1 9.9 %collective-permute-start = (f32[16,2048]{1,0:T(8,128)S(1)}, f32[16,2048]{1,0:T(8,128)S(1)}, u32[]{:S(2)}, u32[]{:S(2)}) collective-permute-start(f32[16,2048]{1,0:T(8,128)S(1)} %get-tuple-element.13), channel_id=1, source_target_pairs={{0,8},{16,24},{8,0},{24,16},{1,9},{17,25},{9,1},{25,17},{2,10},{18... | collective-permute-start | bytes 393224 | tf_op jit(solution)/shard_map/ppermute | solution.py:53
  1.2 9.8 %collective-permute-start.1 = (f32[16,2048]{1,0:T(8,128)S(1)}, f32[16,2048]{1,0:T(8,128)S(1)}, u32[]{:S(2)}, u32[]{:S(2)}) collective-permute-start(f32[16,2048]{1,0:T(8,128)S(1)} %get-tuple-element.14), channel_id=1, source_target_pairs={{8,16},{16,8},{9,17},{17,9},{10,18},{18,10},{11,19},{19,11},{12,20... | collective-permute-start | bytes 393224 | tf_op jit(solution)/shard_map/ppermute | solution.py:53
  1.8 9.1 %collective-permute-start.2 = (f32[4,2048]{1,0:T(4,128)S(1)}, f32[4,2048]{1,0:T(4,128)S(1)}, u32[]{:S(2)}, u32[]{:S(2)}) collective-permute-start(f32[4,2048]{1,0:T(4,128)S(1)} %get-tuple-element.15), channel_id=1, source_target_pairs={{0,1},{2,3},{4,5},{6,7},{1,0},{3,2},{5,4},{7,6},{8,9},{10,11},{12,... | collective-permute-start | bytes 98312 | tf_op jit(solution)/shard_map/ppermute | solution.py:53
  1.9 9.0 %collective-permute-start.3 = (f32[4,2048]{1,0:T(4,128)S(1)}, f32[4,2048]{1,0:T(4,128)S(1)}, u32[]{:S(2)}, u32[]{:S(2)}) collective-permute-start(f32[4,2048]{1,0:T(4,128)S(1)} %get-tuple-element.16), channel_id=1, source_target_pairs={{1,2},{3,4},{5,6},{2,1},{4,3},{6,5},{9,10},{11,12},{13,14},{10,9},... | collective-permute-start | bytes 98312 | tf_op jit(solution)/shard_map/ppermute | solution.py:53
  8.2 1.0 %copy-start.2 = (s32[4,16,2048]{2,1,0:T(8,128)S(1)}, s32[4,16,2048]{2,1,0:T(8,128)}, u32[]{:S(2)}) copy-start(s32[4,16,2048]{2,1,0:T(8,128)} %bins.1) | copy-start | bytes 1572868
  9.2 0.7 %copy-start.3 = (bf16[3,256]{1,0:T(4,128)(2,1)S(1)}, bf16[3,256]{1,0:T(4,128)(2,1)}, u32[]{:S(2)}) copy-start(bf16[3,256]{1,0:T(4,128)(2,1)} %colors.1) | copy-start | bytes 4612
  11.0 1.0 %copy-start.1 = (f32[4,16,2048]{2,1,0:T(8,128)S(1)}, f32[4,16,2048]{2,1,0:T(8,128)}, u32[]{:S(2)}) copy-start(f32[4,16,2048]{2,1,0:T(8,128)} %density.5) | copy-start | bytes 1572868
  12.4 3.5 %collective-permute-start.4 = (f32[2,4,16,512]{3,2,1,0:T(8,128)S(1)}, f32[2,4,16,512]{3,2,1,0:T(8,128)S(1)}, u32[]{:S(2)}, u32[]{:S(2)}) collective-permute-start(f32[2,4,16,512]{3,2,1,0:T(8,128)S(1)} %shade_sent.1), channel_id=1, source_target_pairs={{0,8},{8,0},{16,24},{24,16},{1,9},{9,1},{17,25},{25,17},{2,10},{10... | collective-permute-start | bytes 786440 | tf_op jit(solution)/shard_map/ppermute | solution.py:232
  16.0 5.8 %collective-permute-start.5 = (f32[1,4,16,512]{3,2,1,0:T(8,128)S(1)}, f32[1,4,16,512]{3,2,1,0:T(8,128)S(1)}, u32[]{:S(2)}, u32[]{:S(2)}) collective-permute-start(f32[1,4,16,512]{3,2,1,0:T(8,128)S(1)} %get-tuple-element.20), channel_id=1, source_target_pairs={{0,16},{8,24},{16,0},{24,8},{1,17},{9,25},{17,1},{25,9},{2,18},{10... | collective-permute-start | bytes 393224 | tf_op jit(solution)/shard_map/ppermute | solution.py:232

commit v2 on v1

--- a/solution.py
+++ b/solution.py
@@ -22,6 +22,10 @@
     return pl.BlockSpec(memory_space=pltpu.SMEM)
 
 
+def stay(x):
+    return pltpu.with_memory_space_constraint(x, pltpu.HBM)
+
+
 def params():
     return pltpu.CompilerParams(vmem_limit_bytes=VMEM_LIMIT)
 
@@ -34,10 +38,24 @@
     return jax.ShapeDtypeStruct(shape, jnp.float32)
 
 
-def faces_kernel(density, depth_even, depth_odd, row_even, row_odd):
+def load_kernel(
+    density_in, bins_in, colors_in, opacities_in,
+    density, bins, depth_even, depth_odd, row_even, row_odd, tables,
+    colors, opacities, done,
+):
+    moves = [
+        (density_in, density),
+        (bins_in, bins),
+        (colors_in, colors),
+        (opacities_in, opacities),
+    ]
+    copies = [pltpu.make_async_copy(a, b, done.at[i]) for i, (a, b) in enumerate(moves)]
+    for copy in copies:
+        copy.start()
     slices, rows, _ = density.shape
     depth_low = lax.axis_index("depth") & 1 == 0
     tile_low = lax.axis_index("tile") & 1 == 0
+    copies[0].wait()
     first, last = density[0], density[slices - 1]
     depth_even[...] = jnp.where(depth_low, last, first)
     depth_odd[...] = jnp.where(depth_low, first, last)
@@ -45,11 +63,20 @@
         top, bottom = density[k, 0:1], density[k, rows - 1 : rows]
         row_even[k : k + 1] = jnp.where(tile_low, bottom, top)
         row_odd[k : k + 1] = jnp.where(tile_low, top, bottom)
+    for copy in copies[1:]:
+        copy.wait()
+    color = whole_number(colors[...], COLOR_ONE)
+    opacity = whole_number(opacities[...].reshape(1, -1), OPACITY_ONE)
+    words = [color[0:1] | (color[1:2] << 16), color[2:3] | (opacity << 16)]
+    for part in range(tables.shape[0]):
+        for j in range(2):
+            table = words[j][:, part * LANES : (part + 1) * LANES]
+            tables[part, j] = jnp.broadcast_to(table, (SUBLANES, LANES))
 
 
 def trade(x, axis, first):
     count = lax.axis_size(axis)
-    pairs = [(i, i + 1) for i in range(first, count - 1, 2)]
+    pairs = [(i, (i + 1) % count) for i in range(first, count, 2)]
     return lax.ppermute(x, axis, pairs + [(b, a) for a, b in pairs])
 
 
@@ -57,19 +84,12 @@
     return (x.astype(jnp.float32) * one).astype(jnp.int32)
 
 
-def weights_kernel(count, bins, colors, opacities, weighted, passed):
+def weights_kernel(count, bins, tables, weighted, passed):
     slices, rows, cols = bins.shape
-    color = whole_number(colors[...], COLOR_ONE)
-    opacity = whole_number(opacities[...], OPACITY_ONE)
-    words = [color[0:1] | (color[1:2] << 16), color[2:3] | (opacity << 16)]
-    tables = [
-        [jnp.broadcast_to(word[:, i : i + LANES], (SUBLANES, LANES)) for word in words]
-        for i in range(0, word_count(colors), LANES)
-    ]
-    opacity_unit = [
-        jnp.where(k < count[0, 0], 1.0 / OPACITY_ONE, 0.0).astype(jnp.float32)
-        for k in range(slices)
-    ]
+    parts = tables.shape[0]
+    table = [[tables[part, j] for j in range(2)] for part in range(parts)]
+    occupied = count[0, 0]
+    unit = [flag(k < occupied) * (1.0 / OPACITY_ONE) for k in range(slices)]
     for r in range(0, rows, SUBLANES):
         for c in range(0, cols, LANES):
             at = (slice(r, r + SUBLANES), slice(c, c + LANES))
@@ -77,14 +97,14 @@
             for k in range(slices):
                 index = bins[(k, *at)]
                 lane = index & (LANES - 1)
-                found = [lane_lookup(tables[0][j], lane) for j in range(2)]
-                for part in range(1, len(tables)):
+                found = [lane_lookup(table[0][j], lane) for j in range(2)]
+                for part in range(1, parts):
                     here = index >= part * LANES
                     found = [
-                        jnp.where(here, lane_lookup(tables[part][j], lane), found[j])
+                        jnp.where(here, lane_lookup(table[part][j], lane), found[j])
                         for j in range(2)
                     ]
-                alpha = (found[1] >> 16).astype(jnp.float32) * opacity_unit[k]
+                alpha = (found[1] >> 16).astype(jnp.float32) * unit[k]
                 weight = before * alpha
                 weighted[(0, k, *at)] = weight * (found[0] & 0xFFFF).astype(jnp.float32)
                 weighted[(1, k, *at)] = weight * (found[0] >> 16).astype(jnp.float32)
@@ -93,12 +113,12 @@
             passed[at] = before * COLOR_ONE
 
 
-def word_count(colors):
-    return colors.shape[1]
-
-
 def lane_lookup(table, lane):
     return jnp.take_along_axis(table, lane, axis=1, mode="promise_in_bounds")
+
+
+def flag(condition):
+    return jnp.where(condition, 1.0, 0.0).astype(jnp.float32)
 
 
 def shade_kernel(keeps, density, depth_even, depth_odd, row_even, row_odd, weighted, passed, image):
@@ -107,7 +127,10 @@
     me = lax.axis_index("depth")
     mine = me & 1
     depth_is_low = mine == 0
-    tile_is_low = lax.axis_index("tile") & 1 == 0
+    tile = lax.axis_index("tile")
+    tile_is_low = tile & 1 == 0
+    has_front, has_behind = flag(me > 0), flag(me < lax.axis_size("depth") - 1)
+    has_above, has_below = flag(tile > 0), flag(tile < lax.axis_size("tile") - 1)
     lane = lax.broadcasted_iota(jnp.int32, (SUBLANES, LANES), 1)
     sub = lax.broadcasted_iota(jnp.int32, (SUBLANES, LANES), 0)
     at_left, at_right = lane == 0, lane == LANES - 1
@@ -120,18 +143,18 @@
             start = pl.multiple_of(number * piece + p, LANES)
             left = pl.multiple_of(jnp.maximum(start - LANES, 0), LANES)
             right = pl.multiple_of(jnp.minimum(start + LANES, cols - LANES), LANES)
-            has_left = jnp.where(start > 0, 1.0, 0.0).astype(jnp.float32)
-            has_right = jnp.where(start + LANES < cols, 1.0, 0.0).astype(jnp.float32)
+            has_left = flag(start > 0)
+            has_right = flag(start + LANES < cols)
             here = pl.ds(start, LANES)
             even_rows, odd_rows = row_even[:, here], row_odd[:, here]
-            above_rows = jnp.where(tile_is_low, odd_rows, even_rows)
-            below_rows = jnp.where(tile_is_low, even_rows, odd_rows)
+            above_rows = jnp.where(tile_is_low, odd_rows, even_rows) * has_above
+            below_rows = jnp.where(tile_is_low, even_rows, odd_rows) * has_below
             for g in range(groups):
                 at = (slice(g * SUBLANES, (g + 1) * SUBLANES), here)
                 even_face, odd_face = depth_even[at], depth_odd[at]
-                column = [jnp.where(depth_is_low, odd_face, even_face)]
+                column = [jnp.where(depth_is_low, odd_face, even_face) * has_front]
                 column += [density[(k, *at)] for k in range(slices)]
-                column += [jnp.where(depth_is_low, even_face, odd_face)]
+                column += [jnp.where(depth_is_low, even_face, odd_face) * has_behind]
                 sums = [jnp.zeros((SUBLANES, LANES), jnp.float32) for _ in range(3)]
                 for k in range(slices):
                     v = column[k + 1]
@@ -189,14 +212,29 @@
     slab_count = lax.axis_size("depth")
     half, piece = slab_count // 2, cols // slab_count
     pixels = rows * cols
-    faces = pl.pallas_call(
-        faces_kernel,
-        out_shape=[f32(rows, cols), f32(rows, cols), f32(slices, cols), f32(slices, cols)],
-        in_specs=[vmem()],
-        out_specs=[vmem()] * 4,
+    parts = opacities.shape[0] // LANES
+    here = pl.BlockSpec(memory_space=pltpu.HBM)
+    density, bins, *faces, tables = pl.pallas_call(
+        load_kernel,
+        out_shape=[
+            f32(*density.shape),
+            jax.ShapeDtypeStruct(bins.shape, jnp.int32),
+            f32(rows, cols),
+            f32(rows, cols),
+            f32(slices, cols),
+            f32(slices, cols),
+            jax.ShapeDtypeStruct((parts, 2, SUBLANES, LANES), jnp.int32),
+        ],
+        in_specs=[here] * 4,
+        out_specs=[vmem()] * 7,
+        scratch_shapes=[
+            pltpu.VMEM(colors.shape, colors.dtype),
+            pltpu.VMEM(opacities.shape, opacities.dtype),
+            pltpu.SemaphoreType.DMA((4,)),
+        ],
         compiler_params=params(),
-        name="faces",
-    )(density)
+        name="load",
+    )(*(stay(x) for x in (density, bins, colors, opacities)))
     traded = [
         trade(faces[0], "depth", 0),
         trade(faces[1], "depth", 1),
@@ -206,12 +244,12 @@
     weighted, passed = pl.pallas_call(
         weights_kernel,
         out_shape=[f32(3, slices, rows, cols), f32(rows, cols)],
-        in_specs=[smem(), vmem(), vmem(), vmem()],
+        in_specs=[smem(), vmem(), vmem()],
         out_specs=[vmem(), vmem()],
         compiler_params=params(),
         cost_estimate=cost(64 * slices * pixels, 16 * slices * pixels),
         name="weights",
-    )(counts, bins, colors, opacities[None])
+    )(counts, bins, tables)
 
     def shaded(keeps):
         return pl.pallas_call(

time: 22.8 us -> 21 us (0.921)
  the two profiles are of different devices: /device:TPU:2 before, /device:TPU:0 now
where the time goes in v2:
time: 21 us; the launch traced here: 20.8 us
  starting transfers between devices  8.87 us (42%)
  waiting for transfers between devices  7.52 us (36%)
  Pallas kernels  3.76 us (18%)
  between operations  0.7 us (3%)
    ppermute x4, starting transfers between devices, trade(): return lax.ppermute(x, axis, pairs + [(b, a) for a, b in pairs])  8.22 us
    ppermute x2, waiting for transfers between devices, on_device(): received = lax.ppermute(outgoing, 'depth', partner)  6.16 us
    ppermute x4, waiting for transfers between devices, trade(): return lax.ppermute(x, axis, pairs + [(b, a) for a, b in pairs])  1.36 us
    pallas_call x1, Pallas kernels, on_device(): pl.pallas_call(load_kernel, out_shape=[f32(*density.shape), jax.ShapeDtyp...  1.25 us
    pallas_call x1, Pallas kernels, on_device(): pl.pallas_call(weights_kernel, out_shape=[f32(3, slices, rows, cols), f32...  1.02 us
    pallas_call x2, Pallas kernels, shaded(): pl.pallas_call(functools.partial(shade_kernel, keeps), out_shape=f32(half...  0.76 us
    pallas_call x2, Pallas kernels, on_device(): pl.pallas_call(functools.partial(merge_kernel, level, last), out_shape=sh...  0.72 us
    ppermute x2, starting transfers between devices, on_device(): received = lax.ppermute(outgoing, 'depth', partner)  0.64 us
  transfers between devices with their start and end apart: 6, of which 3 were waited for; matrix products, arithmetic and copies ran while one was open for 0% of the time, Pallas kernels for 7%

profile of v2, /device:TPU:0, one launch (start us, length us, event | category | flops | bytes accessed | tf_op | source)
XLA Modules:
  0.0 20.8 jit_solution(11401860079780971327)
XLA Ops:
  0.0 1.3 %load.1 = (f32[4,16,2048]{2,1,0:T(8,128)S(1)}, s32[4,16,2048]{2,1,0:T(8,128)S(1)}, f32[16,2048]{1,0:T(8,128)S(1)}, f32[16,2048]{1,0:T(8,128)S(1)}, f32[4,2048]{1...) custom-call(f32[4,16,2048]{2,1,0:T(8,128)} %density_in.1, s32[4,16,2048]{2,1,0:T(8,128)} %bins_in.1, ...), custom_call_target="tpu_custom_call" | custom-call | tf_op jit(solution)/shard_map/load/pallas_call | solution.py:217
  1.3 0.5 %collective-permute-start = (f32[16,2048]{1,0:T(8,128)S(1)}, f32[16,2048]{1,0:T(8,128)S(1)}, u32[]{:S(2)}, u32[]{:S(2)}) collective-permute-start(f32[16,2048]{1,0:T(8,128)S(1)} %get-tuple-element.17), channel_id=1, source_target_pairs={{0,8},{16,24},{8,0},{24,16},{1,9},{17,25},{9,1},{25,17},{2,10},{18... | collective-permute-start | bytes 393224 | tf_op jit(solution)/shard_map/ppermute | solution.py:80
  1.8 2.6 %collective-permute-start.1 = (f32[16,2048]{1,0:T(8,128)S(1)}, f32[16,2048]{1,0:T(8,128)S(1)}, u32[]{:S(2)}, u32[]{:S(2)}) collective-permute-start(f32[16,2048]{1,0:T(8,128)S(1)} %get-tuple-element.18), channel_id=1, source_target_pairs={{8,16},{24,0},{16,8},{0,24},{9,17},{25,1},{17,9},{1,25},{10,18},{2... | collective-permute-start | bytes 393224 | tf_op jit(solution)/shard_map/ppermute | solution.py:80
  4.4 1.5 %collective-permute-start.2 = (f32[4,2048]{1,0:T(4,128)S(1)}, f32[4,2048]{1,0:T(4,128)S(1)}, u32[]{:S(2)}, u32[]{:S(2)}) collective-permute-start(f32[4,2048]{1,0:T(4,128)S(1)} %get-tuple-element.19), channel_id=1, source_target_pairs={{0,1},{2,3},{4,5},{6,7},{1,0},{3,2},{5,4},{7,6},{8,9},{10,11},{12,... | collective-permute-start | bytes 98312 | tf_op jit(solution)/shard_map/ppermute | solution.py:80
  5.9 3.6 %collective-permute-start.3 = (f32[4,2048]{1,0:T(4,128)S(1)}, f32[4,2048]{1,0:T(4,128)S(1)}, u32[]{:S(2)}, u32[]{:S(2)}) collective-permute-start(f32[4,2048]{1,0:T(4,128)S(1)} %get-tuple-element.20), channel_id=1, source_target_pairs={{1,2},{3,4},{5,6},{7,0},{2,1},{4,3},{6,5},{0,7},{9,10},{11,12},{13... | collective-permute-start | bytes 98312 | tf_op jit(solution)/shard_map/ppermute | solution.py:80
  10.1 1.0 %weights.1 = (f32[3,4,16,2048]{3,2,1,0:T(8,128)S(1)}, f32[16,2048]{1,0:T(8,128)S(1)}) custom-call(s32[1,1]{1,0:T(1,128)S(6)} %copy.6.count, s32[4,16,2048]{2,1,0:T(8,128)S(1)} %get-tuple-element.21.bins, s32[2,2,8,128]{3,2,1,0:T(8,128)S(1)} %get-tuple-element.22.tables), custom_call_target="tpu_custom_call" | custom-call | flops 8388608 | bytes 2097152 | tf_op jit(solution)/shard_map/weights/pallas_call | solution.py:244
  11.2 0.0 collective-permute-done.2.row_even
  11.2 1.4 %collective-permute-done.3.row_odd = f32[4,2048]{1,0:T(4,128)S(1)} collective-permute-done((f32[4,2048]{1,0:T(4,128)S(1)}, f32[4,2048]{1,0:T(4,128)S(1)}, u32[]{:S(2)}, u32[]{:S(2)}) %collective-permute-start.3) | collective-permute-done | bytes 32800 | tf_op jit(solution)/shard_map/ppermute | solution.py:80
  12.5 0.0 collective-permute-done.depth_even
  12.5 0.0 collective-permute-done.1.depth_odd
  12.5 0.4 %shade_sent.1 = f32[2,4,16,512]{3,2,1,0:T(8,128)S(1)} custom-call(f32[4,16,2048]{2,1,0:T(8,128)S(1)} %get-tuple-element.16.density, f32[16,2048]{1,0:T(8,128)S(1)} %collective-permute-done.depth_even, f32[16,2048]{1,0:T(8,128)S(1)} %collective-permute-done.1.depth_odd, f32[4,2048]{1,0:T(4,128)S(1)} %collective-permute-done.2.row_even, ...), custom_call_target="tpu_custom_call" | custom-call | flops 2621440 | bytes 1048576 | tf_op jit(solution)/shard_map/shade_sent/pallas_call | solution.py:255
  12.9 0.1 collective-permute-start.4
  13.0 0.4 %shade_kept.1.kept = f32[2,4,16,512]{3,2,1,0:T(8,128)S(1)} custom-call(f32[4,16,2048]{2,1,0:T(8,128)S(1)} %get-tuple-element.16.density, f32[16,2048]{1,0:T(8,128)S(1)} %collective-permute-done.depth_even, f32[16,2048]{1,0:T(8,128)S(1)} %collective-permute-done.1.depth_odd, f32[4,2048]{1,0:T(4,128)S(1)} %collective-permute-done.2.row_even, ...), custom_call_target="tpu_custom_call" | custom-call | flops 2621440 | bytes 1048576 | tf_op jit(solution)/shard_map/shade_kept/pallas_call | solution.py:255
  13.4 1.1 %collective-permute-done.4.received = f32[2,4,16,512]{3,2,1,0:T(8,128)S(1)} collective-permute-done((f32[2,4,16,512]{3,2,1,0:T(8,128)S(1)}, f32[2,4,16,512]{3,2,1,0:T(8,128)S(1)}, u32[]{:S(2)}, u32[]{:S(2)}) %collective-permute-start.4) | collective-permute-done | bytes 262176 | tf_op jit(solution)/shard_map/ppermute | solution.py:270
  14.6 0.6 %collective-permute-start.5 = (f32[1,4,16,512]{3,2,1,0:T(8,128)S(1)}, f32[1,4,16,512]{3,2,1,0:T(8,128)S(1)}, u32[]{:S(2)}, u32[]{:S(2)}) collective-permute-start(f32[1,4,16,512]{3,2,1,0:T(8,128)S(1)} %get-tuple-element.26), channel_id=1, source_target_pairs={{0,16},{8,24},{16,0},{24,8},{1,17},{9,25},{17,1},{25,9},{2,18},{10... | collective-permute-start | bytes 393224 | tf_op jit(solution)/shard_map/ppermute | solution.py:270
  15.1 5.0 %collective-permute-done.5.received = f32[1,4,16,512]{3,2,1,0:T(8,128)S(1)} collective-permute-done((f32[1,4,16,512]{3,2,1,0:T(8,128)S(1)}, f32[1,4,16,512]{3,2,1,0:T(8,128)S(1)}, u32[]{:S(2)}, u32[]{:S(2)}) %collective-permute-start.5) | collective-permute-done | bytes 131104 | tf_op jit(solution)/shard_map/ppermute | solution.py:270
  20.2 0.7 %merge.3 = f32[4,16,512]{2,1,0:T(8,128)} custom-call(f32[1,4,16,512]{3,2,1,0:T(8,128)S(1)} %get-tuple-element.25.kept, f32[1,4,16,512]{3,2,1,0:T(8,128)S(1)} %collective-permute-done.5.received), custom_call_target="tpu_custom_call" | custom-call | tf_op jit(solution)/shard_map/merge/pallas_call | solution.py:274
  (1 shorter events, 0.0 us)
Async XLA Ops:
  1.3 11.3 %collective-permute-start = (f32[16,2048]{1,0:T(8,128)S(1)}, f32[16,2048]{1,0:T(8,128)S(1)}, u32[]{:S(2)}, u32[]{:S(2)}) collective-permute-start(f32[16,2048]{1,0:T(8,128)S(1)} %get-tuple-element.17), channel_id=1, source_target_pairs={{0,8},{16,24},{8,0},{24,16},{1,9},{17,25},{9,1},{25,17},{2,10},{18... | collective-permute-start | bytes 393224 | tf_op jit(solution)/shard_map/ppermute | solution.py:80
  1.8 10.8 %collective-permute-start.1 = (f32[16,2048]{1,0:T(8,128)S(1)}, f32[16,2048]{1,0:T(8,128)S(1)}, u32[]{:S(2)}, u32[]{:S(2)}) collective-permute-start(f32[16,2048]{1,0:T(8,128)S(1)} %get-tuple-element.18), channel_id=1, source_target_pairs={{8,16},{24,0},{16,8},{0,24},{9,17},{25,1},{17,9},{1,25},{10,18},{2... | collective-permute-start | bytes 393224 | tf_op jit(solution)/shard_map/ppermute | solution.py:80
  4.4 6.7 %collective-permute-start.2 = (f32[4,2048]{1,0:T(4,128)S(1)}, f32[4,2048]{1,0:T(4,128)S(1)}, u32[]{:S(2)}, u32[]{:S(2)}) collective-permute-start(f32[4,2048]{1,0:T(4,128)S(1)} %get-tuple-element.19), channel_id=1, source_target_pairs={{0,1},{2,3},{4,5},{6,7},{1,0},{3,2},{5,4},{7,6},{8,9},{10,11},{12,... | collective-permute-start | bytes 98312 | tf_op jit(solution)/shard_map/ppermute | solution.py:80
  5.9 6.6 %collective-permute-start.3 = (f32[4,2048]{1,0:T(4,128)S(1)}, f32[4,2048]{1,0:T(4,128)S(1)}, u32[]{:S(2)}, u32[]{:S(2)}) collective-permute-start(f32[4,2048]{1,0:T(4,128)S(1)} %get-tuple-element.20), channel_id=1, source_target_pairs={{1,2},{3,4},{5,6},{7,0},{2,1},{4,3},{6,5},{0,7},{9,10},{11,12},{13... | collective-permute-start | bytes 98312 | tf_op jit(solution)/shard_map/ppermute | solution.py:80
  12.9 1.6 %collective-permute-start.4 = (f32[2,4,16,512]{3,2,1,0:T(8,128)S(1)}, f32[2,4,16,512]{3,2,1,0:T(8,128)S(1)}, u32[]{:S(2)}, u32[]{:S(2)}) collective-permute-start(f32[2,4,16,512]{3,2,1,0:T(8,128)S(1)} %shade_sent.1), channel_id=1, source_target_pairs={{0,8},{8,0},{16,24},{24,16},{1,9},{9,1},{17,25},{25,17},{2,10},{10... | collective-permute-start | bytes 786440 | tf_op jit(solution)/shard_map/ppermute | solution.py:270
  14.6 5.6 %collective-permute-start.5 = (f32[1,4,16,512]{3,2,1,0:T(8,128)S(1)}, f32[1,4,16,512]{3,2,1,0:T(8,128)S(1)}, u32[]{:S(2)}, u32[]{:S(2)}) collective-permute-start(f32[1,4,16,512]{3,2,1,0:T(8,128)S(1)} %get-tuple-element.26), channel_id=1, source_target_pairs={{0,16},{8,24},{16,0},{24,8},{1,17},{9,25},{17,1},{25,9},{2,18},{10... | collective-permute-start | bytes 393224 | tf_op jit(solution)/shard_map/ppermute | solution.py:270

commit v3 on v2

--- a/solution.py
+++ b/solution.py
@@ -75,9 +75,18 @@
 
 
 def trade(x, axis, first):
-    count = lax.axis_size(axis)
-    pairs = [(i, (i + 1) % count) for i in range(first, count, 2)]
-    return lax.ppermute(x, axis, pairs + [(b, a) for a, b in pairs])
+    slabs, tiles = lax.axis_size("depth"), lax.axis_size("tile")
+    pairs = []
+    for d in range(slabs):
+        for t in range(tiles):
+            if axis == "depth":
+                inside = 0 <= ((d - first) ^ 1) + first < slabs
+                partner = (((d - first) ^ 1) + first, t) if inside else (d, t ^ 1)
+            else:
+                inside = 0 <= ((t - first) ^ 1) + first < tiles
+                partner = (d, ((t - first) ^ 1) + first) if inside else (d ^ 1, t)
+            pairs.append((d * tiles + t, partner[0] * tiles + partner[1]))
+    return lax.ppermute(x, ("depth", "tile"), pairs)
 
 
 def whole_number(x, one):

time: 21 us -> 16.9 us (0.80)
  starting transfers between devices: 8.87 us -> 5.28 us
  waiting for transfers between devices: 7.52 us -> 6.85 us
    ppermute x4, starting transfers between devices: 8.22 us -> 4.44 us  [trade(): return lax.ppermute(x, ('depth', 'tile'), pairs)]
    ppermute x4, waiting for transfers between devices: 1.36 us -> 0.89 us  [trade(): return lax.ppermute(x, ('depth', 'tile'), pairs)]
  transfers between devices with their start and end apart: 6 -> 6, of which waited for: 3 -> 3; matrix products, arithmetic and copies ran while one was open for 0% -> 0% of each run, Pallas kernels for 7% -> 8%
where the time goes in v3:
time: 16.9 us; the launch traced here: 16.6 us
  waiting for transfers between devices  6.85 us (41%)
  starting transfers between devices  5.28 us (31%)
  Pallas kernels  3.77 us (22%)
  between operations  0.69 us (4%)
    ppermute x2, waiting for transfers between devices, on_device(): received = lax.ppermute(outgoing, 'depth', partner)  5.96 us
    ppermute x4, starting transfers between devices, trade(): return lax.ppermute(x, ('depth', 'tile'), pairs)  4.44 us
    pallas_call x1, Pallas kernels, on_device(): pl.pallas_call(load_kernel, out_shape=[f32(*density.shape), jax.ShapeDtyp...  1.25 us
    pallas_call x1, Pallas kernels, on_device(): pl.pallas_call(weights_kernel, out_shape=[f32(3, slices, rows, cols), f32...  1.02 us
    ppermute x4, waiting for transfers between devices, trade(): return lax.ppermute(x, ('depth', 'tile'), pairs)  0.89 us
    ppermute x2, starting transfers between devices, on_device(): received = lax.ppermute(outgoing, 'depth', partner)  0.84 us
    pallas_call x2, Pallas kernels, shaded(): pl.pallas_call(functools.partial(shade_kernel, keeps), out_shape=f32(half...  0.77 us
    pallas_call x2, Pallas kernels, on_device(): pl.pallas_call(functools.partial(merge_kernel, level, last), out_shape=sh...  0.72 us
  transfers between devices with their start and end apart: 6, of which 3 were waited for; matrix products, arithmetic and copies ran while one was open for 0% of the time, Pallas kernels for 8%

profile of v3, /device:TPU:0, one launch (start us, length us, event | category | flops | bytes accessed | tf_op | source)
XLA Modules:
  0.0 16.6 jit_solution(9588489703393489115)
XLA Ops:
  0.0 1.3 %load.1 = (f32[4,16,2048]{2,1,0:T(8,128)S(1)}, s32[4,16,2048]{2,1,0:T(8,128)S(1)}, f32[16,2048]{1,0:T(8,128)S(1)}, f32[16,2048]{1,0:T(8,128)S(1)}, f32[4,2048]{1...) custom-call(f32[4,16,2048]{2,1,0:T(8,128)} %density_in.1, s32[4,16,2048]{2,1,0:T(8,128)} %bins_in.1, ...), custom_call_target="tpu_custom_call" | custom-call | tf_op jit(solution)/shard_map/load/pallas_call | solution.py:226
  1.3 0.5 %collective-permute-start = (f32[16,2048]{1,0:T(8,128)S(1)}, f32[16,2048]{1,0:T(8,128)S(1)}, u32[]{:S(2)}, u32[]{:S(2)}) collective-permute-start(f32[16,2048]{1,0:T(8,128)S(1)} %get-tuple-element.17), channel_id=1, source_target_pairs={{0,8},{1,9},{2,10},{3,11},{4,12},{5,13},{6,14},{7,15},{8,0},{9,1},... | collective-permute-start | bytes 393224 | tf_op jit(solution)/shard_map/ppermute | solution.py:89
  1.8 2.6 %collective-permute-start.1 = (f32[16,2048]{1,0:T(8,128)S(1)}, f32[16,2048]{1,0:T(8,128)S(1)}, u32[]{:S(2)}, u32[]{:S(2)}) collective-permute-start(f32[16,2048]{1,0:T(8,128)S(1)} %get-tuple-element.18), channel_id=1, source_target_pairs={{0,1},{1,0},{2,3},{3,2},{4,5},{5,4},{6,7},{7,6},{8,16},{9,17},{10,... | collective-permute-start | bytes 393224 | tf_op jit(solution)/shard_map/ppermute | solution.py:89
  4.3 0.1 collective-permute-start.2
  4.4 1.3 %collective-permute-start.3 = (f32[4,2048]{1,0:T(4,128)S(1)}, f32[4,2048]{1,0:T(4,128)S(1)}, u32[]{:S(2)}, u32[]{:S(2)}) collective-permute-start(f32[4,2048]{1,0:T(4,128)S(1)} %get-tuple-element.20), channel_id=1, source_target_pairs={{0,8},{1,2},{2,1},{3,4},{4,3},{5,6},{6,5},{7,15},{8,0},{9,10},{10,... | collective-permute-start | bytes 98312 | tf_op jit(solution)/shard_map/ppermute | solution.py:89
  6.3 1.0 %weights.1 = (f32[3,4,16,2048]{3,2,1,0:T(8,128)S(1)}, f32[16,2048]{1,0:T(8,128)S(1)}) custom-call(s32[1,1]{1,0:T(1,128)S(6)} %copy.6.count, s32[4,16,2048]{2,1,0:T(8,128)S(1)} %get-tuple-element.21.bins, s32[2,2,8,128]{3,2,1,0:T(8,128)S(1)} %get-tuple-element.22.tables), custom_call_target="tpu_custom_call" | custom-call | flops 8388608 | bytes 2097152 | tf_op jit(solution)/shard_map/weights/pallas_call | solution.py:253
  7.4 0.9 %collective-permute-done.2.row_even = f32[4,2048]{1,0:T(4,128)S(1)} collective-permute-done((f32[4,2048]{1,0:T(4,128)S(1)}, f32[4,2048]{1,0:T(4,128)S(1)}, u32[]{:S(2)}, u32[]{:S(2)}) %collective-permute-start.2) | collective-permute-done | bytes 32800 | tf_op jit(solution)/shard_map/ppermute | solution.py:89
  8.3 0.0 collective-permute-done.3.row_odd
  8.3 0.0 collective-permute-done.depth_even
  8.3 0.0 collective-permute-done.1.depth_odd
  8.3 0.4 %shade_sent.1 = f32[2,4,16,512]{3,2,1,0:T(8,128)S(1)} custom-call(f32[4,16,2048]{2,1,0:T(8,128)S(1)} %get-tuple-element.16.density, f32[16,2048]{1,0:T(8,128)S(1)} %collective-permute-done.depth_even, f32[16,2048]{1,0:T(8,128)S(1)} %collective-permute-done.1.depth_odd, f32[4,2048]{1,0:T(4,128)S(1)} %collective-permute-done.2.row_even, ...), custom_call_target="tpu_custom_call" | custom-call | flops 2621440 | bytes 1048576 | tf_op jit(solution)/shard_map/shade_sent/pallas_call | solution.py:264
  8.7 0.1 collective-permute-start.4
  8.7 0.4 %shade_kept.1.kept = f32[2,4,16,512]{3,2,1,0:T(8,128)S(1)} custom-call(f32[4,16,2048]{2,1,0:T(8,128)S(1)} %get-tuple-element.16.density, f32[16,2048]{1,0:T(8,128)S(1)} %collective-permute-done.depth_even, f32[16,2048]{1,0:T(8,128)S(1)} %collective-permute-done.1.depth_odd, f32[4,2048]{1,0:T(4,128)S(1)} %collective-permute-done.2.row_even, ...), custom_call_target="tpu_custom_call" | custom-call | flops 2621440 | bytes 1048576 | tf_op jit(solution)/shard_map/shade_kept/pallas_call | solution.py:264
  9.1 1.1 %collective-permute-done.4.received = f32[2,4,16,512]{3,2,1,0:T(8,128)S(1)} collective-permute-done((f32[2,4,16,512]{3,2,1,0:T(8,128)S(1)}, f32[2,4,16,512]{3,2,1,0:T(8,128)S(1)}, u32[]{:S(2)}, u32[]{:S(2)}) %collective-permute-start.4) | collective-permute-done | bytes 262176 | tf_op jit(solution)/shard_map/ppermute | solution.py:279
  10.3 0.8 %collective-permute-start.5 = (f32[1,4,16,512]{3,2,1,0:T(8,128)S(1)}, f32[1,4,16,512]{3,2,1,0:T(8,128)S(1)}, u32[]{:S(2)}, u32[]{:S(2)}) collective-permute-start(f32[1,4,16,512]{3,2,1,0:T(8,128)S(1)} %get-tuple-element.26), channel_id=1, source_target_pairs={{0,16},{8,24},{16,0},{24,8},{1,17},{9,25},{17,1},{25,9},{2,18},{10... | collective-permute-start | bytes 393224 | tf_op jit(solution)/shard_map/ppermute | solution.py:279
  11.1 4.8 %collective-permute-done.5.received = f32[1,4,16,512]{3,2,1,0:T(8,128)S(1)} collective-permute-done((f32[1,4,16,512]{3,2,1,0:T(8,128)S(1)}, f32[1,4,16,512]{3,2,1,0:T(8,128)S(1)}, u32[]{:S(2)}, u32[]{:S(2)}) %collective-permute-start.5) | collective-permute-done | bytes 131104 | tf_op jit(solution)/shard_map/ppermute | solution.py:279
  15.9 0.7 %merge.3 = f32[4,16,512]{2,1,0:T(8,128)} custom-call(f32[1,4,16,512]{3,2,1,0:T(8,128)S(1)} %get-tuple-element.25.kept, f32[1,4,16,512]{3,2,1,0:T(8,128)S(1)} %collective-permute-done.5.received), custom_call_target="tpu_custom_call" | custom-call | tf_op jit(solution)/shard_map/merge/pallas_call | solution.py:283
  (1 shorter events, 0.0 us)
Async XLA Ops:
  1.3 7.0 %collective-permute-start = (f32[16,2048]{1,0:T(8,128)S(1)}, f32[16,2048]{1,0:T(8,128)S(1)}, u32[]{:S(2)}, u32[]{:S(2)}) collective-permute-start(f32[16,2048]{1,0:T(8,128)S(1)} %get-tuple-element.17), channel_id=1, source_target_pairs={{0,8},{1,9},{2,10},{3,11},{4,12},{5,13},{6,14},{7,15},{8,0},{9,1},... | collective-permute-start | bytes 393224 | tf_op jit(solution)/shard_map/ppermute | solution.py:89
  1.8 6.5 %collective-permute-start.1 = (f32[16,2048]{1,0:T(8,128)S(1)}, f32[16,2048]{1,0:T(8,128)S(1)}, u32[]{:S(2)}, u32[]{:S(2)}) collective-permute-start(f32[16,2048]{1,0:T(8,128)S(1)} %get-tuple-element.18), channel_id=1, source_target_pairs={{0,1},{1,0},{2,3},{3,2},{4,5},{5,4},{6,7},{7,6},{8,16},{9,17},{10,... | collective-permute-start | bytes 393224 | tf_op jit(solution)/shard_map/ppermute | solution.py:89
  4.3 3.9 %collective-permute-start.2 = (f32[4,2048]{1,0:T(4,128)S(1)}, f32[4,2048]{1,0:T(4,128)S(1)}, u32[]{:S(2)}, u32[]{:S(2)}) collective-permute-start(f32[4,2048]{1,0:T(4,128)S(1)} %get-tuple-element.19), channel_id=1, source_target_pairs={{0,1},{1,0},{2,3},{3,2},{4,5},{5,4},{6,7},{7,6},{8,9},{9,8},{10,11... | collective-permute-start | bytes 98312 | tf_op jit(solution)/shard_map/ppermute | solution.py:89
  4.4 3.8 %collective-permute-start.3 = (f32[4,2048]{1,0:T(4,128)S(1)}, f32[4,2048]{1,0:T(4,128)S(1)}, u32[]{:S(2)}, u32[]{:S(2)}) collective-permute-start(f32[4,2048]{1,0:T(4,128)S(1)} %get-tuple-element.20), channel_id=1, source_target_pairs={{0,8},{1,2},{2,1},{3,4},{4,3},{5,6},{6,5},{7,15},{8,0},{9,10},{10,... | collective-permute-start | bytes 98312 | tf_op jit(solution)/shard_map/ppermute | solution.py:89
  8.7 1.6 %collective-permute-start.4 = (f32[2,4,16,512]{3,2,1,0:T(8,128)S(1)}, f32[2,4,16,512]{3,2,1,0:T(8,128)S(1)}, u32[]{:S(2)}, u32[]{:S(2)}) collective-permute-start(f32[2,4,16,512]{3,2,1,0:T(8,128)S(1)} %shade_sent.1), channel_id=1, source_target_pairs={{0,8},{8,0},{16,24},{24,16},{1,9},{9,1},{17,25},{25,17},{2,10},{10... | collective-permute-start | bytes 786440 | tf_op jit(solution)/shard_map/ppermute | solution.py:279
  10.3 5.6 %collective-permute-start.5 = (f32[1,4,16,512]{3,2,1,0:T(8,128)S(1)}, f32[1,4,16,512]{3,2,1,0:T(8,128)S(1)}, u32[]{:S(2)}, u32[]{:S(2)}) collective-permute-start(f32[1,4,16,512]{3,2,1,0:T(8,128)S(1)} %get-tuple-element.26), channel_id=1, source_target_pairs={{0,16},{8,24},{16,0},{24,8},{1,17},{9,25},{17,1},{25,9},{2,18},{10... | collective-permute-start | bytes 393224 | tf_op jit(solution)/shard_map/ppermute | solution.py:279

commit v4 on v3

--- a/solution.py
+++ b/solution.py
@@ -93,33 +93,41 @@
     return (x.astype(jnp.float32) * one).astype(jnp.int32)
 
 
-def weights_kernel(count, bins, tables, weighted, passed):
-    slices, rows, cols = bins.shape
+def weights_kernel(count, bins, tables, weighted, passed_kept, passed_sent):
+    slices, rows, _ = bins.shape
+    half, _, piece = passed_kept.shape
     parts = tables.shape[0]
     table = [[tables[part, j] for j in range(2)] for part in range(parts)]
     occupied = count[0, 0]
     unit = [flag(k < occupied) * (1.0 / OPACITY_ONE) for k in range(slices)]
-    for r in range(0, rows, SUBLANES):
-        for c in range(0, cols, LANES):
-            at = (slice(r, r + SUBLANES), slice(c, c + LANES))
-            before = jnp.full((SUBLANES, LANES), 1.0 / COLOR_ONE, jnp.float32)
-            for k in range(slices):
-                index = bins[(k, *at)]
-                lane = index & (LANES - 1)
-                found = [lane_lookup(table[0][j], lane) for j in range(2)]
-                for part in range(1, parts):
-                    here = index >= part * LANES
-                    found = [
-                        jnp.where(here, lane_lookup(table[part][j], lane), found[j])
-                        for j in range(2)
-                    ]
-                alpha = (found[1] >> 16).astype(jnp.float32) * unit[k]
-                weight = before * alpha
-                weighted[(0, k, *at)] = weight * (found[0] & 0xFFFF).astype(jnp.float32)
-                weighted[(1, k, *at)] = weight * (found[0] >> 16).astype(jnp.float32)
-                weighted[(2, k, *at)] = weight * (found[1] & 0xFFFF).astype(jnp.float32)
-                before = before - weight
-            passed[at] = before * COLOR_ONE
+    mine = lax.axis_index("depth") & 1
+    for passed, parity in ((passed_sent, 1 - mine), (passed_kept, mine)):
+        for i in range(half):
+            for p in range(0, piece, LANES):
+                here = pl.ds(pl.multiple_of((2 * i + parity) * piece + p, LANES), LANES)
+                for r in range(0, rows, SUBLANES):
+                    at = (slice(r, r + SUBLANES), here)
+                    before = jnp.full((SUBLANES, LANES), 1.0 / COLOR_ONE, jnp.float32)
+                    for k in range(slices):
+                        index = bins[(k, *at)]
+                        lane = index & (LANES - 1)
+                        found = [lane_lookup(table[0][j], lane) for j in range(2)]
+                        for part in range(1, parts):
+                            later = index >= part * LANES
+                            found = [
+                                jnp.where(later, lane_lookup(table[part][j], lane), found[j])
+                                for j in range(2)
+                            ]
+                        alpha = (found[1] >> 16).astype(jnp.float32) * unit[k]
+                        weight = before * alpha
+                        red = (found[0] & 0xFFFF).astype(jnp.float32)
+                        green = (found[0] >> 16).astype(jnp.float32)
+                        blue = (found[1] & 0xFFFF).astype(jnp.float32)
+                        weighted[(0, k, *at)] = weight * red
+                        weighted[(1, k, *at)] = weight * green
+                        weighted[(2, k, *at)] = weight * blue
+                        before = before - weight
+                    passed[i, r : r + SUBLANES, p : p + LANES] = before * COLOR_ONE
 
 
 def lane_lookup(table, lane):
@@ -130,11 +138,12 @@
     return jnp.where(condition, 1.0, 0.0).astype(jnp.float32)
 
 
-def shade_kernel(keeps, density, depth_even, depth_odd, row_even, row_odd, weighted, passed, image):
+def shade_kernel(stays, density, depth_even, depth_odd, row_even, row_odd, weighted, image):
     slices, rows, cols = density.shape
-    half, _, _, piece = image.shape
+    pieces, _, _, piece = image.shape
     me = lax.axis_index("depth")
     mine = me & 1
+    bits = [(me >> i) & 1 if stays[i] else 1 - ((me >> i) & 1) for i in range(2)]
     depth_is_low = mine == 0
     tile = lax.axis_index("tile")
     tile_is_low = tile & 1 == 0
@@ -146,8 +155,8 @@
     at_top, at_bottom = sub == 0, sub == SUBLANES - 1
     groups = rows // SUBLANES
 
-    for i in range(half):
-        number = 2 * i + (mine if keeps else 1 - mine)
+    for i in range(pieces):
+        number = 4 * i + 2 * bits[1] + bits[0]
         for p in range(0, piece, LANES):
             start = pl.multiple_of(number * piece + p, LANES)
             left = pl.multiple_of(jnp.maximum(start - LANES, 0), LANES)
@@ -193,27 +202,53 @@
                 out = (slice(g * SUBLANES, (g + 1) * SUBLANES), slice(p, p + LANES))
                 for channel in range(3):
                     image[(i, channel, *out)] = sums[channel]
-                image[(i, 3, *out)] = 1.0 - passed[at]
-
-
-def merge_kernel(level, last, kept, received, *outs):
-    pieces = kept.shape[0]
+
+
+def passed_kernel(level, kept, received, *outs):
+    bit = (lax.axis_index("depth") >> (level + 1)) & 1
+    for i in range(kept.shape[0] // 2):
+        for out, j in zip(outs, (2 * i + bit, 2 * i + 1 - bit)):
+            out[i] = kept[j] * received[j]
+
+
+def first_merge_kernel(stays, kept, received, passed_kept, passed_received, out):
+    me = lax.axis_index("depth")
+    bit = (me >> 1) & 1
+    for i in range(kept.shape[0]):
+        j = 2 * i + (bit if stays else 1 - bit)
+        out[i] = merged(me & 1 == 1, kept[i], received[i], passed_kept[j], passed_received[j])
+
+
+def merged(behind, kept, received, passed_kept, passed_received):
+    front = jnp.where(behind, received, kept)
+    back = jnp.where(behind, kept, received)
+    return front + jnp.where(behind, passed_received, passed_kept)[None] * back
+
+
+def merge_kernel(level, kept, received, passed_kept, passed_received, *outs):
     me = lax.axis_index("depth")
     behind = (me >> level) & 1 == 1
-
-    def merged(piece):
-        a, b = kept[piece], received[piece]
-        front = jnp.where(behind, b, a)
-        back = jnp.where(behind, a, b)
-        return front + (1.0 - front[3:4]) * back
-
-    if last:
-        outs[0][...] = merged(0)
-        return
     bit = (me >> (level + 1)) & 1
-    for i in range(pieces // 2):
-        outs[0][i] = merged(2 * i + bit)
-        outs[1][i] = merged(2 * i + 1 - bit)
+    for i in range(kept.shape[0] // 2):
+        for out, j in zip(outs, (2 * i + bit, 2 * i + 1 - bit)):
+            out[i] = merged(behind, kept[j], received[j], passed_kept[j], passed_received[j])
+
+
+def last_merge_kernel(level, kept, received, passed_kept, passed_received, out):
+    behind = (lax.axis_index("depth") >> level) & 1 == 1
+    out[0:3] = merged(behind, kept[0], received[0], passed_kept[0], passed_received[0])
+    out[3] = 1.0 - passed_kept[0] * passed_received[0]
+
+
+def call(kernel, name, out_shape, *args):
+    return pl.pallas_call(
+        kernel,
+        out_shape=out_shape,
+        in_specs=[vmem()] * len(args),
+        out_specs=jax.tree.map(lambda _: vmem(), out_shape),
+        compiler_params=params(),
+        name=name,
+    )(*args)
 
 
 def on_device(density, bins, counts, colors, opacities):
@@ -250,47 +285,56 @@
         trade(faces[2], "tile", 0),
         trade(faces[3], "tile", 1),
     ]
-    weighted, passed = pl.pallas_call(
+    weighted, passed_kept, passed_sent = pl.pallas_call(
         weights_kernel,
-        out_shape=[f32(3, slices, rows, cols), f32(rows, cols)],
+        out_shape=[f32(3, slices, rows, cols)] + [f32(half, rows, piece)] * 2,
         in_specs=[smem(), vmem(), vmem()],
-        out_specs=[vmem(), vmem()],
+        out_specs=[vmem()] * 3,
         compiler_params=params(),
         cost_estimate=cost(64 * slices * pixels, 16 * slices * pixels),
         name="weights",
     )(counts, bins, tables)
 
-    def shaded(keeps):
+    def swap(x, level):
+        return lax.ppermute(x, "depth", [(i, i ^ 1 << level) for i in range(slab_count)])
+
+    def shaded(*stays):
         return pl.pallas_call(
-            functools.partial(shade_kernel, keeps),
-            out_shape=f32(half, 4, rows, piece),
-            in_specs=[vmem()] * 7,
+            functools.partial(shade_kernel, stays),
+            out_shape=f32(half // 2, 3, rows, piece),
+            in_specs=[vmem()] * 6,
             out_specs=vmem(),
             compiler_params=params(),
-            cost_estimate=cost(20 * slices * pixels, 8 * slices * pixels),
-            name="shade_kept" if keeps else "shade_sent",
-        )(density, *traded, weighted, passed)
-
-    outgoing = shaded(False)
+            cost_estimate=cost(10 * slices * pixels, 4 * slices * pixels),
+            name="shade",
+        )(density, *traded, weighted)
+
     levels = slab_count.bit_length() - 1
-    kept = shaded(True)
-    for level in range(levels):
-        partner = [(i, i ^ 1 << level) for i in range(slab_count)]
-        received = lax.ppermute(outgoing, "depth", partner)
-        last = level == levels - 1
-        left = kept.shape[0] // 2
-        shapes = [f32(4, rows, piece)] if last else [f32(left, 4, rows, piece)] * 2
-        merged = pl.pallas_call(
-            functools.partial(merge_kernel, level, last),
-            out_shape=shapes,
-            in_specs=[vmem()] * 2,
-            out_specs=[vmem()] * len(shapes),
-            compiler_params=params(),
-            name="merge",
-        )(kept, received)
-        if last:
-            return merged[0]
-        kept, outgoing = merged
+    passed = [(passed_kept, swap(passed_sent, 0))]
+    for level in range(levels - 1):
+        left = f32(passed[level][0].shape[0] // 2, rows, piece)
+        kernel = functools.partial(passed_kernel, level)
+        kept, sent = call(kernel, "passed", [left, left], *passed[level])
+        passed.append((kept, swap(sent, level + 1)))
+
+    def first_merge(stays):
+        received = swap(shaded(False, stays), 0)
+        kernel = functools.partial(first_merge_kernel, stays)
+        return call(
+            kernel, "first_merge", f32(half // 2, 3, rows, piece),
+            shaded(True, stays), received, *passed[0],
+        )
+
+    sent = first_merge(False)
+    received = swap(sent, 1)
+    kept = first_merge(True)
+    for level in range(1, levels - 1):
+        left = f32(kept.shape[0] // 2, 3, rows, piece)
+        kernel = functools.partial(merge_kernel, level)
+        kept, sent = call(kernel, "merge", [left, left], kept, received, *passed[level])
+        received = swap(sent, level + 1)
+    kernel = functools.partial(last_merge_kernel, levels - 1)
+    return call(kernel, "last_merge", f32(4, rows, piece), kept, received, *passed[-1])
 
 
 def solution(mesh):

time: 16.9 us -> 16.8 us (level)
  waiting for transfers between devices: 6.85 us -> 4.57 us
  starting transfers between devices: 5.28 us -> 7.3 us
    ppermute x2 -> x5, waiting for transfers between devices: 5.96 us -> 3.7 us  [swap(): lax.ppermute(x, 'depth', [(i, i ^ 1 << level) for i in range(slab_count)])]
    ppermute x2 -> x5, starting transfers between devices: 0.84 us -> 2.87 us  [swap(): lax.ppermute(x, 'depth', [(i, i ^ 1 << level) for i in range(slab_count)])]
    pallas_call x5 -> x9, Pallas kernels: 2.52 us -> 2.66 us  [the longest x1 1.04 us: on_device(): pl.pallas_call(weights_kernel, out_shape=[f32(3, slices, rows, cols)] + [...]
  transfers between devices with their start and end apart: 6 -> 9, of which waited for: 3 -> 3; matrix products, arithmetic and copies ran while one was open for 0% -> 0% of each run, Pallas kernels for 8% -> 11%
where the time goes in v4:
time: 16.8 us; the launch traced here: 16.5 us
  starting transfers between devices  7.3 us (43%)
  waiting for transfers between devices  4.57 us (27%)
  Pallas kernels  3.91 us (23%)
  between operations  0.73 us (4%)
    ppermute x4, starting transfers between devices, trade(): return lax.ppermute(x, ('depth', 'tile'), pairs)  4.44 us
    ppermute x5, waiting for transfers between devices, swap(): lax.ppermute(x, 'depth', [(i, i ^ 1 << level) for i in range(slab_count)])  3.7 us
    ppermute x5, starting transfers between devices, swap(): lax.ppermute(x, 'depth', [(i, i ^ 1 << level) for i in range(slab_count)])  2.87 us
    pallas_call x1, Pallas kernels, on_device(): pl.pallas_call(load_kernel, out_shape=[f32(*density.shape), jax.ShapeDtyp...  1.25 us
    pallas_call x1, Pallas kernels, on_device(): pl.pallas_call(weights_kernel, out_shape=[f32(3, slices, rows, cols)] + [...  1.04 us
    pallas_call x4, Pallas kernels, shaded(): pl.pallas_call(functools.partial(shade_kernel, stays), out_shape=f32(half...  0.89 us
    ppermute x4, waiting for transfers between devices, trade(): return lax.ppermute(x, ('depth', 'tile'), pairs)  0.88 us
    pallas_call x4, Pallas kernels, call(): pl.pallas_call(kernel, out_shape=out_shape, in_specs=[vmem()] * len(args)...  0.74 us
  transfers between devices with their start and end apart: 9, of which 3 were waited for; matrix products, arithmetic and copies ran while one was open for 0% of the time, Pallas kernels for 11%

profile of v4, /device:TPU:0, one launch (start us, length us, event | category | flops | bytes accessed | tf_op | source)
XLA Modules:
  0.0 16.5 jit_solution(11405691031655249495)
XLA Ops:
  0.0 1.3 %load.1 = (f32[4,16,2048]{2,1,0:T(8,128)S(1)}, s32[4,16,2048]{2,1,0:T(8,128)S(1)}, f32[16,2048]{1,0:T(8,128)S(1)}, f32[16,2048]{1,0:T(8,128)S(1)}, f32[4,2048]{1...) custom-call(f32[4,16,2048]{2,1,0:T(8,128)} %density_in.1, s32[4,16,2048]{2,1,0:T(8,128)} %bins_in.1, ...), custom_call_target="tpu_custom_call" | custom-call | tf_op jit(solution)/shard_map/load/pallas_call | solution.py:261
  1.3 0.5 %collective-permute-start = (f32[16,2048]{1,0:T(8,128)S(1)}, f32[16,2048]{1,0:T(8,128)S(1)}, u32[]{:S(2)}, u32[]{:S(2)}) collective-permute-start(f32[16,2048]{1,0:T(8,128)S(1)} %get-tuple-element.18), channel_id=1, source_target_pairs={{0,8},{1,9},{2,10},{3,11},{4,12},{5,13},{6,14},{7,15},{8,0},{9,1},... | collective-permute-start | bytes 393224 | tf_op jit(solution)/shard_map/ppermute | solution.py:89
  1.8 2.6 %collective-permute-start.1 = (f32[16,2048]{1,0:T(8,128)S(1)}, f32[16,2048]{1,0:T(8,128)S(1)}, u32[]{:S(2)}, u32[]{:S(2)}) collective-permute-start(f32[16,2048]{1,0:T(8,128)S(1)} %get-tuple-element.19), channel_id=1, source_target_pairs={{0,1},{1,0},{2,3},{3,2},{4,5},{5,4},{6,7},{7,6},{8,16},{9,17},{10,... | collective-permute-start | bytes 393224 | tf_op jit(solution)/shard_map/ppermute | solution.py:89
  4.3 0.1 collective-permute-start.2
  4.4 1.3 %collective-permute-start.3 = (f32[4,2048]{1,0:T(4,128)S(1)}, f32[4,2048]{1,0:T(4,128)S(1)}, u32[]{:S(2)}, u32[]{:S(2)}) collective-permute-start(f32[4,2048]{1,0:T(4,128)S(1)} %get-tuple-element.21), channel_id=1, source_target_pairs={{0,8},{1,2},{2,1},{3,4},{4,3},{5,6},{6,5},{7,15},{8,0},{9,10},{10,... | collective-permute-start | bytes 98312 | tf_op jit(solution)/shard_map/ppermute | solution.py:89
  6.3 1.0 %weights.1 = (f32[3,4,16,2048]{3,2,1,0:T(8,128)S(1)}, f32[2,16,512]{2,1,0:T(8,128)S(1)}, f32[2,16,512]{2,1,0:T(8,128)S(1)}) custom-call(s32[1,1]{1,0:T(1,128)S(6)} %copy.6.count, s32[4,16,2048]{2,1,0:T(8,128)S(1)} %get-tuple-element.22.bins, s32[2,2,8,128]{3,2,1,0:T(8,128)S(1)} %get-tuple-element.23.tables), custom_call_target="tpu_custom_call" | custom-call | flops 8388608 | bytes 2097152 | tf_op jit(solution)/shard_map/weights/pallas_call | solution.py:288
  7.4 0.9 %collective-permute-done.2.row_even = f32[4,2048]{1,0:T(4,128)S(1)} collective-permute-done((f32[4,2048]{1,0:T(4,128)S(1)}, f32[4,2048]{1,0:T(4,128)S(1)}, u32[]{:S(2)}, u32[]{:S(2)}) %collective-permute-start.2) | collective-permute-done | bytes 32800 | tf_op jit(solution)/shard_map/ppermute | solution.py:89
  8.3 0.0 collective-permute-done.3.row_odd
  8.3 0.0 collective-permute-done.depth_even
  8.3 0.0 collective-permute-done.1.depth_odd
  8.3 0.2 %shade.7 = f32[1,3,16,512]{3,2,1,0:T(8,128)S(1)} custom-call(f32[4,16,2048]{2,1,0:T(8,128)S(1)} %get-tuple-element.17.density, f32[16,2048]{1,0:T(8,128)S(1)} %collective-permute-done.depth_even, f32[16,2048]{1,0:T(8,128)S(1)} %collective-permute-done.1.depth_odd, f32[4,2048]{1,0:T(4,128)S(1)} %collective-permute-done.2.row_even, ...), custom_call_target="tpu_custom_call" | custom-call | flops 1310720 | bytes 524288 | tf_op jit(solution)/shard_map/shade/pallas_call | solution.py:302
  8.5 0.1 collective-permute-start.6
  8.6 0.5 %collective-permute-start.5 = (f32[2,16,512]{2,1,0:T(8,128)S(1)}, f32[2,16,512]{2,1,0:T(8,128)S(1)}, u32[]{:S(2)}, u32[]{:S(2)}) collective-permute-start(f32[2,16,512]{2,1,0:T(8,128)S(1)} %get-tuple-element.26), channel_id=1, source_target_pairs={{0,8},{8,0},{16,24},{24,16},{1,9},{9,1},{17,25},{25,17},{2,10},{10... | collective-permute-start | bytes 196616 | tf_op jit(solution)/shard_map/ppermute | solution.py:299
  9.1 0.2 %shade.5 = f32[1,3,16,512]{3,2,1,0:T(8,128)S(1)} custom-call(f32[4,16,2048]{2,1,0:T(8,128)S(1)} %get-tuple-element.17.density, f32[16,2048]{1,0:T(8,128)S(1)} %collective-permute-done.depth_even, f32[16,2048]{1,0:T(8,128)S(1)} %collective-permute-done.1.depth_odd, f32[4,2048]{1,0:T(4,128)S(1)} %collective-permute-done.2.row_even, ...), custom_call_target="tpu_custom_call" | custom-call | flops 1310720 | bytes 524288 | tf_op jit(solution)/shard_map/shade/pallas_call | solution.py:302
  9.3 0.1 collective-permute-start.4
  9.5 0.2 %shade.6.kept = f32[1,3,16,512]{3,2,1,0:T(8,128)S(1)} custom-call(f32[4,16,2048]{2,1,0:T(8,128)S(1)} %get-tuple-element.17.density, f32[16,2048]{1,0:T(8,128)S(1)} %collective-permute-done.depth_even, f32[16,2048]{1,0:T(8,128)S(1)} %collective-permute-done.1.depth_odd, f32[4,2048]{1,0:T(4,128)S(1)} %collective-permute-done.2.row_even, ...), custom_call_target="tpu_custom_call" | custom-call | flops 1310720 | bytes 524288 | tf_op jit(solution)/shard_map/shade/pallas_call | solution.py:302
  9.7 0.3 %collective-permute-done.5.passed_received.received = f32[2,16,512]{2,1,0:T(8,128)S(1)} collective-permute-done((f32[2,16,512]{2,1,0:T(8,128)S(1)}, f32[2,16,512]{2,1,0:T(8,128)S(1)}, u32[]{:S(2)}, u32[]{:S(2)}) %collective-permute-start.5) | collective-permute-done | bytes 65568 | tf_op jit(solution)/shard_map/ppermute | solution.py:299
  10.0 0.0 collective-permute-done.6.received
  10.0 1.0 %collective-permute-start.7 = (f32[1,3,16,512]{3,2,1,0:T(8,128)S(1)}, f32[1,3,16,512]{3,2,1,0:T(8,128)S(1)}, u32[]{:S(2)}, u32[]{:S(2)}) collective-permute-start(f32[1,3,16,512]{3,2,1,0:T(8,128)S(1)} %first_merge.3), channel_id=1, source_target_pairs={{0,16},{8,24},{16,0},{24,8},{1,17},{9,25},{17,1},{25,9},{2,18},{10... | collective-permute-start | bytes 294920 | tf_op jit(solution)/shard_map/ppermute | solution.py:299
  11.0 1.2 %collective-permute-start.8 = (f32[1,16,512]{2,1,0:T(8,128)S(1)}, f32[1,16,512]{2,1,0:T(8,128)S(1)}, u32[]{:S(2)}, u32[]{:S(2)}) collective-permute-start(f32[1,16,512]{2,1,0:T(8,128)S(1)} %get-tuple-element.28), channel_id=1, source_target_pairs={{0,16},{8,24},{16,0},{24,8},{1,17},{9,25},{17,1},{25,9},{2,18},{10... | collective-permute-start | bytes 98312 | tf_op jit(solution)/shard_map/ppermute | solution.py:299
  12.2 0.2 %shade.4.kept = f32[1,3,16,512]{3,2,1,0:T(8,128)S(1)} custom-call(f32[4,16,2048]{2,1,0:T(8,128)S(1)} %get-tuple-element.17.density, f32[16,2048]{1,0:T(8,128)S(1)} %collective-permute-done.depth_even, f32[16,2048]{1,0:T(8,128)S(1)} %collective-permute-done.1.depth_odd, f32[4,2048]{1,0:T(4,128)S(1)} %collective-permute-done.2.row_even, ...), custom_call_target="tpu_custom_call" | custom-call | flops 1310720 | bytes 524288 | tf_op jit(solution)/shard_map/shade/pallas_call | solution.py:302
  12.4 0.0 collective-permute-done.4.received
  12.5 3.4 %collective-permute-done.8.passed_received = f32[1,16,512]{2,1,0:T(8,128)S(1)} collective-permute-done((f32[1,16,512]{2,1,0:T(8,128)S(1)}, f32[1,16,512]{2,1,0:T(8,128)S(1)}, u32[]{:S(2)}, u32[]{:S(2)}) %collective-permute-start.8) | collective-permute-done | bytes 32800 | tf_op jit(solution)/shard_map/ppermute | solution.py:299
  15.8 0.7 %last_merge.1 = f32[4,16,512]{2,1,0:T(8,128)} custom-call(f32[1,3,16,512]{3,2,1,0:T(8,128)S(1)} %first_merge.2.kept, f32[1,3,16,512]{3,2,1,0:T(8,128)S(1)} %collective-permute-done.7.received, f32[1,16,512]{2,1,0:T(8,128)S(1)} %get-tuple-element.27.passed_kept, f32[1,16,512]{2,1,0:T(8,128)S(1)} %collective-permute-done.8.passed_received), custom_call_target="tpu_custom_call" | custom-call | tf_op jit(solution)/shard_map/last_merge/pallas_call | solution.py:244
  (4 shorter events, 0.1 us)
Async XLA Ops:
  1.3 7.0 %collective-permute-start = (f32[16,2048]{1,0:T(8,128)S(1)}, f32[16,2048]{1,0:T(8,128)S(1)}, u32[]{:S(2)}, u32[]{:S(2)}) collective-permute-start(f32[16,2048]{1,0:T(8,128)S(1)} %get-tuple-element.18), channel_id=1, source_target_pairs={{0,8},{1,9},{2,10},{3,11},{4,12},{5,13},{6,14},{7,15},{8,0},{9,1},... | collective-permute-start | bytes 393224 | tf_op jit(solution)/shard_map/ppermute | solution.py:89
  1.8 6.5 %collective-permute-start.1 = (f32[16,2048]{1,0:T(8,128)S(1)}, f32[16,2048]{1,0:T(8,128)S(1)}, u32[]{:S(2)}, u32[]{:S(2)}) collective-permute-start(f32[16,2048]{1,0:T(8,128)S(1)} %get-tuple-element.19), channel_id=1, source_target_pairs={{0,1},{1,0},{2,3},{3,2},{4,5},{5,4},{6,7},{7,6},{8,16},{9,17},{10,... | collective-permute-start | bytes 393224 | tf_op jit(solution)/shard_map/ppermute | solution.py:89
  4.3 3.9 %collective-permute-start.2 = (f32[4,2048]{1,0:T(4,128)S(1)}, f32[4,2048]{1,0:T(4,128)S(1)}, u32[]{:S(2)}, u32[]{:S(2)}) collective-permute-start(f32[4,2048]{1,0:T(4,128)S(1)} %get-tuple-element.20), channel_id=1, source_target_pairs={{0,1},{1,0},{2,3},{3,2},{4,5},{5,4},{6,7},{7,6},{8,9},{9,8},{10,11... | collective-permute-start | bytes 98312 | tf_op jit(solution)/shard_map/ppermute | solution.py:89
  4.4 3.8 %collective-permute-start.3 = (f32[4,2048]{1,0:T(4,128)S(1)}, f32[4,2048]{1,0:T(4,128)S(1)}, u32[]{:S(2)}, u32[]{:S(2)}) collective-permute-start(f32[4,2048]{1,0:T(4,128)S(1)} %get-tuple-element.21), channel_id=1, source_target_pairs={{0,8},{1,2},{2,1},{3,4},{4,3},{5,6},{6,5},{7,15},{8,0},{9,10},{10,... | collective-permute-start | bytes 98312 | tf_op jit(solution)/shard_map/ppermute | solution.py:89
  8.5 1.5 %collective-permute-start.6 = (f32[1,3,16,512]{3,2,1,0:T(8,128)S(1)}, f32[1,3,16,512]{3,2,1,0:T(8,128)S(1)}, u32[]{:S(2)}, u32[]{:S(2)}) collective-permute-start(f32[1,3,16,512]{3,2,1,0:T(8,128)S(1)} %shade.7), channel_id=1, source_target_pairs={{0,8},{8,0},{16,24},{24,16},{1,9},{9,1},{17,25},{25,17},{2,10},{10... | collective-permute-start | bytes 294920 | tf_op jit(solution)/shard_map/ppermute | solution.py:299
  8.6 1.4 %collective-permute-start.5 = (f32[2,16,512]{2,1,0:T(8,128)S(1)}, f32[2,16,512]{2,1,0:T(8,128)S(1)}, u32[]{:S(2)}, u32[]{:S(2)}) collective-permute-start(f32[2,16,512]{2,1,0:T(8,128)S(1)} %get-tuple-element.26), channel_id=1, source_target_pairs={{0,8},{8,0},{16,24},{24,16},{1,9},{9,1},{17,25},{25,17},{2,10},{10... | collective-permute-start | bytes 196616 | tf_op jit(solution)/shard_map/ppermute | solution.py:299
  9.3 3.1 %collective-permute-start.4 = (f32[1,3,16,512]{3,2,1,0:T(8,128)S(1)}, f32[1,3,16,512]{3,2,1,0:T(8,128)S(1)}, u32[]{:S(2)}, u32[]{:S(2)}) collective-permute-start(f32[1,3,16,512]{3,2,1,0:T(8,128)S(1)} %shade.5), channel_id=1, source_target_pairs={{0,8},{8,0},{16,24},{24,16},{1,9},{9,1},{17,25},{25,17},{2,10},{10... | collective-permute-start | bytes 294920 | tf_op jit(solution)/shard_map/ppermute | solution.py:299
  10.0 5.8 %collective-permute-start.7 = (f32[1,3,16,512]{3,2,1,0:T(8,128)S(1)}, f32[1,3,16,512]{3,2,1,0:T(8,128)S(1)}, u32[]{:S(2)}, u32[]{:S(2)}) collective-permute-start(f32[1,3,16,512]{3,2,1,0:T(8,128)S(1)} %first_merge.3), channel_id=1, source_target_pairs={{0,16},{8,24},{16,0},{24,8},{1,17},{9,25},{17,1},{25,9},{2,18},{10... | collective-permute-start | bytes 294920 | tf_op jit(solution)/shard_map/ppermute | solution.py:299
  11.0 4.8 %collective-permute-start.8 = (f32[1,16,512]{2,1,0:T(8,128)S(1)}, f32[1,16,512]{2,1,0:T(8,128)S(1)}, u32[]{:S(2)}, u32[]{:S(2)}) collective-permute-start(f32[1,16,512]{2,1,0:T(8,128)S(1)} %get-tuple-element.28), channel_id=1, source_target_pairs={{0,16},{8,24},{16,0},{24,8},{1,17},{9,25},{17,1},{25,9},{2,18},{10... | collective-permute-start | bytes 98312 | tf_op jit(solution)/shard_map/ppermute | solution.py:299

commit v5 on v3

--- a/solution.py
+++ b/solution.py
@@ -43,19 +43,17 @@
     density, bins, depth_even, depth_odd, row_even, row_odd, tables,
     colors, opacities, done,
 ):
-    moves = [
-        (density_in, density),
-        (bins_in, bins),
-        (colors_in, colors),
-        (opacities_in, opacities),
-    ]
+    slices, rows, _ = density.shape
+    moves = [(density_in.at[k], density.at[k]) for k in range(slices)]
+    moves += [(bins_in.at[k], bins.at[k]) for k in range(slices)]
+    moves += [(colors_in, colors), (opacities_in, opacities)]
     copies = [pltpu.make_async_copy(a, b, done.at[i]) for i, (a, b) in enumerate(moves)]
     for copy in copies:
         copy.start()
-    slices, rows, _ = density.shape
     depth_low = lax.axis_index("depth") & 1 == 0
     tile_low = lax.axis_index("tile") & 1 == 0
-    copies[0].wait()
+    for copy in copies[:slices]:
+        copy.wait()
     first, last = density[0], density[slices - 1]
     depth_even[...] = jnp.where(depth_low, last, first)
     depth_odd[...] = jnp.where(depth_low, first, last)
@@ -63,7 +61,7 @@
         top, bottom = density[k, 0:1], density[k, rows - 1 : rows]
         row_even[k : k + 1] = jnp.where(tile_low, bottom, top)
         row_odd[k : k + 1] = jnp.where(tile_low, top, bottom)
-    for copy in copies[1:]:
+    for copy in copies[slices:]:
         copy.wait()
     color = whole_number(colors[...], COLOR_ONE)
     opacity = whole_number(opacities[...].reshape(1, -1), OPACITY_ONE)
@@ -108,9 +106,9 @@
                 lane = index & (LANES - 1)
                 found = [lane_lookup(table[0][j], lane) for j in range(2)]
                 for part in range(1, parts):
-                    here = index >= part * LANES
+                    later = index >= part * LANES
                     found = [
-                        jnp.where(here, lane_lookup(table[part][j], lane), found[j])
+                        jnp.where(later, lane_lookup(table[part][j], lane), found[j])
                         for j in range(2)
                     ]
                 alpha = (found[1] >> 16).astype(jnp.float32) * unit[k]
@@ -130,11 +128,12 @@
     return jnp.where(condition, 1.0, 0.0).astype(jnp.float32)
 
 
-def shade_kernel(keeps, density, depth_even, depth_odd, row_even, row_odd, weighted, passed, image):
+def shade_kernel(stays, top, density, depth_even, depth_odd, row_even, row_odd, weighted, passed, image):
     slices, rows, cols = density.shape
-    half, _, _, piece = image.shape
+    pieces, _, image_rows, piece = image.shape
     me = lax.axis_index("depth")
     mine = me & 1
+    bits = [(me >> i) & 1 if stays[i] else 1 - ((me >> i) & 1) for i in range(2)]
     depth_is_low = mine == 0
     tile = lax.axis_index("tile")
     tile_is_low = tile & 1 == 0
@@ -146,8 +145,8 @@
     at_top, at_bottom = sub == 0, sub == SUBLANES - 1
     groups = rows // SUBLANES
 
-    for i in range(half):
-        number = 2 * i + (mine if keeps else 1 - mine)
+    for i in range(pieces):
+        number = 4 * i + 2 * bits[1] + bits[0]
         for p in range(0, piece, LANES):
             start = pl.multiple_of(number * piece + p, LANES)
             left = pl.multiple_of(jnp.maximum(start - LANES, 0), LANES)
@@ -158,7 +157,7 @@
             even_rows, odd_rows = row_even[:, here], row_odd[:, here]
             above_rows = jnp.where(tile_is_low, odd_rows, even_rows) * has_above
             below_rows = jnp.where(tile_is_low, even_rows, odd_rows) * has_below
-            for g in range(groups):
+            for g in range(top // SUBLANES, (top + image_rows) // SUBLANES):
                 at = (slice(g * SUBLANES, (g + 1) * SUBLANES), here)
                 even_face, odd_face = depth_even[at], depth_odd[at]
                 column = [jnp.where(depth_is_low, odd_face, even_face) * has_front]
@@ -190,30 +189,62 @@
                     shade = 0.3 + facing * lax.rsqrt(jnp.maximum(square, 4.0))
                     for channel in range(3):
                         sums[channel] = sums[channel] + weighted[(channel, k, *at)] * shade
-                out = (slice(g * SUBLANES, (g + 1) * SUBLANES), slice(p, p + LANES))
+                r = g * SUBLANES - top
+                out = (slice(r, r + SUBLANES), slice(p, p + LANES))
                 for channel in range(3):
                     image[(i, channel, *out)] = sums[channel]
-                image[(i, 3, *out)] = 1.0 - passed[at]
-
-
-def merge_kernel(level, last, kept, received, *outs):
-    pieces = kept.shape[0]
+                image[(i, 3, *out)] = passed[at]
+
+
+def merged(behind, kept, received):
+    front = jnp.where(behind, received, kept)
+    back = jnp.where(behind, kept, received)
+    light = front[0:3] + front[3:4] * back[0:3]
+    return light, front[3] * back[3]
+
+
+def first_merge_kernel(kept, received, out):
+    behind = lax.axis_index("depth") & 1 == 1
+    for i in range(kept.shape[0]):
+        out[i, 0:3], out[i, 3] = merged(behind, kept[i], received[i])
+
+
+def merge_kernel(level, bands, kept, *rest):
     me = lax.axis_index("depth")
     behind = (me >> level) & 1 == 1
-
-    def merged(piece):
-        a, b = kept[piece], received[piece]
-        front = jnp.where(behind, b, a)
-        back = jnp.where(behind, a, b)
-        return front + (1.0 - front[3:4]) * back
-
-    if last:
-        outs[0][...] = merged(0)
-        return
     bit = (me >> (level + 1)) & 1
-    for i in range(pieces // 2):
-        outs[0][i] = merged(2 * i + bit)
-        outs[1][i] = merged(2 * i + 1 - bit)
+    received, (kept_out, *sent) = rest[:bands], rest[bands:]
+    height = kept.shape[2] // bands
+    for i in range(kept.shape[0] // 2):
+        for band in range(bands):
+            rows = slice(band * height, (band + 1) * height)
+            j = 2 * i + bit
+            light, through = merged(behind, kept[j, :, rows], received[band][j])
+            kept_out[i, 0:3, rows], kept_out[i, 3, rows] = light, through
+            j = 2 * i + 1 - bit
+            light, through = merged(behind, kept[j, :, rows], received[band][j])
+            sent[band][i, 0:3], sent[band][i, 3] = light, through
+
+
+def last_merge_kernel(level, bands, kept, *rest):
+    behind = (lax.axis_index("depth") >> level) & 1 == 1
+    received, out = rest[:bands], rest[bands]
+    height = kept.shape[2] // bands
+    for band in range(bands):
+        rows = slice(band * height, (band + 1) * height)
+        light, through = merged(behind, kept[0, :, rows], received[band][0])
+        out[0:3, rows], out[3, rows] = light, 1.0 - through
+
+
+def call(kernel, name, out_shape, *args):
+    return pl.pallas_call(
+        kernel,
+        out_shape=out_shape,
+        in_specs=[vmem()] * len(args),
+        out_specs=jax.tree.map(lambda _: vmem(), out_shape),
+        compiler_params=params(),
+        name=name,
+    )(*args)
 
 
 def on_device(density, bins, counts, colors, opacities):
@@ -239,7 +270,7 @@
         scratch_shapes=[
             pltpu.VMEM(colors.shape, colors.dtype),
             pltpu.VMEM(opacities.shape, opacities.dtype),
-            pltpu.SemaphoreType.DMA((4,)),
+            pltpu.SemaphoreType.DMA((2 * slices + 2,)),
         ],
         compiler_params=params(),
         name="load",
@@ -254,43 +285,43 @@
         weights_kernel,
         out_shape=[f32(3, slices, rows, cols), f32(rows, cols)],
         in_specs=[smem(), vmem(), vmem()],
-        out_specs=[vmem(), vmem()],
+        out_specs=[vmem()] * 2,
         compiler_params=params(),
         cost_estimate=cost(64 * slices * pixels, 16 * slices * pixels),
         name="weights",
     )(counts, bins, tables)
 
-    def shaded(keeps):
+    def swap(x, level):
+        return lax.ppermute(x, "depth", [(i, i ^ 1 << level) for i in range(slab_count)])
+
+    def shaded(stays, top, height):
         return pl.pallas_call(
-            functools.partial(shade_kernel, keeps),
-            out_shape=f32(half, 4, rows, piece),
+            functools.partial(shade_kernel, stays, top),
+            out_shape=f32(half // 2, 4, height, piece),
             in_specs=[vmem()] * 7,
             out_specs=vmem(),
             compiler_params=params(),
-            cost_estimate=cost(20 * slices * pixels, 8 * slices * pixels),
-            name="shade_kept" if keeps else "shade_sent",
+            cost_estimate=cost(5 * slices * pixels, 2 * slices * pixels),
+            name="shade",
         )(density, *traded, weighted, passed)
 
-    outgoing = shaded(False)
+    def first_merge(stays, top, height):
+        received = swap(shaded((False, stays), top, height), 0)
+        kept = shaded((True, stays), top, height)
+        return call(first_merge_kernel, "first_merge", f32(half // 2, 4, height, piece), kept, received)
+
     levels = slab_count.bit_length() - 1
-    kept = shaded(True)
-    for level in range(levels):
-        partner = [(i, i ^ 1 << level) for i in range(slab_count)]
-        received = lax.ppermute(outgoing, "depth", partner)
-        last = level == levels - 1
+    bands = rows // SUBLANES
+    received = [swap(first_merge(False, band * SUBLANES, SUBLANES), 1) for band in range(bands)]
+    kept = first_merge(True, 0, rows)
+    for level in range(1, levels - 1):
         left = kept.shape[0] // 2
-        shapes = [f32(4, rows, piece)] if last else [f32(left, 4, rows, piece)] * 2
-        merged = pl.pallas_call(
-            functools.partial(merge_kernel, level, last),
-            out_shape=shapes,
-            in_specs=[vmem()] * 2,
-            out_specs=[vmem()] * len(shapes),
-            compiler_params=params(),
-            name="merge",
-        )(kept, received)
-        if last:
-            return merged[0]
-        kept, outgoing = merged
+        shapes = [f32(left, 4, rows, piece)] + [f32(left, 4, SUBLANES, piece)] * bands
+        kernel = functools.partial(merge_kernel, level, bands)
+        kept, *sent = call(kernel, "merge", shapes, kept, *received)
+        received = [swap(x, level + 1) for x in sent]
+    kernel = functools.partial(last_merge_kernel, levels - 1, bands)
+    return call(kernel, "last_merge", f32(4, rows, piece), kept, *received)
 
 
 def solution(mesh):

time: 16.9 us -> 17 us (level)
  waiting for transfers between devices: 6.85 us -> 4.39 us
  starting transfers between devices: 5.28 us -> 7.3 us
  Pallas kernels: 3.77 us -> 4.24 us
    ppermute x2 -> x5, waiting for transfers between devices: 5.96 us -> 3.5 us  [swap(): lax.ppermute(x, 'depth', [(i, i ^ 1 << level) for i in range(slab_count)])]
    ppermute x2 -> x5, starting transfers between devices: 0.84 us -> 2.87 us  [swap(): lax.ppermute(x, 'depth', [(i, i ^ 1 << level) for i in range(slab_count)])]
    pallas_call x4 -> x10, Pallas kernels: 1.49 us -> 1.83 us  [the longest x6 1.08 us: shaded(): pl.pallas_call(functools.partial(shade_kernel, stays, top), out_shape=f32...]
  transfers between devices with their start and end apart: 6 -> 9, of which waited for: 3 -> 3; matrix products, arithmetic and copies ran while one was open for 0% -> 0% of each run, Pallas kernels for 8% -> 12%
where the time goes in v5:
time: 17 us; the launch traced here: 16.7 us
  starting transfers between devices  7.3 us (43%)
  waiting for transfers between devices  4.39 us (26%)
  Pallas kernels  4.24 us (25%)
  between operations  0.75 us (4%)
    ppermute x4, starting transfers between devices, trade(): return lax.ppermute(x, ('depth', 'tile'), pairs)  4.44 us
    ppermute x5, waiting for transfers between devices, swap(): lax.ppermute(x, 'depth', [(i, i ^ 1 << level) for i in range(slab_count)])  3.5 us
    ppermute x5, starting transfers between devices, swap(): lax.ppermute(x, 'depth', [(i, i ^ 1 << level) for i in range(slab_count)])  2.87 us
    pallas_call x1, Pallas kernels, on_device(): pl.pallas_call(load_kernel, out_shape=[f32(*density.shape), jax.ShapeDtyp...  1.38 us
    pallas_call x6, Pallas kernels, shaded(): pl.pallas_call(functools.partial(shade_kernel, stays, top), out_shape=f32...  1.08 us
    pallas_call x1, Pallas kernels, on_device(): pl.pallas_call(weights_kernel, out_shape=[f32(3, slices, rows, cols), f32...  1.02 us
    ppermute x4, waiting for transfers between devices, trade(): return lax.ppermute(x, ('depth', 'tile'), pairs)  0.89 us
    pallas_call x4, Pallas kernels, call(): pl.pallas_call(kernel, out_shape=out_shape, in_specs=[vmem()] * len(args)...  0.75 us
  transfers between devices with their start and end apart: 9, of which 3 were waited for; matrix products, arithmetic and copies ran while one was open for 0% of the time, Pallas kernels for 12%

profile of v5, /device:TPU:0, one launch (start us, length us, event | category | flops | bytes accessed | tf_op | source)
XLA Modules:
  0.0 16.7 jit_solution(6480933283595022154)
XLA Ops:
  0.0 1.4 %load.1 = (f32[4,16,2048]{2,1,0:T(8,128)S(1)}, s32[4,16,2048]{2,1,0:T(8,128)S(1)}, f32[16,2048]{1,0:T(8,128)S(1)}, f32[16,2048]{1,0:T(8,128)S(1)}, f32[4,2048]{1...) custom-call(f32[4,16,2048]{2,1,0:T(8,128)} %density_in.1, s32[4,16,2048]{2,1,0:T(8,128)} %bins_in.1, ...), custom_call_target="tpu_custom_call" | custom-call | tf_op jit(solution)/shard_map/load/pallas_call | solution.py:257
  1.4 0.5 %collective-permute-start = (f32[16,2048]{1,0:T(8,128)S(1)}, f32[16,2048]{1,0:T(8,128)S(1)}, u32[]{:S(2)}, u32[]{:S(2)}) collective-permute-start(f32[16,2048]{1,0:T(8,128)S(1)} %get-tuple-element.15), channel_id=1, source_target_pairs={{0,8},{1,9},{2,10},{3,11},{4,12},{5,13},{6,14},{7,15},{8,0},{9,1},... | collective-permute-start | bytes 393224 | tf_op jit(solution)/shard_map/ppermute | solution.py:87
  1.9 2.6 %collective-permute-start.1 = (f32[16,2048]{1,0:T(8,128)S(1)}, f32[16,2048]{1,0:T(8,128)S(1)}, u32[]{:S(2)}, u32[]{:S(2)}) collective-permute-start(f32[16,2048]{1,0:T(8,128)S(1)} %get-tuple-element.16), channel_id=1, source_target_pairs={{0,1},{1,0},{2,3},{3,2},{4,5},{5,4},{6,7},{7,6},{8,16},{9,17},{10,... | collective-permute-start | bytes 393224 | tf_op jit(solution)/shard_map/ppermute | solution.py:87
  4.5 0.1 collective-permute-start.2
  4.6 1.3 %collective-permute-start.3 = (f32[4,2048]{1,0:T(4,128)S(1)}, f32[4,2048]{1,0:T(4,128)S(1)}, u32[]{:S(2)}, u32[]{:S(2)}) collective-permute-start(f32[4,2048]{1,0:T(4,128)S(1)} %get-tuple-element.18), channel_id=1, source_target_pairs={{0,8},{1,2},{2,1},{3,4},{4,3},{5,6},{6,5},{7,15},{8,0},{9,10},{10,... | collective-permute-start | bytes 98312 | tf_op jit(solution)/shard_map/ppermute | solution.py:87
  6.5 1.0 %weights.1 = (f32[3,4,16,2048]{3,2,1,0:T(8,128)S(1)}, f32[16,2048]{1,0:T(8,128)S(1)}) custom-call(s32[1,1]{1,0:T(1,128)S(6)} %copy.6.count, s32[4,16,2048]{2,1,0:T(8,128)S(1)} %get-tuple-element.19.bins, s32[2,2,8,128]{3,2,1,0:T(8,128)S(1)} %get-tuple-element.20.tables), custom_call_target="tpu_custom_call" | custom-call | flops 8388608 | bytes 2097152 | tf_op jit(solution)/shard_map/weights/pallas_call | solution.py:284
  7.5 0.9 %collective-permute-done.2.row_even = f32[4,2048]{1,0:T(4,128)S(1)} collective-permute-done((f32[4,2048]{1,0:T(4,128)S(1)}, f32[4,2048]{1,0:T(4,128)S(1)}, u32[]{:S(2)}, u32[]{:S(2)}) %collective-permute-start.2) | collective-permute-done | bytes 32800 | tf_op jit(solution)/shard_map/ppermute | solution.py:87
  8.4 0.0 collective-permute-done.1.depth_odd
  8.4 0.2 shade.9
  8.6 0.1 collective-permute-start.5
  8.7 0.2 %shade.7 = f32[1,4,16,512]{3,2,1,0:T(8,128)S(1)} custom-call(f32[4,16,2048]{2,1,0:T(8,128)S(1)} %get-tuple-element.14.density, f32[16,2048]{1,0:T(8,128)S(1)} %collective-permute-done.depth_even, f32[16,2048]{1,0:T(8,128)S(1)} %collective-permute-done.1.depth_odd, f32[4,2048]{1,0:T(4,128)S(1)} %collective-permute-done.2.row_even, ...), custom_call_target="tpu_custom_call" | custom-call | flops 655360 | bytes 262144 | tf_op jit(solution)/shard_map/shade/pallas_call | solution.py:298
  8.9 0.5 %collective-permute-start.4 = (f32[1,4,16,512]{3,2,1,0:T(8,128)S(1)}, f32[1,4,16,512]{3,2,1,0:T(8,128)S(1)}, u32[]{:S(2)}, u32[]{:S(2)}) collective-permute-start(f32[1,4,16,512]{3,2,1,0:T(8,128)S(1)} %shade.7), channel_id=1, source_target_pairs={{0,8},{8,0},{16,24},{24,16},{1,9},{9,1},{17,25},{25,17},{2,10},{10... | collective-permute-start | bytes 393224 | tf_op jit(solution)/shard_map/ppermute | solution.py:295
  9.4 0.2 shade.11
  9.6 0.1 collective-permute-start.7
  9.7 0.2 shade.10.kept
  9.8 0.2 shade.8.kept
  10.0 0.0 collective-permute-done.5.received
  10.0 1.1 %collective-permute-start.6 = (f32[1,4,8,512]{3,2,1,0:T(8,128)S(1)}, f32[1,4,8,512]{3,2,1,0:T(8,128)S(1)}, u32[]{:S(2)}, u32[]{:S(2)}) collective-permute-start(f32[1,4,8,512]{3,2,1,0:T(8,128)S(1)} %first_merge.4), channel_id=1, source_target_pairs={{0,16},{8,24},{16,0},{24,8},{1,17},{9,25},{17,1},{25,9},{2,18},{10... | collective-permute-start | bytes 196616 | tf_op jit(solution)/shard_map/ppermute | solution.py:295
  11.2 1.1 %collective-permute-start.8 = (f32[1,4,8,512]{3,2,1,0:T(8,128)S(1)}, f32[1,4,8,512]{3,2,1,0:T(8,128)S(1)}, u32[]{:S(2)}, u32[]{:S(2)}) collective-permute-start(f32[1,4,8,512]{3,2,1,0:T(8,128)S(1)} %first_merge.5), channel_id=1, source_target_pairs={{0,16},{8,24},{16,0},{24,8},{1,17},{9,25},{17,1},{25,9},{2,18},{10... | collective-permute-start | bytes 196616 | tf_op jit(solution)/shard_map/ppermute | solution.py:295
  12.2 0.2 %shade.6.kept = f32[1,4,16,512]{3,2,1,0:T(8,128)S(1)} custom-call(f32[4,16,2048]{2,1,0:T(8,128)S(1)} %get-tuple-element.14.density, f32[16,2048]{1,0:T(8,128)S(1)} %collective-permute-done.depth_even, f32[16,2048]{1,0:T(8,128)S(1)} %collective-permute-done.1.depth_odd, f32[4,2048]{1,0:T(4,128)S(1)} %collective-permute-done.2.row_even, ...), custom_call_target="tpu_custom_call" | custom-call | flops 655360 | bytes 262144 | tf_op jit(solution)/shard_map/shade/pallas_call | solution.py:298
  12.5 0.0 collective-permute-done.4.received
  12.5 2.5 %collective-permute-done.6.rest_0_ = f32[1,4,8,512]{3,2,1,0:T(8,128)S(1)} collective-permute-done((f32[1,4,8,512]{3,2,1,0:T(8,128)S(1)}, f32[1,4,8,512]{3,2,1,0:T(8,128)S(1)}, u32[]{:S(2)}, u32[]{:S(2)}) %collective-permute-start.6) | collective-permute-done | bytes 65568 | tf_op jit(solution)/shard_map/ppermute | solution.py:295
  15.0 1.0 %collective-permute-done.8.rest_1_ = f32[1,4,8,512]{3,2,1,0:T(8,128)S(1)} collective-permute-done((f32[1,4,8,512]{3,2,1,0:T(8,128)S(1)}, f32[1,4,8,512]{3,2,1,0:T(8,128)S(1)}, u32[]{:S(2)}, u32[]{:S(2)}) %collective-permute-start.8) | collective-permute-done | bytes 65568 | tf_op jit(solution)/shard_map/ppermute | solution.py:295
  16.0 0.7 %last_merge.1 = f32[4,16,512]{2,1,0:T(8,128)} custom-call(f32[1,4,16,512]{3,2,1,0:T(8,128)S(1)} %first_merge.3.kept, f32[1,4,8,512]{3,2,1,0:T(8,128)S(1)} %collective-permute-done.6.rest_0_, f32[1,4,8,512]{3,2,1,0:T(8,128)S(1)} %collective-permute-done.8.rest_1_), custom_call_target="tpu_custom_call" | custom-call | tf_op jit(solution)/shard_map/last_merge/pallas_call | solution.py:240
  (6 shorter events, 0.1 us)
Async XLA Ops:
  1.4 7.0 %collective-permute-start = (f32[16,2048]{1,0:T(8,128)S(1)}, f32[16,2048]{1,0:T(8,128)S(1)}, u32[]{:S(2)}, u32[]{:S(2)}) collective-permute-start(f32[16,2048]{1,0:T(8,128)S(1)} %get-tuple-element.15), channel_id=1, source_target_pairs={{0,8},{1,9},{2,10},{3,11},{4,12},{5,13},{6,14},{7,15},{8,0},{9,1},... | collective-permute-start | bytes 393224 | tf_op jit(solution)/shard_map/ppermute | solution.py:87
  1.9 6.5 %collective-permute-start.1 = (f32[16,2048]{1,0:T(8,128)S(1)}, f32[16,2048]{1,0:T(8,128)S(1)}, u32[]{:S(2)}, u32[]{:S(2)}) collective-permute-start(f32[16,2048]{1,0:T(8,128)S(1)} %get-tuple-element.16), channel_id=1, source_target_pairs={{0,1},{1,0},{2,3},{3,2},{4,5},{5,4},{6,7},{7,6},{8,16},{9,17},{10,... | collective-permute-start | bytes 393224 | tf_op jit(solution)/shard_map/ppermute | solution.py:87
  4.5 3.9 %collective-permute-start.2 = (f32[4,2048]{1,0:T(4,128)S(1)}, f32[4,2048]{1,0:T(4,128)S(1)}, u32[]{:S(2)}, u32[]{:S(2)}) collective-permute-start(f32[4,2048]{1,0:T(4,128)S(1)} %get-tuple-element.17), channel_id=1, source_target_pairs={{0,1},{1,0},{2,3},{3,2},{4,5},{5,4},{6,7},{7,6},{8,9},{9,8},{10,11... | collective-permute-start | bytes 98312 | tf_op jit(solution)/shard_map/ppermute | solution.py:87
  4.6 3.8 %collective-permute-start.3 = (f32[4,2048]{1,0:T(4,128)S(1)}, f32[4,2048]{1,0:T(4,128)S(1)}, u32[]{:S(2)}, u32[]{:S(2)}) collective-permute-start(f32[4,2048]{1,0:T(4,128)S(1)} %get-tuple-element.18), channel_id=1, source_target_pairs={{0,8},{1,2},{2,1},{3,4},{4,3},{5,6},{6,5},{7,15},{8,0},{9,10},{10,... | collective-permute-start | bytes 98312 | tf_op jit(solution)/shard_map/ppermute | solution.py:87
  8.6 1.4 %collective-permute-start.5 = (f32[1,4,8,512]{3,2,1,0:T(8,128)S(1)}, f32[1,4,8,512]{3,2,1,0:T(8,128)S(1)}, u32[]{:S(2)}, u32[]{:S(2)}) collective-permute-start(f32[1,4,8,512]{3,2,1,0:T(8,128)S(1)} %shade.9), channel_id=1, source_target_pairs={{0,8},{8,0},{16,24},{24,16},{1,9},{9,1},{17,25},{25,17},{2,10},{10... | collective-permute-start | bytes 196616 | tf_op jit(solution)/shard_map/ppermute | solution.py:295
  8.9 3.6 %collective-permute-start.4 = (f32[1,4,16,512]{3,2,1,0:T(8,128)S(1)}, f32[1,4,16,512]{3,2,1,0:T(8,128)S(1)}, u32[]{:S(2)}, u32[]{:S(2)}) collective-permute-start(f32[1,4,16,512]{3,2,1,0:T(8,128)S(1)} %shade.7), channel_id=1, source_target_pairs={{0,8},{8,0},{16,24},{24,16},{1,9},{9,1},{17,25},{25,17},{2,10},{10... | collective-permute-start | bytes 393224 | tf_op jit(solution)/shard_map/ppermute | solution.py:295
  9.6 1.6 %collective-permute-start.7 = (f32[1,4,8,512]{3,2,1,0:T(8,128)S(1)}, f32[1,4,8,512]{3,2,1,0:T(8,128)S(1)}, u32[]{:S(2)}, u32[]{:S(2)}) collective-permute-start(f32[1,4,8,512]{3,2,1,0:T(8,128)S(1)} %shade.11), channel_id=1, source_target_pairs={{0,8},{8,0},{16,24},{24,16},{1,9},{9,1},{17,25},{25,17},{2,10},{10... | collective-permute-start | bytes 196616 | tf_op jit(solution)/shard_map/ppermute | solution.py:295
  10.0 5.0 %collective-permute-start.6 = (f32[1,4,8,512]{3,2,1,0:T(8,128)S(1)}, f32[1,4,8,512]{3,2,1,0:T(8,128)S(1)}, u32[]{:S(2)}, u32[]{:S(2)}) collective-permute-start(f32[1,4,8,512]{3,2,1,0:T(8,128)S(1)} %first_merge.4), channel_id=1, source_target_pairs={{0,16},{8,24},{16,0},{24,8},{1,17},{9,25},{17,1},{25,9},{2,18},{10... | collective-permute-start | bytes 196616 | tf_op jit(solution)/shard_map/ppermute | solution.py:295
  11.2 4.8 %collective-permute-start.8 = (f32[1,4,8,512]{3,2,1,0:T(8,128)S(1)}, f32[1,4,8,512]{3,2,1,0:T(8,128)S(1)}, u32[]{:S(2)}, u32[]{:S(2)}) collective-permute-start(f32[1,4,8,512]{3,2,1,0:T(8,128)S(1)} %first_merge.5), channel_id=1, source_target_pairs={{0,16},{8,24},{16,0},{24,8},{1,17},{9,25},{17,1},{25,9},{2,18},{10... | collective-permute-start | bytes 196616 | tf_op jit(solution)/shard_map/ppermute | solution.py:295

commit v6 on v5

--- a/solution.py
+++ b/solution.py
@@ -44,16 +44,18 @@
     colors, opacities, done,
 ):
     slices, rows, _ = density.shape
-    moves = [(density_in.at[k], density.at[k]) for k in range(slices)]
-    moves += [(bins_in.at[k], bins.at[k]) for k in range(slices)]
-    moves += [(colors_in, colors), (opacities_in, opacities)]
+    moves = [
+        (density_in, density),
+        (bins_in, bins),
+        (colors_in, colors),
+        (opacities_in, opacities),
+    ]
     copies = [pltpu.make_async_copy(a, b, done.at[i]) for i, (a, b) in enumerate(moves)]
     for copy in copies:
         copy.start()
     depth_low = lax.axis_index("depth") & 1 == 0
     tile_low = lax.axis_index("tile") & 1 == 0
-    for copy in copies[:slices]:
-        copy.wait()
+    copies[0].wait()
     first, last = density[0], density[slices - 1]
     depth_even[...] = jnp.where(depth_low, last, first)
     depth_odd[...] = jnp.where(depth_low, first, last)
@@ -61,7 +63,7 @@
         top, bottom = density[k, 0:1], density[k, rows - 1 : rows]
         row_even[k : k + 1] = jnp.where(tile_low, bottom, top)
         row_odd[k : k + 1] = jnp.where(tile_low, top, bottom)
-    for copy in copies[slices:]:
+    for copy in copies[1:]:
         copy.wait()
     color = whole_number(colors[...], COLOR_ONE)
     opacity = whole_number(opacities[...].reshape(1, -1), OPACITY_ONE)
@@ -128,22 +130,27 @@
     return jnp.where(condition, 1.0, 0.0).astype(jnp.float32)
 
 
-def shade_kernel(stays, top, density, depth_even, depth_odd, row_even, row_odd, weighted, passed, image):
+EVEN, ODD = 0, 1
+
+
+def lower(band):
+    tile_is_low = 1 - (lax.axis_index("tile") & 1)
+    return tile_is_low if band == EVEN else 1 - tile_is_low
+
+
+def shade_kernel(stays, bands, density, depth_even, depth_odd, weighted, passed, *rest):
+    trades, image = rest[:-1], rest[-1]
     slices, rows, cols = density.shape
-    pieces, _, image_rows, piece = image.shape
-    me = lax.axis_index("depth")
-    mine = me & 1
+    pieces, _, _, piece = image.shape
+    me, tile = lax.axis_index("depth"), lax.axis_index("tile")
     bits = [(me >> i) & 1 if stays[i] else 1 - ((me >> i) & 1) for i in range(2)]
-    depth_is_low = mine == 0
-    tile = lax.axis_index("tile")
-    tile_is_low = tile & 1 == 0
+    depth_is_low = me & 1 == 0
     has_front, has_behind = flag(me > 0), flag(me < lax.axis_size("depth") - 1)
-    has_above, has_below = flag(tile > 0), flag(tile < lax.axis_size("tile") - 1)
+    inside = flag(jnp.logical_and(tile > 0, tile < lax.axis_size("tile") - 1))
     lane = lax.broadcasted_iota(jnp.int32, (SUBLANES, LANES), 1)
     sub = lax.broadcasted_iota(jnp.int32, (SUBLANES, LANES), 0)
     at_left, at_right = lane == 0, lane == LANES - 1
     at_top, at_bottom = sub == 0, sub == SUBLANES - 1
-    groups = rows // SUBLANES
 
     for i in range(pieces):
         number = 4 * i + 2 * bits[1] + bits[0]
@@ -151,37 +158,35 @@
             start = pl.multiple_of(number * piece + p, LANES)
             left = pl.multiple_of(jnp.maximum(start - LANES, 0), LANES)
             right = pl.multiple_of(jnp.minimum(start + LANES, cols - LANES), LANES)
-            has_left = flag(start > 0)
-            has_right = flag(start + LANES < cols)
+            has_left, has_right = flag(start > 0), flag(start + LANES < cols)
             here = pl.ds(start, LANES)
-            even_rows, odd_rows = row_even[:, here], row_odd[:, here]
-            above_rows = jnp.where(tile_is_low, odd_rows, even_rows) * has_above
-            below_rows = jnp.where(tile_is_low, even_rows, odd_rows) * has_below
-            for g in range(top // SUBLANES, (top + image_rows) // SUBLANES):
-                at = (slice(g * SUBLANES, (g + 1) * SUBLANES), here)
+            for n, (band, traded) in enumerate(zip(bands, trades)):
+                is_lower = lower(band)
+                band_rows = pl.ds(pl.multiple_of(is_lower * SUBLANES, SUBLANES), SUBLANES)
+                other_rows = pl.ds(pl.multiple_of((1 - is_lower) * SUBLANES, SUBLANES), SUBLANES)
+                is_lower = is_lower == 1
+                at = (band_rows, here)
                 even_face, odd_face = depth_even[at], depth_odd[at]
                 column = [jnp.where(depth_is_low, odd_face, even_face) * has_front]
                 column += [density[(k, *at)] for k in range(slices)]
                 column += [jnp.where(depth_is_low, even_face, odd_face) * has_behind]
+                outside = traded[:, here]
+                if band == ODD:
+                    outside = outside * inside
                 sums = [jnp.zeros((SUBLANES, LANES), jnp.float32) for _ in range(3)]
                 for k in range(slices):
                     v = column[k + 1]
-                    band = slice(g * SUBLANES, (g + 1) * SUBLANES)
-                    lv = density[k, band, pl.ds(left, LANES)] * has_left
-                    rv = density[k, band, pl.ds(right, LANES)] * has_right
+                    lv = density[k, band_rows, pl.ds(left, LANES)] * has_left
+                    rv = density[k, band_rows, pl.ds(right, LANES)] * has_right
                     plus = jnp.where(at_right, pltpu.roll(rv, LANES - 1, 1), pltpu.roll(v, LANES - 1, 1))
                     minus = jnp.where(at_left, pltpu.roll(lv, 1, 1), pltpu.roll(v, 1, 1))
                     by_col = plus - minus
-                    if g == 0:
-                        edge = jnp.broadcast_to(above_rows[k : k + 1], (SUBLANES, LANES))
-                    else:
-                        edge = pltpu.roll(density[k, (g - 1) * SUBLANES : g * SUBLANES, here], 1, 0)
-                    up = jnp.where(at_top, edge, pltpu.roll(v, 1, 0))
-                    if g == groups - 1:
-                        edge = jnp.broadcast_to(below_rows[k : k + 1], (SUBLANES, LANES))
-                    else:
-                        edge = pltpu.roll(density[k, (g + 1) * SUBLANES : (g + 2) * SUBLANES, here], SUBLANES - 1, 0)
-                    down = jnp.where(at_bottom, edge, pltpu.roll(v, SUBLANES - 1, 0))
+                    far = jnp.broadcast_to(outside[k : k + 1], (SUBLANES, LANES))
+                    other = density[k, other_rows, here]
+                    above = jnp.where(is_lower, pltpu.roll(other, 1, 0), far)
+                    below = jnp.where(is_lower, far, pltpu.roll(other, SUBLANES - 1, 0))
+                    up = jnp.where(at_top, above, pltpu.roll(v, 1, 0))
+                    down = jnp.where(at_bottom, below, pltpu.roll(v, SUBLANES - 1, 0))
                     by_row = down - up
                     by_depth = column[k + 2] - column[k]
                     square = by_depth * by_depth + by_row * by_row + by_col * by_col
@@ -189,8 +194,7 @@
                     shade = 0.3 + facing * lax.rsqrt(jnp.maximum(square, 4.0))
                     for channel in range(3):
                         sums[channel] = sums[channel] + weighted[(channel, k, *at)] * shade
-                r = g * SUBLANES - top
-                out = (slice(r, r + SUBLANES), slice(p, p + LANES))
+                out = (slice(n * SUBLANES, (n + 1) * SUBLANES), slice(p, p + LANES))
                 for channel in range(3):
                     image[(i, channel, *out)] = sums[channel]
                 image[(i, 3, *out)] = passed[at]
@@ -233,7 +237,8 @@
     for band in range(bands):
         rows = slice(band * height, (band + 1) * height)
         light, through = merged(behind, kept[0, :, rows], received[band][0])
-        out[0:3, rows], out[3, rows] = light, 1.0 - through
+        place = pl.ds(pl.multiple_of(lower(band) * SUBLANES, SUBLANES), SUBLANES)
+        out[0:3, place], out[3, place] = light, 1.0 - through
 
 
 def call(kernel, name, out_shape, *args):
@@ -270,7 +275,7 @@
         scratch_shapes=[
             pltpu.VMEM(colors.shape, colors.dtype),
             pltpu.VMEM(opacities.shape, opacities.dtype),
-            pltpu.SemaphoreType.DMA((2 * slices + 2,)),
+            pltpu.SemaphoreType.DMA((4,)),
         ],
         compiler_params=params(),
         name="load",
@@ -294,33 +299,41 @@
     def swap(x, level):
         return lax.ppermute(x, "depth", [(i, i ^ 1 << level) for i in range(slab_count)])
 
-    def shaded(stays, top, height):
+    *faces, row_even, row_odd = traded
+    rows_of = {EVEN: row_even, ODD: row_odd}
+
+    def shaded(stays, bands):
         return pl.pallas_call(
-            functools.partial(shade_kernel, stays, top),
-            out_shape=f32(half // 2, 4, height, piece),
-            in_specs=[vmem()] * 7,
+            functools.partial(shade_kernel, stays, bands),
+            out_shape=f32(half // 2, 4, SUBLANES * len(bands), piece),
+            in_specs=[vmem()] * (5 + len(bands)),
             out_specs=vmem(),
             compiler_params=params(),
             cost_estimate=cost(5 * slices * pixels, 2 * slices * pixels),
             name="shade",
-        )(density, *traded, weighted, passed)
-
-    def first_merge(stays, top, height):
-        received = swap(shaded((False, stays), top, height), 0)
-        kept = shaded((True, stays), top, height)
-        return call(first_merge_kernel, "first_merge", f32(half // 2, 4, height, piece), kept, received)
+        )(density, *faces, weighted, passed, *(rows_of[band] for band in bands))
 
     levels = slab_count.bit_length() - 1
-    bands = rows // SUBLANES
-    received = [swap(first_merge(False, band * SUBLANES, SUBLANES), 1) for band in range(bands)]
-    kept = first_merge(True, 0, rows)
+    bands = (EVEN, ODD)
+    sent_far = []
+    for band in bands:
+        sent = shaded((False, False), (band,))
+        received = swap(sent, 0)
+        kept = shaded((True, False), (band,))
+        _, kept, weighted = lax.optimization_barrier((sent, kept, weighted))
+        if sent_far:
+            _, kept = lax.optimization_barrier((sent_far[-1], kept))
+        sent_far.append(call(first_merge_kernel, "first_merge", f32(*kept.shape), kept, received))
+    received = [swap(x, 1) for x in sent_far]
+    sent, kept = shaded((False, True), bands), shaded((True, True), bands)
+    kept = call(first_merge_kernel, "first_merge", f32(*kept.shape), kept, swap(sent, 0))
     for level in range(1, levels - 1):
         left = kept.shape[0] // 2
-        shapes = [f32(left, 4, rows, piece)] + [f32(left, 4, SUBLANES, piece)] * bands
-        kernel = functools.partial(merge_kernel, level, bands)
+        shapes = [f32(left, 4, rows, piece)] + [f32(left, 4, SUBLANES, piece)] * len(bands)
+        kernel = functools.partial(merge_kernel, level, len(bands))
         kept, *sent = call(kernel, "merge", shapes, kept, *received)
         received = [swap(x, level + 1) for x in sent]
-    kernel = functools.partial(last_merge_kernel, levels - 1, bands)
+    kernel = functools.partial(last_merge_kernel, levels - 1, len(bands))
     return call(kernel, "last_merge", f32(4, rows, piece), kept, *received)
 
 

time: 17 us -> 17 us (level)
  waiting for transfers between devices: 4.39 us -> 4.73 us
    ppermute x5, waiting for transfers between devices: 3.5 us -> 3.84 us  [swap(): lax.ppermute(x, 'depth', [(i, i ^ 1 << level) for i in range(slab_count)])]
  transfers between devices with their start and end apart: 9 -> 9, of which waited for: 3 -> 4; matrix products, arithmetic and copies ran while one was open for 0% -> 0% of each run, Pallas kernels for 12% -> 13%
where the time goes in v6:
time: 17 us; the launch traced here: 16.8 us
  starting transfers between devices  7.24 us (43%)
  waiting for transfers between devices  4.73 us (28%)
  Pallas kernels  4.13 us (24%)
  between operations  0.73 us (4%)
    ppermute x4, starting transfers between devices, trade(): return lax.ppermute(x, ('depth', 'tile'), pairs)  4.44 us
    ppermute x5, waiting for transfers between devices, swap(): lax.ppermute(x, 'depth', [(i, i ^ 1 << level) for i in range(slab_count)])  3.84 us
    ppermute x5, starting transfers between devices, swap(): lax.ppermute(x, 'depth', [(i, i ^ 1 << level) for i in range(slab_count)])  2.8 us
    pallas_call x1, Pallas kernels, on_device(): pl.pallas_call(load_kernel, out_shape=[f32(*density.shape), jax.ShapeDtyp...  1.25 us
    pallas_call x6, Pallas kernels, shaded(): pl.pallas_call(functools.partial(shade_kernel, stays, bands), out_shape=f...  1.11 us
    pallas_call x1, Pallas kernels, on_device(): pl.pallas_call(weights_kernel, out_shape=[f32(3, slices, rows, cols), f32...  1.02 us
    ppermute x4, waiting for transfers between devices, trade(): return lax.ppermute(x, ('depth', 'tile'), pairs)  0.89 us
    pallas_call x4, Pallas kernels, call(): pl.pallas_call(kernel, out_shape=out_shape, in_specs=[vmem()] * len(args)...  0.74 us
  transfers between devices with their start and end apart: 9, of which 4 were waited for; matrix products, arithmetic and copies ran while one was open for 0% of the time, Pallas kernels for 13%

profile of v6, /device:TPU:0, one launch (start us, length us, event | category | flops | bytes accessed | tf_op | source)
XLA Modules:
  0.0 16.8 jit_solution(1342987309816912550)
XLA Ops:
  0.0 1.3 %load.1 = (f32[4,16,2048]{2,1,0:T(8,128)S(1)}, s32[4,16,2048]{2,1,0:T(8,128)S(1)}, f32[16,2048]{1,0:T(8,128)S(1)}, f32[16,2048]{1,0:T(8,128)S(1)}, f32[4,2048]{1...) custom-call(f32[4,16,2048]{2,1,0:T(8,128)} %density_in.1, s32[4,16,2048]{2,1,0:T(8,128)} %bins_in.1, ...), custom_call_target="tpu_custom_call" | custom-call | tf_op jit(solution)/shard_map/load/pallas_call | solution.py:262
  1.3 0.5 %collective-permute-start = (f32[16,2048]{1,0:T(8,128)S(1)}, f32[16,2048]{1,0:T(8,128)S(1)}, u32[]{:S(2)}, u32[]{:S(2)}) collective-permute-start(f32[16,2048]{1,0:T(8,128)S(1)} %get-tuple-element.20), channel_id=1, source_target_pairs={{0,8},{1,9},{2,10},{3,11},{4,12},{5,13},{6,14},{7,15},{8,0},{9,1},... | collective-permute-start | bytes 393224 | tf_op jit(solution)/shard_map/ppermute | solution.py:89
  1.8 2.6 %collective-permute-start.1 = (f32[16,2048]{1,0:T(8,128)S(1)}, f32[16,2048]{1,0:T(8,128)S(1)}, u32[]{:S(2)}, u32[]{:S(2)}) collective-permute-start(f32[16,2048]{1,0:T(8,128)S(1)} %get-tuple-element.21), channel_id=1, source_target_pairs={{0,1},{1,0},{2,3},{3,2},{4,5},{5,4},{6,7},{7,6},{8,16},{9,17},{10,... | collective-permute-start | bytes 393224 | tf_op jit(solution)/shard_map/ppermute | solution.py:89
  4.3 0.1 collective-permute-start.2
  4.4 1.3 %collective-permute-start.3 = (f32[4,2048]{1,0:T(4,128)S(1)}, f32[4,2048]{1,0:T(4,128)S(1)}, u32[]{:S(2)}, u32[]{:S(2)}) collective-permute-start(f32[4,2048]{1,0:T(4,128)S(1)} %get-tuple-element.28), channel_id=1, source_target_pairs={{0,8},{1,2},{2,1},{3,4},{4,3},{5,6},{6,5},{7,15},{8,0},{9,10},{10,... | collective-permute-start | bytes 98312 | tf_op jit(solution)/shard_map/ppermute | solution.py:89
  6.3 1.0 %weights.1 = (f32[3,4,16,2048]{3,2,1,0:T(8,128)S(1)}, f32[16,2048]{1,0:T(8,128)S(1)}) custom-call(s32[1,1]{1,0:T(1,128)S(6)} %copy.6.count, s32[4,16,2048]{2,1,0:T(8,128)S(1)} %get-tuple-element.22.bins, s32[2,2,8,128]{3,2,1,0:T(8,128)S(1)} %get-tuple-element.23.tables), custom_call_target="tpu_custom_call" | custom-call | flops 8388608 | bytes 2097152 | tf_op jit(solution)/shard_map/weights/pallas_call | solution.py:289
  7.4 0.9 %collective-permute-done.2.rest_0_ = f32[4,2048]{1,0:T(4,128)S(1)} collective-permute-done((f32[4,2048]{1,0:T(4,128)S(1)}, f32[4,2048]{1,0:T(4,128)S(1)}, u32[]{:S(2)}, u32[]{:S(2)}) %collective-permute-start.2) | collective-permute-done | bytes 32800 | tf_op jit(solution)/shard_map/ppermute | solution.py:89
  8.3 0.0 collective-permute-done.depth_even
  8.3 0.0 collective-permute-done.1.depth_odd
  8.3 0.2 shade.6
  8.4 0.1 collective-permute-start.5
  8.5 0.2 %shade.7.kept = f32[1,4,8,512]{3,2,1,0:T(8,128)S(1)} custom-call(f32[4,16,2048]{2,1,0:T(8,128)S(1)} %get-tuple-element.19.density, f32[16,2048]{1,0:T(8,128)S(1)} %collective-permute-done.depth_even, f32[16,2048]{1,0:T(8,128)S(1)} %collective-permute-done.1.depth_odd, f32[3,4,16,2048]{3,2,1,0:T(8,128)S(1)} %get-tuple-element.29.weighted, ...), custom_call_target="tpu_custom_call" | custom-call | flops 655360 | bytes 262144 | tf_op jit(solution)/shard_map/shade/pallas_call | solution.py:306
  8.7 0.2 %shade.8 = f32[1,4,8,512]{3,2,1,0:T(8,128)S(1)} custom-call(f32[4,16,2048]{2,1,0:T(8,128)S(1)} %get-tuple-element.19.density, f32[16,2048]{1,0:T(8,128)S(1)} %collective-permute-done.depth_even, f32[16,2048]{1,0:T(8,128)S(1)} %collective-permute-done.1.depth_odd, f32[3,4,16,2048]{3,2,1,0:T(8,128)S(1)} %get-tuple-element.29.weighted, ...), custom_call_target="tpu_custom_call" | custom-call | flops 655360 | bytes 262144 | tf_op jit(solution)/shard_map/shade/pallas_call | solution.py:306
  8.9 0.5 %collective-permute-start.7 = (f32[1,4,8,512]{3,2,1,0:T(8,128)S(1)}, f32[1,4,8,512]{3,2,1,0:T(8,128)S(1)}, u32[]{:S(2)}, u32[]{:S(2)}) collective-permute-start(f32[1,4,8,512]{3,2,1,0:T(8,128)S(1)} %shade.8), channel_id=1, source_target_pairs={{0,8},{8,0},{16,24},{24,16},{1,9},{9,1},{17,25},{25,17},{2,10},{10... | collective-permute-start | bytes 196616 | tf_op jit(solution)/shard_map/ppermute | solution.py:300
  9.4 0.2 shade.9.kept
  9.6 0.2 %shade.11 = f32[1,4,16,512]{3,2,1,0:T(8,128)S(1)} custom-call(f32[4,16,2048]{2,1,0:T(8,128)S(1)} %get-tuple-element.19.density, f32[16,2048]{1,0:T(8,128)S(1)} %collective-permute-done.depth_even, f32[16,2048]{1,0:T(8,128)S(1)} %collective-permute-done.1.depth_odd, f32[3,4,16,2048]{3,2,1,0:T(8,128)S(1)} %get-tuple-element.29.weighted, ...), custom_call_target="tpu_custom_call" | custom-call | flops 655360 | bytes 262144 | tf_op jit(solution)/shard_map/shade/pallas_call | solution.py:306
  9.8 0.1 collective-permute-start.4
  9.9 0.4 %collective-permute-done.7.received = f32[1,4,8,512]{3,2,1,0:T(8,128)S(1)} collective-permute-done((f32[1,4,8,512]{3,2,1,0:T(8,128)S(1)}, f32[1,4,8,512]{3,2,1,0:T(8,128)S(1)}, u32[]{:S(2)}, u32[]{:S(2)}) %collective-permute-start.7) | collective-permute-done | bytes 65568 | tf_op jit(solution)/shard_map/ppermute | solution.py:300
  10.3 1.0 %collective-permute-start.8 = (f32[1,4,8,512]{3,2,1,0:T(8,128)S(1)}, f32[1,4,8,512]{3,2,1,0:T(8,128)S(1)}, u32[]{:S(2)}, u32[]{:S(2)}) collective-permute-start(f32[1,4,8,512]{3,2,1,0:T(8,128)S(1)} %first_merge.5), channel_id=1, source_target_pairs={{0,16},{8,24},{16,0},{24,8},{1,17},{9,25},{17,1},{25,9},{2,18},{10... | collective-permute-start | bytes 196616 | tf_op jit(solution)/shard_map/ppermute | solution.py:300
  11.3 1.1 %collective-permute-start.6 = (f32[1,4,8,512]{3,2,1,0:T(8,128)S(1)}, f32[1,4,8,512]{3,2,1,0:T(8,128)S(1)}, u32[]{:S(2)}, u32[]{:S(2)}) collective-permute-start(f32[1,4,8,512]{3,2,1,0:T(8,128)S(1)} %first_merge.4), channel_id=1, source_target_pairs={{0,16},{8,24},{16,0},{24,8},{1,17},{9,25},{17,1},{25,9},{2,18},{10... | collective-permute-start | bytes 196616 | tf_op jit(solution)/shard_map/ppermute | solution.py:300
  12.4 0.2 %shade.10.kept = f32[1,4,16,512]{3,2,1,0:T(8,128)S(1)} custom-call(f32[4,16,2048]{2,1,0:T(8,128)S(1)} %get-tuple-element.19.density, f32[16,2048]{1,0:T(8,128)S(1)} %collective-permute-done.depth_even, f32[16,2048]{1,0:T(8,128)S(1)} %collective-permute-done.1.depth_odd, f32[3,4,16,2048]{3,2,1,0:T(8,128)S(1)} %get-tuple-element.29.weighted, ...), custom_call_target="tpu_custom_call" | custom-call | flops 655360 | bytes 262144 | tf_op jit(solution)/shard_map/shade/pallas_call | solution.py:306
  12.7 2.6 %collective-permute-done.8.rest_1_ = f32[1,4,8,512]{3,2,1,0:T(8,128)S(1)} collective-permute-done((f32[1,4,8,512]{3,2,1,0:T(8,128)S(1)}, f32[1,4,8,512]{3,2,1,0:T(8,128)S(1)}, u32[]{:S(2)}, u32[]{:S(2)}) %collective-permute-start.8) | collective-permute-done | bytes 65568 | tf_op jit(solution)/shard_map/ppermute | solution.py:300
  15.3 0.8 %collective-permute-done.6.rest_0_ = f32[1,4,8,512]{3,2,1,0:T(8,128)S(1)} collective-permute-done((f32[1,4,8,512]{3,2,1,0:T(8,128)S(1)}, f32[1,4,8,512]{3,2,1,0:T(8,128)S(1)}, u32[]{:S(2)}, u32[]{:S(2)}) %collective-permute-start.6) | collective-permute-done | bytes 65568 | tf_op jit(solution)/shard_map/ppermute | solution.py:300
  16.1 0.7 %last_merge.1 = f32[4,16,512]{2,1,0:T(8,128)} custom-call(f32[1,4,16,512]{3,2,1,0:T(8,128)S(1)} %first_merge.3.kept, f32[1,4,8,512]{3,2,1,0:T(8,128)S(1)} %collective-permute-done.6.rest_0_, f32[1,4,8,512]{3,2,1,0:T(8,128)S(1)} %collective-permute-done.8.rest_1_), custom_call_target="tpu_custom_call" | custom-call | tf_op jit(solution)/shard_map/last_merge/pallas_call | solution.py:245
  (6 shorter events, 0.1 us)
Async XLA Ops:
  1.3 7.0 %collective-permute-start = (f32[16,2048]{1,0:T(8,128)S(1)}, f32[16,2048]{1,0:T(8,128)S(1)}, u32[]{:S(2)}, u32[]{:S(2)}) collective-permute-start(f32[16,2048]{1,0:T(8,128)S(1)} %get-tuple-element.20), channel_id=1, source_target_pairs={{0,8},{1,9},{2,10},{3,11},{4,12},{5,13},{6,14},{7,15},{8,0},{9,1},... | collective-permute-start | bytes 393224 | tf_op jit(solution)/shard_map/ppermute | solution.py:89
  1.8 6.5 %collective-permute-start.1 = (f32[16,2048]{1,0:T(8,128)S(1)}, f32[16,2048]{1,0:T(8,128)S(1)}, u32[]{:S(2)}, u32[]{:S(2)}) collective-permute-start(f32[16,2048]{1,0:T(8,128)S(1)} %get-tuple-element.21), channel_id=1, source_target_pairs={{0,1},{1,0},{2,3},{3,2},{4,5},{5,4},{6,7},{7,6},{8,16},{9,17},{10,... | collective-permute-start | bytes 393224 | tf_op jit(solution)/shard_map/ppermute | solution.py:89
  4.3 3.9 %collective-permute-start.2 = (f32[4,2048]{1,0:T(4,128)S(1)}, f32[4,2048]{1,0:T(4,128)S(1)}, u32[]{:S(2)}, u32[]{:S(2)}) collective-permute-start(f32[4,2048]{1,0:T(4,128)S(1)} %get-tuple-element.26), channel_id=1, source_target_pairs={{0,1},{1,0},{2,3},{3,2},{4,5},{5,4},{6,7},{7,6},{8,9},{9,8},{10,11... | collective-permute-start | bytes 98312 | tf_op jit(solution)/shard_map/ppermute | solution.py:89
  4.4 4.3 %collective-permute-start.3 = (f32[4,2048]{1,0:T(4,128)S(1)}, f32[4,2048]{1,0:T(4,128)S(1)}, u32[]{:S(2)}, u32[]{:S(2)}) collective-permute-start(f32[4,2048]{1,0:T(4,128)S(1)} %get-tuple-element.28), channel_id=1, source_target_pairs={{0,8},{1,2},{2,1},{3,4},{4,3},{5,6},{6,5},{7,15},{8,0},{9,10},{10,... | collective-permute-start | bytes 98312 | tf_op jit(solution)/shard_map/ppermute | solution.py:89
  8.4 1.5 %collective-permute-start.5 = (f32[1,4,8,512]{3,2,1,0:T(8,128)S(1)}, f32[1,4,8,512]{3,2,1,0:T(8,128)S(1)}, u32[]{:S(2)}, u32[]{:S(2)}) collective-permute-start(f32[1,4,8,512]{3,2,1,0:T(8,128)S(1)} %shade.6), channel_id=1, source_target_pairs={{0,8},{8,0},{16,24},{24,16},{1,9},{9,1},{17,25},{25,17},{2,10},{10... | collective-permute-start | bytes 196616 | tf_op jit(solution)/shard_map/ppermute | solution.py:300
  8.9 1.4 %collective-permute-start.7 = (f32[1,4,8,512]{3,2,1,0:T(8,128)S(1)}, f32[1,4,8,512]{3,2,1,0:T(8,128)S(1)}, u32[]{:S(2)}, u32[]{:S(2)}) collective-permute-start(f32[1,4,8,512]{3,2,1,0:T(8,128)S(1)} %shade.8), channel_id=1, source_target_pairs={{0,8},{8,0},{16,24},{24,16},{1,9},{9,1},{17,25},{25,17},{2,10},{10... | collective-permute-start | bytes 196616 | tf_op jit(solution)/shard_map/ppermute | solution.py:300
  9.8 2.8 %collective-permute-start.4 = (f32[1,4,16,512]{3,2,1,0:T(8,128)S(1)}, f32[1,4,16,512]{3,2,1,0:T(8,128)S(1)}, u32[]{:S(2)}, u32[]{:S(2)}) collective-permute-start(f32[1,4,16,512]{3,2,1,0:T(8,128)S(1)} %shade.11), channel_id=1, source_target_pairs={{0,8},{8,0},{16,24},{24,16},{1,9},{9,1},{17,25},{25,17},{2,10},{10... | collective-permute-start | bytes 393224 | tf_op jit(solution)/shard_map/ppermute | solution.py:300
  10.3 5.0 %collective-permute-start.8 = (f32[1,4,8,512]{3,2,1,0:T(8,128)S(1)}, f32[1,4,8,512]{3,2,1,0:T(8,128)S(1)}, u32[]{:S(2)}, u32[]{:S(2)}) collective-permute-start(f32[1,4,8,512]{3,2,1,0:T(8,128)S(1)} %first_merge.5), channel_id=1, source_target_pairs={{0,16},{8,24},{16,0},{24,8},{1,17},{9,25},{17,1},{25,9},{2,18},{10... | collective-permute-start | bytes 196616 | tf_op jit(solution)/shard_map/ppermute | solution.py:300
  11.3 4.8 %collective-permute-start.6 = (f32[1,4,8,512]{3,2,1,0:T(8,128)S(1)}, f32[1,4,8,512]{3,2,1,0:T(8,128)S(1)}, u32[]{:S(2)}, u32[]{:S(2)}) collective-permute-start(f32[1,4,8,512]{3,2,1,0:T(8,128)S(1)} %first_merge.4), channel_id=1, source_target_pairs={{0,16},{8,24},{16,0},{24,8},{1,17},{9,25},{17,1},{25,9},{2,18},{10... | collective-permute-start | bytes 196616 | tf_op jit(solution)/shard_map/ppermute | solution.py:300

commit v7 on v6

--- a/solution.py
+++ b/solution.py
@@ -325,7 +325,9 @@
             _, kept = lax.optimization_barrier((sent_far[-1], kept))
         sent_far.append(call(first_merge_kernel, "first_merge", f32(*kept.shape), kept, received))
     received = [swap(x, 1) for x in sent_far]
-    sent, kept = shaded((False, True), bands), shaded((True, True), bands)
+    sent = shaded((False, True), bands)
+    received[0], weighted = lax.optimization_barrier((received[0], weighted))
+    kept = shaded((True, True), bands)
     kept = call(first_merge_kernel, "first_merge", f32(*kept.shape), kept, swap(sent, 0))
     for level in range(1, levels - 1):
         left = kept.shape[0] // 2

time: 17 us -> 16.7 us (0.982)
  waiting for transfers between devices: 4.73 us -> 4.38 us
    ppermute x5, waiting for transfers between devices: 3.84 us -> 3.49 us  [swap(): lax.ppermute(x, 'depth', [(i, i ^ 1 << level) for i in range(slab_count)])]
  transfers between devices with their start and end apart: 9 -> 9, of which waited for: 4 -> 3; matrix products, arithmetic and copies ran while one was open for 0% -> 0% of each run, Pallas kernels for 13% -> 13%
where the time goes in v7:
time: 16.7 us; the launch traced here: 16.6 us
  starting transfers between devices  7.3 us (44%)
  waiting for transfers between devices  4.38 us (26%)
  Pallas kernels  4.13 us (25%)
  between operations  0.74 us (4%)
    ppermute x4, starting transfers between devices, trade(): return lax.ppermute(x, ('depth', 'tile'), pairs)  4.44 us
    ppermute x5, waiting for transfers between devices, swap(): lax.ppermute(x, 'depth', [(i, i ^ 1 << level) for i in range(slab_count)])  3.49 us
    ppermute x5, starting transfers between devices, swap(): lax.ppermute(x, 'depth', [(i, i ^ 1 << level) for i in range(slab_count)])  2.87 us
    pallas_call x1, Pallas kernels, on_device(): pl.pallas_call(load_kernel, out_shape=[f32(*density.shape), jax.ShapeDtyp...  1.25 us
    pallas_call x6, Pallas kernels, shaded(): pl.pallas_call(functools.partial(shade_kernel, stays, bands), out_shape=f...  1.11 us
    pallas_call x1, Pallas kernels, on_device(): pl.pallas_call(weights_kernel, out_shape=[f32(3, slices, rows, cols), f32...  1.02 us
    ppermute x4, waiting for transfers between devices, trade(): return lax.ppermute(x, ('depth', 'tile'), pairs)  0.89 us
    pallas_call x4, Pallas kernels, call(): pl.pallas_call(kernel, out_shape=out_shape, in_specs=[vmem()] * len(args)...  0.74 us
  transfers between devices with their start and end apart: 9, of which 3 were waited for; matrix products, arithmetic and copies ran while one was open for 0% of the time, Pallas kernels for 13%

profile of v7, /device:TPU:0, one launch (start us, length us, event | category | flops | bytes accessed | tf_op | source)
XLA Modules:
  0.0 16.6 jit_solution(15136693961200154401)
XLA Ops:
  0.0 1.3 %load.1 = (f32[4,16,2048]{2,1,0:T(8,128)S(1)}, s32[4,16,2048]{2,1,0:T(8,128)S(1)}, f32[16,2048]{1,0:T(8,128)S(1)}, f32[16,2048]{1,0:T(8,128)S(1)}, f32[4,2048]{1...) custom-call(f32[4,16,2048]{2,1,0:T(8,128)} %density_in.1, s32[4,16,2048]{2,1,0:T(8,128)} %bins_in.1, ...), custom_call_target="tpu_custom_call" | custom-call | tf_op jit(solution)/shard_map/load/pallas_call | solution.py:262
  1.3 0.5 %collective-permute-start = (f32[16,2048]{1,0:T(8,128)S(1)}, f32[16,2048]{1,0:T(8,128)S(1)}, u32[]{:S(2)}, u32[]{:S(2)}) collective-permute-start(f32[16,2048]{1,0:T(8,128)S(1)} %get-tuple-element.22), channel_id=1, source_target_pairs={{0,8},{1,9},{2,10},{3,11},{4,12},{5,13},{6,14},{7,15},{8,0},{9,1},... | collective-permute-start | bytes 393224 | tf_op jit(solution)/shard_map/ppermute | solution.py:89
  1.8 2.6 %collective-permute-start.1 = (f32[16,2048]{1,0:T(8,128)S(1)}, f32[16,2048]{1,0:T(8,128)S(1)}, u32[]{:S(2)}, u32[]{:S(2)}) collective-permute-start(f32[16,2048]{1,0:T(8,128)S(1)} %get-tuple-element.23), channel_id=1, source_target_pairs={{0,1},{1,0},{2,3},{3,2},{4,5},{5,4},{6,7},{7,6},{8,16},{9,17},{10,... | collective-permute-start | bytes 393224 | tf_op jit(solution)/shard_map/ppermute | solution.py:89
  4.3 0.1 collective-permute-start.2
  4.4 1.3 %collective-permute-start.5 = (f32[4,2048]{1,0:T(4,128)S(1)}, f32[4,2048]{1,0:T(4,128)S(1)}, u32[]{:S(2)}, u32[]{:S(2)}) collective-permute-start(f32[4,2048]{1,0:T(4,128)S(1)} %get-tuple-element.31), channel_id=1, source_target_pairs={{0,8},{1,2},{2,1},{3,4},{4,3},{5,6},{6,5},{7,15},{8,0},{9,10},{10,... | collective-permute-start | bytes 98312 | tf_op jit(solution)/shard_map/ppermute | solution.py:89
  6.3 1.0 %weights.1 = (f32[3,4,16,2048]{3,2,1,0:T(8,128)S(1)}, f32[16,2048]{1,0:T(8,128)S(1)}) custom-call(s32[1,1]{1,0:T(1,128)S(6)} %copy.6.count, s32[4,16,2048]{2,1,0:T(8,128)S(1)} %get-tuple-element.24.bins, s32[2,2,8,128]{3,2,1,0:T(8,128)S(1)} %get-tuple-element.25.tables), custom_call_target="tpu_custom_call" | custom-call | flops 8388608 | bytes 2097152 | tf_op jit(solution)/shard_map/weights/pallas_call | solution.py:289
  7.4 0.9 %collective-permute-done.2.rest_0_ = f32[4,2048]{1,0:T(4,128)S(1)} collective-permute-done((f32[4,2048]{1,0:T(4,128)S(1)}, f32[4,2048]{1,0:T(4,128)S(1)}, u32[]{:S(2)}, u32[]{:S(2)}) %collective-permute-start.2) | collective-permute-done | bytes 32800 | tf_op jit(solution)/shard_map/ppermute | solution.py:89
  8.3 0.0 collective-permute-done.depth_even
  8.3 0.0 collective-permute-done.1.depth_odd
  8.3 0.2 shade.6
  8.4 0.1 collective-permute-start.3
  8.5 0.2 %shade.7.kept = f32[1,4,8,512]{3,2,1,0:T(8,128)S(1)} custom-call(f32[4,16,2048]{2,1,0:T(8,128)S(1)} %get-tuple-element.21.density, f32[16,2048]{1,0:T(8,128)S(1)} %collective-permute-done.depth_even, f32[16,2048]{1,0:T(8,128)S(1)} %collective-permute-done.1.depth_odd, f32[3,4,16,2048]{3,2,1,0:T(8,128)S(1)} %get-tuple-element.33.weighted, ...), custom_call_target="tpu_custom_call" | custom-call | flops 655360 | bytes 262144 | tf_op jit(solution)/shard_map/shade/pallas_call | solution.py:306
  8.7 0.2 %shade.8 = f32[1,4,8,512]{3,2,1,0:T(8,128)S(1)} custom-call(f32[4,16,2048]{2,1,0:T(8,128)S(1)} %get-tuple-element.21.density, f32[16,2048]{1,0:T(8,128)S(1)} %collective-permute-done.depth_even, f32[16,2048]{1,0:T(8,128)S(1)} %collective-permute-done.1.depth_odd, f32[3,4,16,2048]{3,2,1,0:T(8,128)S(1)} %get-tuple-element.33.weighted, ...), custom_call_target="tpu_custom_call" | custom-call | flops 655360 | bytes 262144 | tf_op jit(solution)/shard_map/shade/pallas_call | solution.py:306
  8.9 0.5 %collective-permute-start.7 = (f32[1,4,8,512]{3,2,1,0:T(8,128)S(1)}, f32[1,4,8,512]{3,2,1,0:T(8,128)S(1)}, u32[]{:S(2)}, u32[]{:S(2)}) collective-permute-start(f32[1,4,8,512]{3,2,1,0:T(8,128)S(1)} %shade.8), channel_id=1, source_target_pairs={{0,8},{8,0},{16,24},{24,16},{1,9},{9,1},{17,25},{25,17},{2,10},{10... | collective-permute-start | bytes 196616 | tf_op jit(solution)/shard_map/ppermute | solution.py:300
  9.4 0.2 shade.9.kept
  9.6 0.2 %shade.11 = f32[1,4,16,512]{3,2,1,0:T(8,128)S(1)} custom-call(f32[4,16,2048]{2,1,0:T(8,128)S(1)} %get-tuple-element.21.density, f32[16,2048]{1,0:T(8,128)S(1)} %collective-permute-done.depth_even, f32[16,2048]{1,0:T(8,128)S(1)} %collective-permute-done.1.depth_odd, f32[3,4,16,2048]{3,2,1,0:T(8,128)S(1)} %get-tuple-element.33.weighted, ...), custom_call_target="tpu_custom_call" | custom-call | flops 655360 | bytes 262144 | tf_op jit(solution)/shard_map/shade/pallas_call | solution.py:306
  9.8 0.1 collective-permute-start.6
  9.9 1.1 %collective-permute-start.4 = (f32[1,4,8,512]{3,2,1,0:T(8,128)S(1)}, f32[1,4,8,512]{3,2,1,0:T(8,128)S(1)}, u32[]{:S(2)}, u32[]{:S(2)}) collective-permute-start(f32[1,4,8,512]{3,2,1,0:T(8,128)S(1)} %first_merge.3), channel_id=1, source_target_pairs={{0,16},{8,24},{16,0},{24,8},{1,17},{9,25},{17,1},{25,9},{2,18},{10... | collective-permute-start | bytes 196616 | tf_op jit(solution)/shard_map/ppermute | solution.py:300
  11.1 1.1 %collective-permute-start.8 = (f32[1,4,8,512]{3,2,1,0:T(8,128)S(1)}, f32[1,4,8,512]{3,2,1,0:T(8,128)S(1)}, u32[]{:S(2)}, u32[]{:S(2)}) collective-permute-start(f32[1,4,8,512]{3,2,1,0:T(8,128)S(1)} %first_merge.5), channel_id=1, source_target_pairs={{0,16},{8,24},{16,0},{24,8},{1,17},{9,25},{17,1},{25,9},{2,18},{10... | collective-permute-start | bytes 196616 | tf_op jit(solution)/shard_map/ppermute | solution.py:300
  12.1 2.8 %collective-permute-done.4.rest_0_ = f32[1,4,8,512]{3,2,1,0:T(8,128)S(1)} collective-permute-done((f32[1,4,8,512]{3,2,1,0:T(8,128)S(1)}, f32[1,4,8,512]{3,2,1,0:T(8,128)S(1)}, u32[]{:S(2)}, u32[]{:S(2)}) %collective-permute-start.4) | collective-permute-done | bytes 65568 | tf_op jit(solution)/shard_map/ppermute | solution.py:300
  14.9 0.2 %shade.10.kept = f32[1,4,16,512]{3,2,1,0:T(8,128)S(1)} custom-call(f32[4,16,2048]{2,1,0:T(8,128)S(1)} %get-tuple-element.21.density, f32[16,2048]{1,0:T(8,128)S(1)} %collective-permute-done.depth_even, f32[16,2048]{1,0:T(8,128)S(1)} %collective-permute-done.1.depth_odd, f32[3,4,16,2048]{3,2,1,0:T(8,128)S(1)} %get-tuple-element.33.weighted, ...), custom_call_target="tpu_custom_call" | custom-call | flops 655360 | bytes 262144 | tf_op jit(solution)/shard_map/shade/pallas_call | solution.py:306
  15.1 0.0 collective-permute-done.6.received
  15.2 0.7 %collective-permute-done.8.rest_1_ = f32[1,4,8,512]{3,2,1,0:T(8,128)S(1)} collective-permute-done((f32[1,4,8,512]{3,2,1,0:T(8,128)S(1)}, f32[1,4,8,512]{3,2,1,0:T(8,128)S(1)}, u32[]{:S(2)}, u32[]{:S(2)}) %collective-permute-start.8) | collective-permute-done | bytes 65568 | tf_op jit(solution)/shard_map/ppermute | solution.py:300
  15.9 0.7 %last_merge.1 = f32[4,16,512]{2,1,0:T(8,128)} custom-call(f32[1,4,16,512]{3,2,1,0:T(8,128)S(1)} %first_merge.4.kept, f32[1,4,8,512]{3,2,1,0:T(8,128)S(1)} %collective-permute-done.4.rest_0_, f32[1,4,8,512]{3,2,1,0:T(8,128)S(1)} %collective-permute-done.8.rest_1_), custom_call_target="tpu_custom_call" | custom-call | tf_op jit(solution)/shard_map/last_merge/pallas_call | solution.py:245
  (6 shorter events, 0.1 us)
Async XLA Ops:
  1.3 7.0 %collective-permute-start = (f32[16,2048]{1,0:T(8,128)S(1)}, f32[16,2048]{1,0:T(8,128)S(1)}, u32[]{:S(2)}, u32[]{:S(2)}) collective-permute-start(f32[16,2048]{1,0:T(8,128)S(1)} %get-tuple-element.22), channel_id=1, source_target_pairs={{0,8},{1,9},{2,10},{3,11},{4,12},{5,13},{6,14},{7,15},{8,0},{9,1},... | collective-permute-start | bytes 393224 | tf_op jit(solution)/shard_map/ppermute | solution.py:89
  1.8 6.5 %collective-permute-start.1 = (f32[16,2048]{1,0:T(8,128)S(1)}, f32[16,2048]{1,0:T(8,128)S(1)}, u32[]{:S(2)}, u32[]{:S(2)}) collective-permute-start(f32[16,2048]{1,0:T(8,128)S(1)} %get-tuple-element.23), channel_id=1, source_target_pairs={{0,1},{1,0},{2,3},{3,2},{4,5},{5,4},{6,7},{7,6},{8,16},{9,17},{10,... | collective-permute-start | bytes 393224 | tf_op jit(solution)/shard_map/ppermute | solution.py:89
  4.3 3.9 %collective-permute-start.2 = (f32[4,2048]{1,0:T(4,128)S(1)}, f32[4,2048]{1,0:T(4,128)S(1)}, u32[]{:S(2)}, u32[]{:S(2)}) collective-permute-start(f32[4,2048]{1,0:T(4,128)S(1)} %get-tuple-element.28), channel_id=1, source_target_pairs={{0,1},{1,0},{2,3},{3,2},{4,5},{5,4},{6,7},{7,6},{8,9},{9,8},{10,11... | collective-permute-start | bytes 98312 | tf_op jit(solution)/shard_map/ppermute | solution.py:89
  4.4 4.3 %collective-permute-start.5 = (f32[4,2048]{1,0:T(4,128)S(1)}, f32[4,2048]{1,0:T(4,128)S(1)}, u32[]{:S(2)}, u32[]{:S(2)}) collective-permute-start(f32[4,2048]{1,0:T(4,128)S(1)} %get-tuple-element.31), channel_id=1, source_target_pairs={{0,8},{1,2},{2,1},{3,4},{4,3},{5,6},{6,5},{7,15},{8,0},{9,10},{10,... | collective-permute-start | bytes 98312 | tf_op jit(solution)/shard_map/ppermute | solution.py:89
  8.4 1.5 %collective-permute-start.3 = (f32[1,4,8,512]{3,2,1,0:T(8,128)S(1)}, f32[1,4,8,512]{3,2,1,0:T(8,128)S(1)}, u32[]{:S(2)}, u32[]{:S(2)}) collective-permute-start(f32[1,4,8,512]{3,2,1,0:T(8,128)S(1)} %shade.6), channel_id=1, source_target_pairs={{0,8},{8,0},{16,24},{24,16},{1,9},{9,1},{17,25},{25,17},{2,10},{10... | collective-permute-start | bytes 196616 | tf_op jit(solution)/shard_map/ppermute | solution.py:300
  8.9 2.2 %collective-permute-start.7 = (f32[1,4,8,512]{3,2,1,0:T(8,128)S(1)}, f32[1,4,8,512]{3,2,1,0:T(8,128)S(1)}, u32[]{:S(2)}, u32[]{:S(2)}) collective-permute-start(f32[1,4,8,512]{3,2,1,0:T(8,128)S(1)} %shade.8), channel_id=1, source_target_pairs={{0,8},{8,0},{16,24},{24,16},{1,9},{9,1},{17,25},{25,17},{2,10},{10... | collective-permute-start | bytes 196616 | tf_op jit(solution)/shard_map/ppermute | solution.py:300
  9.8 5.3 %collective-permute-start.6 = (f32[1,4,16,512]{3,2,1,0:T(8,128)S(1)}, f32[1,4,16,512]{3,2,1,0:T(8,128)S(1)}, u32[]{:S(2)}, u32[]{:S(2)}) collective-permute-start(f32[1,4,16,512]{3,2,1,0:T(8,128)S(1)} %shade.11), channel_id=1, source_target_pairs={{0,8},{8,0},{16,24},{24,16},{1,9},{9,1},{17,25},{25,17},{2,10},{10... | collective-permute-start | bytes 393224 | tf_op jit(solution)/shard_map/ppermute | solution.py:300
  9.9 5.0 %collective-permute-start.4 = (f32[1,4,8,512]{3,2,1,0:T(8,128)S(1)}, f32[1,4,8,512]{3,2,1,0:T(8,128)S(1)}, u32[]{:S(2)}, u32[]{:S(2)}) collective-permute-start(f32[1,4,8,512]{3,2,1,0:T(8,128)S(1)} %first_merge.3), channel_id=1, source_target_pairs={{0,16},{8,24},{16,0},{24,8},{1,17},{9,25},{17,1},{25,9},{2,18},{10... | collective-permute-start | bytes 196616 | tf_op jit(solution)/shard_map/ppermute | solution.py:300
  11.1 4.8 %collective-permute-start.8 = (f32[1,4,8,512]{3,2,1,0:T(8,128)S(1)}, f32[1,4,8,512]{3,2,1,0:T(8,128)S(1)}, u32[]{:S(2)}, u32[]{:S(2)}) collective-permute-start(f32[1,4,8,512]{3,2,1,0:T(8,128)S(1)} %first_merge.5), channel_id=1, source_target_pairs={{0,16},{8,24},{16,0},{24,8},{1,17},{9,25},{17,1},{25,9},{2,18},{10... | collective-permute-start | bytes 196616 | tf_op jit(solution)/shard_map/ppermute | solution.py:300

commit v8 on v7

--- a/solution.py
+++ b/solution.py
@@ -139,9 +139,10 @@
 
 
 def shade_kernel(stays, bands, density, depth_even, depth_odd, weighted, passed, *rest):
-    trades, image = rest[:-1], rest[-1]
+    trades, images = rest[: len(bands)], rest[len(bands) :]
     slices, rows, cols = density.shape
-    pieces, _, _, piece = image.shape
+    pieces, _, _, piece = images[0].shape
+    planes = 4 * len(bands) // len(images)
     me, tile = lax.axis_index("depth"), lax.axis_index("tile")
     bits = [(me >> i) & 1 if stays[i] else 1 - ((me >> i) & 1) for i in range(2)]
     depth_is_low = me & 1 == 0
@@ -194,10 +195,9 @@
                     shade = 0.3 + facing * lax.rsqrt(jnp.maximum(square, 4.0))
                     for channel in range(3):
                         sums[channel] = sums[channel] + weighted[(channel, k, *at)] * shade
-                out = (slice(n * SUBLANES, (n + 1) * SUBLANES), slice(p, p + LANES))
-                for channel in range(3):
-                    image[(i, channel, *out)] = sums[channel]
-                image[(i, 3, *out)] = passed[at]
+                for channel, value in enumerate([*sums, passed[at]]):
+                    image, plane = divmod(4 * n + channel, planes)
+                    images[image][i, plane, :, p : p + LANES] = value
 
 
 def merged(behind, kept, received):
@@ -207,10 +207,14 @@
     return light, front[3] * back[3]
 
 
-def first_merge_kernel(kept, received, out):
+def first_merge_kernel(kept, *rest):
     behind = lax.axis_index("depth") & 1 == 1
+    received, out = rest[:-1], rest[-1]
     for i in range(kept.shape[0]):
-        out[i, 0:3], out[i, 3] = merged(behind, kept[i], received[i])
+        theirs = jnp.concatenate([x[i] for x in received], 0)
+        for at in range(0, kept.shape[1], 4):
+            one = slice(at, at + 4)
+            out[i, at : at + 3], out[i, at + 3] = merged(behind, kept[i, one], theirs[one])
 
 
 def merge_kernel(level, bands, kept, *rest):
@@ -218,25 +222,22 @@
     behind = (me >> level) & 1 == 1
     bit = (me >> (level + 1)) & 1
     received, (kept_out, *sent) = rest[:bands], rest[bands:]
-    height = kept.shape[2] // bands
     for i in range(kept.shape[0] // 2):
         for band in range(bands):
-            rows = slice(band * height, (band + 1) * height)
+            at = 4 * band
             j = 2 * i + bit
-            light, through = merged(behind, kept[j, :, rows], received[band][j])
-            kept_out[i, 0:3, rows], kept_out[i, 3, rows] = light, through
+            light, through = merged(behind, kept[j, at : at + 4], received[band][j])
+            kept_out[i, at : at + 3], kept_out[i, at + 3] = light, through
             j = 2 * i + 1 - bit
-            light, through = merged(behind, kept[j, :, rows], received[band][j])
+            light, through = merged(behind, kept[j, at : at + 4], received[band][j])
             sent[band][i, 0:3], sent[band][i, 3] = light, through
 
 
 def last_merge_kernel(level, bands, kept, *rest):
     behind = (lax.axis_index("depth") >> level) & 1 == 1
     received, out = rest[:bands], rest[bands]
-    height = kept.shape[2] // bands
     for band in range(bands):
-        rows = slice(band * height, (band + 1) * height)
-        light, through = merged(behind, kept[0, :, rows], received[band][0])
+        light, through = merged(behind, kept[0, 4 * band : 4 * band + 4], received[band][0])
         place = pl.ds(pl.multiple_of(lower(band) * SUBLANES, SUBLANES), SUBLANES)
         out[0:3, place], out[3, place] = light, 1.0 - through
 
@@ -302,12 +303,13 @@
     *faces, row_even, row_odd = traded
     rows_of = {EVEN: row_even, ODD: row_odd}
 
-    def shaded(stays, bands):
+    def shaded(stays, bands, count=1):
+        planes = 4 * len(bands) // count
         return pl.pallas_call(
             functools.partial(shade_kernel, stays, bands),
-            out_shape=f32(half // 2, 4, SUBLANES * len(bands), piece),
+            out_shape=[f32(half // 2, planes, SUBLANES, piece)] * count,
             in_specs=[vmem()] * (5 + len(bands)),
-            out_specs=vmem(),
+            out_specs=[vmem()] * count,
             compiler_params=params(),
             cost_estimate=cost(5 * slices * pixels, 2 * slices * pixels),
             name="shade",
@@ -317,21 +319,22 @@
     bands = (EVEN, ODD)
     sent_far = []
     for band in bands:
-        sent = shaded((False, False), (band,))
-        received = swap(sent, 0)
-        kept = shaded((True, False), (band,))
+        sent = shaded((False, False), (band,), 2 if band == EVEN else 1)
+        received = [swap(x, 0) for x in sent]
+        (kept,) = shaded((True, False), (band,))
         _, kept, weighted = lax.optimization_barrier((sent, kept, weighted))
         if sent_far:
             _, kept = lax.optimization_barrier((sent_far[-1], kept))
-        sent_far.append(call(first_merge_kernel, "first_merge", f32(*kept.shape), kept, received))
+        sent_far.append(call(first_merge_kernel, "first_merge", f32(*kept.shape), kept, *received))
     received = [swap(x, 1) for x in sent_far]
-    sent = shaded((False, True), bands)
+    _, weighted = lax.optimization_barrier((sent_far[-1], weighted))
+    near = [swap(x, 0) for x in shaded((False, True), bands, 4)]
     received[0], weighted = lax.optimization_barrier((received[0], weighted))
-    kept = shaded((True, True), bands)
-    kept = call(first_merge_kernel, "first_merge", f32(*kept.shape), kept, swap(sent, 0))
+    (kept,) = shaded((True, True), bands)
+    kept = call(first_merge_kernel, "first_merge", f32(*kept.shape), kept, *near)
     for level in range(1, levels - 1):
         left = kept.shape[0] // 2
-        shapes = [f32(left, 4, rows, piece)] + [f32(left, 4, SUBLANES, piece)] * len(bands)
+        shapes = [f32(left, 4 * len(bands), SUBLANES, piece)] + [f32(left, 4, SUBLANES, piece)] * len(bands)
         kernel = functools.partial(merge_kernel, level, len(bands))
         kept, *sent = call(kernel, "merge", shapes, kept, *received)
         received = [swap(x, level + 1) for x in sent]

time: 16.7 us -> 17 us (1.018)
  starting transfers between devices: 7.3 us -> 7.95 us
  waiting for transfers between devices: 4.38 us -> 3.96 us
    ppermute x5 -> x9, starting transfers between devices: 2.87 us -> 3.52 us  [swap(): lax.ppermute(x, 'depth', [(i, i ^ 1 << level) for i in range(slab_count)])]
    ppermute x5 -> x9, waiting for transfers between devices: 3.49 us -> 3.07 us  [swap(): lax.ppermute(x, 'depth', [(i, i ^ 1 << level) for i in range(slab_count)])]
  transfers between devices with their start and end apart: 9 -> 13, of which waited for: 3 -> 5; matrix products, arithmetic and copies ran while one was open for 0% -> 0% of each run, Pallas kernels for 13% -> 13%
where the time goes in v8:
time: 17 us; the launch traced here: 16.8 us
  starting transfers between devices  7.95 us (47%)
  Pallas kernels  4.11 us (24%)
  waiting for transfers between devices  3.96 us (23%)
  between operations  0.77 us (5%)
    ppermute x4, starting transfers between devices, trade(): return lax.ppermute(x, ('depth', 'tile'), pairs)  4.44 us
    ppermute x9, starting transfers between devices, swap(): lax.ppermute(x, 'depth', [(i, i ^ 1 << level) for i in range(slab_count)])  3.52 us
    ppermute x9, waiting for transfers between devices, swap(): lax.ppermute(x, 'depth', [(i, i ^ 1 << level) for i in range(slab_count)])  3.07 us
    pallas_call x1, Pallas kernels, on_device(): pl.pallas_call(load_kernel, out_shape=[f32(*density.shape), jax.ShapeDtyp...  1.25 us
    pallas_call x6, Pallas kernels, shaded(): pl.pallas_call(functools.partial(shade_kernel, stays, bands), out_shape=[...  1.08 us
    pallas_call x1, Pallas kernels, on_device(): pl.pallas_call(weights_kernel, out_shape=[f32(3, slices, rows, cols), f32...  1.02 us
    ppermute x4, waiting for transfers between devices, trade(): return lax.ppermute(x, ('depth', 'tile'), pairs)  0.89 us
    pallas_call x4, Pallas kernels, call(): pl.pallas_call(kernel, out_shape=out_shape, in_specs=[vmem()] * len(args)...  0.75 us
  transfers between devices with their start and end apart: 13, of which 5 were waited for; matrix products, arithmetic and copies ran while one was open for 0% of the time, Pallas kernels for 13%

profile of v8, /device:TPU:0, one launch (start us, length us, event | category | flops | bytes accessed | tf_op | source)
XLA Modules:
  0.0 16.8 jit_solution(249444369741055225)
XLA Ops:
  0.0 1.3 %load.1 = (f32[4,16,2048]{2,1,0:T(8,128)S(1)}, s32[4,16,2048]{2,1,0:T(8,128)S(1)}, f32[16,2048]{1,0:T(8,128)S(1)}, f32[16,2048]{1,0:T(8,128)S(1)}, f32[4,2048]{1...) custom-call(f32[4,16,2048]{2,1,0:T(8,128)} %density_in.1, s32[4,16,2048]{2,1,0:T(8,128)} %bins_in.1, ...), custom_call_target="tpu_custom_call" | custom-call | tf_op jit(solution)/shard_map/load/pallas_call | solution.py:263
  1.3 0.5 %collective-permute-start = (f32[16,2048]{1,0:T(8,128)S(1)}, f32[16,2048]{1,0:T(8,128)S(1)}, u32[]{:S(2)}, u32[]{:S(2)}) collective-permute-start(f32[16,2048]{1,0:T(8,128)S(1)} %get-tuple-element.29), channel_id=1, source_target_pairs={{0,8},{1,9},{2,10},{3,11},{4,12},{5,13},{6,14},{7,15},{8,0},{9,1},... | collective-permute-start | bytes 393224 | tf_op jit(solution)/shard_map/ppermute | solution.py:89
  1.8 2.6 %collective-permute-start.1 = (f32[16,2048]{1,0:T(8,128)S(1)}, f32[16,2048]{1,0:T(8,128)S(1)}, u32[]{:S(2)}, u32[]{:S(2)}) collective-permute-start(f32[16,2048]{1,0:T(8,128)S(1)} %get-tuple-element.30), channel_id=1, source_target_pairs={{0,1},{1,0},{2,3},{3,2},{4,5},{5,4},{6,7},{7,6},{8,16},{9,17},{10,... | collective-permute-start | bytes 393224 | tf_op jit(solution)/shard_map/ppermute | solution.py:89
  4.3 0.1 collective-permute-start.2
  4.4 1.3 %collective-permute-start.6 = (f32[4,2048]{1,0:T(4,128)S(1)}, f32[4,2048]{1,0:T(4,128)S(1)}, u32[]{:S(2)}, u32[]{:S(2)}) collective-permute-start(f32[4,2048]{1,0:T(4,128)S(1)} %get-tuple-element.40), channel_id=1, source_target_pairs={{0,8},{1,2},{2,1},{3,4},{4,3},{5,6},{6,5},{7,15},{8,0},{9,10},{10,... | collective-permute-start | bytes 98312 | tf_op jit(solution)/shard_map/ppermute | solution.py:89
  6.3 1.0 %weights.1 = (f32[3,4,16,2048]{3,2,1,0:T(8,128)S(1)}, f32[16,2048]{1,0:T(8,128)S(1)}) custom-call(s32[1,1]{1,0:T(1,128)S(6)} %copy.6.count, s32[4,16,2048]{2,1,0:T(8,128)S(1)} %get-tuple-element.31.bins, s32[2,2,8,128]{3,2,1,0:T(8,128)S(1)} %get-tuple-element.32.tables), custom_call_target="tpu_custom_call" | custom-call | flops 8388608 | bytes 2097152 | tf_op jit(solution)/shard_map/weights/pallas_call | solution.py:290
  7.4 0.9 %collective-permute-done.2.rest_0_ = f32[4,2048]{1,0:T(4,128)S(1)} collective-permute-done((f32[4,2048]{1,0:T(4,128)S(1)}, f32[4,2048]{1,0:T(4,128)S(1)}, u32[]{:S(2)}, u32[]{:S(2)}) %collective-permute-start.2) | collective-permute-done | bytes 32800 | tf_op jit(solution)/shard_map/ppermute | solution.py:89
  8.3 0.2 shade.6
  8.5 0.5 %collective-permute-start.4 = (f32[1,2,8,512]{3,2,1,0:T(8,128)S(1)}, f32[1,2,8,512]{3,2,1,0:T(8,128)S(1)}, u32[]{:S(2)}, u32[]{:S(2)}) collective-permute-start(f32[1,2,8,512]{3,2,1,0:T(8,128)S(1)} %get-tuple-element.37), channel_id=1, source_target_pairs={{0,8},{8,0},{16,24},{24,16},{1,9},{9,1},{17,25},{25,17},{2,10},{10... | collective-permute-start | bytes 98312 | tf_op jit(solution)/shard_map/ppermute | solution.py:301
  9.0 0.2 shade.7.kept
  9.2 0.2 %shade.8 = f32[1,4,8,512]{3,2,1,0:T(8,128)S(1)} custom-call(f32[4,16,2048]{2,1,0:T(8,128)S(1)} %get-tuple-element.28.density, f32[16,2048]{1,0:T(8,128)S(1)} %collective-permute-done.depth_even, f32[16,2048]{1,0:T(8,128)S(1)} %collective-permute-done.1.depth_odd, f32[3,4,16,2048]{3,2,1,0:T(8,128)S(1)} %get-tuple-element.45.weighted, ...), custom_call_target="tpu_custom_call" | custom-call | flops 655360 | bytes 262144 | tf_op jit(solution)/shard_map/shade/pallas_call | solution.py:308
  9.3 0.1 collective-permute-start.7
  9.5 0.2 %collective-permute-done.3.rest_0_ = f32[1,2,8,512]{3,2,1,0:T(8,128)S(1)} collective-permute-done((f32[1,2,8,512]{3,2,1,0:T(8,128)S(1)}, f32[1,2,8,512]{3,2,1,0:T(8,128)S(1)}, u32[]{:S(2)}, u32[]{:S(2)}) %collective-permute-start.3) | collective-permute-done | bytes 32800 | tf_op jit(solution)/shard_map/ppermute | solution.py:301
  9.7 0.2 collective-permute-done.4.rest_1_
  9.9 1.0 %collective-permute-start.5 = (f32[1,4,8,512]{3,2,1,0:T(8,128)S(1)}, f32[1,4,8,512]{3,2,1,0:T(8,128)S(1)}, u32[]{:S(2)}, u32[]{:S(2)}) collective-permute-start(f32[1,4,8,512]{3,2,1,0:T(8,128)S(1)} %first_merge.3), channel_id=1, source_target_pairs={{0,16},{8,24},{16,0},{24,8},{1,17},{9,25},{17,1},{25,9},{2,18},{10... | collective-permute-start | bytes 196616 | tf_op jit(solution)/shard_map/ppermute | solution.py:301
  10.9 0.2 shade.9.kept
  11.1 1.2 %collective-permute-start.12 = (f32[1,4,8,512]{3,2,1,0:T(8,128)S(1)}, f32[1,4,8,512]{3,2,1,0:T(8,128)S(1)}, u32[]{:S(2)}, u32[]{:S(2)}) collective-permute-start(f32[1,4,8,512]{3,2,1,0:T(8,128)S(1)} %first_merge.4), channel_id=1, source_target_pairs={{0,16},{8,24},{16,0},{24,8},{1,17},{9,25},{17,1},{25,9},{2,18},{10... | collective-permute-start | bytes 196616 | tf_op jit(solution)/shard_map/ppermute | solution.py:301
  12.2 0.2 %shade.11 = (f32[1,2,8,512]{3,2,1,0:T(8,128)S(1)}, f32[1,2,8,512]{3,2,1,0:T(8,128)S(1)}, f32[1,2,8,512]{3,2,1,0:T(8,128)S(1)}, f32[1,2,8,512]{3,2,1,0:T(8,128)S(1)}) custom-call(f32[4,16,2048]{2,1,0:T(8,128)S(1)} %get-tuple-element.28.density, f32[16,2048]{1,0:T(8,128)S(1)} %collective-permute-done.depth_even, ...), custom_call_target="tpu_custom_call" | custom-call | flops 655360 | bytes 262144 | tf_op jit(solution)/shard_map/shade/pallas_call | solution.py:308
  12.5 0.5 %collective-permute-start.9 = (f32[1,2,8,512]{3,2,1,0:T(8,128)S(1)}, f32[1,2,8,512]{3,2,1,0:T(8,128)S(1)}, u32[]{:S(2)}, u32[]{:S(2)}) collective-permute-start(f32[1,2,8,512]{3,2,1,0:T(8,128)S(1)} %get-tuple-element.47), channel_id=1, source_target_pairs={{0,8},{8,0},{16,24},{24,16},{1,9},{9,1},{17,25},{25,17},{2,10},{10... | collective-permute-start | bytes 98312 | tf_op jit(solution)/shard_map/ppermute | solution.py:301
  13.0 0.1 collective-permute-start.10
  13.1 1.7 %collective-permute-done.5.rest_0_ = f32[1,4,8,512]{3,2,1,0:T(8,128)S(1)} collective-permute-done((f32[1,4,8,512]{3,2,1,0:T(8,128)S(1)}, f32[1,4,8,512]{3,2,1,0:T(8,128)S(1)}, u32[]{:S(2)}, u32[]{:S(2)}) %collective-permute-start.5) | collective-permute-done | bytes 65568 | tf_op jit(solution)/shard_map/ppermute | solution.py:301
  14.9 0.2 %shade.10.kept = f32[1,8,8,512]{3,2,1,0:T(8,128)S(1)} custom-call(f32[4,16,2048]{2,1,0:T(8,128)S(1)} %get-tuple-element.28.density, f32[16,2048]{1,0:T(8,128)S(1)} %collective-permute-done.depth_even, f32[16,2048]{1,0:T(8,128)S(1)} %collective-permute-done.1.depth_odd, f32[3,4,16,2048]{3,2,1,0:T(8,128)S(1)} %get-tuple-element.45.weighted, ...), custom_call_target="tpu_custom_call" | custom-call | flops 655360 | bytes 262144 | tf_op jit(solution)/shard_map/shade/pallas_call | solution.py:308
  15.1 0.9 %collective-permute-done.11.rest_3_ = f32[1,2,8,512]{3,2,1,0:T(8,128)S(1)} collective-permute-done((f32[1,2,8,512]{3,2,1,0:T(8,128)S(1)}, f32[1,2,8,512]{3,2,1,0:T(8,128)S(1)}, u32[]{:S(2)}, u32[]{:S(2)}) %collective-permute-start.11) | collective-permute-done | bytes 32800 | tf_op jit(solution)/shard_map/ppermute | solution.py:301
  16.1 0.7 %last_merge.1 = f32[4,16,512]{2,1,0:T(8,128)} custom-call(f32[1,8,8,512]{3,2,1,0:T(8,128)S(1)} %first_merge.5.kept, f32[1,4,8,512]{3,2,1,0:T(8,128)S(1)} %collective-permute-done.5.rest_0_, f32[1,4,8,512]{3,2,1,0:T(8,128)S(1)} %collective-permute-done.12.rest_1_), custom_call_target="tpu_custom_call" | custom-call | tf_op jit(solution)/shard_map/last_merge/pallas_call | solution.py:246
  (14 shorter events, 0.2 us)
Async XLA Ops:
  1.3 7.0 %collective-permute-start = (f32[16,2048]{1,0:T(8,128)S(1)}, f32[16,2048]{1,0:T(8,128)S(1)}, u32[]{:S(2)}, u32[]{:S(2)}) collective-permute-start(f32[16,2048]{1,0:T(8,128)S(1)} %get-tuple-element.29), channel_id=1, source_target_pairs={{0,8},{1,9},{2,10},{3,11},{4,12},{5,13},{6,14},{7,15},{8,0},{9,1},... | collective-permute-start | bytes 393224 | tf_op jit(solution)/shard_map/ppermute | solution.py:89
  1.8 6.5 %collective-permute-start.1 = (f32[16,2048]{1,0:T(8,128)S(1)}, f32[16,2048]{1,0:T(8,128)S(1)}, u32[]{:S(2)}, u32[]{:S(2)}) collective-permute-start(f32[16,2048]{1,0:T(8,128)S(1)} %get-tuple-element.30), channel_id=1, source_target_pairs={{0,1},{1,0},{2,3},{3,2},{4,5},{5,4},{6,7},{7,6},{8,16},{9,17},{10,... | collective-permute-start | bytes 393224 | tf_op jit(solution)/shard_map/ppermute | solution.py:89
  4.3 3.9 %collective-permute-start.2 = (f32[4,2048]{1,0:T(4,128)S(1)}, f32[4,2048]{1,0:T(4,128)S(1)}, u32[]{:S(2)}, u32[]{:S(2)}) collective-permute-start(f32[4,2048]{1,0:T(4,128)S(1)} %get-tuple-element.35), channel_id=1, source_target_pairs={{0,1},{1,0},{2,3},{3,2},{4,5},{5,4},{6,7},{7,6},{8,9},{9,8},{10,11... | collective-permute-start | bytes 98312 | tf_op jit(solution)/shard_map/ppermute | solution.py:89
  4.4 4.7 %collective-permute-start.6 = (f32[4,2048]{1,0:T(4,128)S(1)}, f32[4,2048]{1,0:T(4,128)S(1)}, u32[]{:S(2)}, u32[]{:S(2)}) collective-permute-start(f32[4,2048]{1,0:T(4,128)S(1)} %get-tuple-element.40), channel_id=1, source_target_pairs={{0,8},{1,2},{2,1},{3,4},{4,3},{5,6},{6,5},{7,15},{8,0},{9,10},{10,... | collective-permute-start | bytes 98312 | tf_op jit(solution)/shard_map/ppermute | solution.py:89
  8.4 1.3 %collective-permute-start.3 = (f32[1,2,8,512]{3,2,1,0:T(8,128)S(1)}, f32[1,2,8,512]{3,2,1,0:T(8,128)S(1)}, u32[]{:S(2)}, u32[]{:S(2)}) collective-permute-start(f32[1,2,8,512]{3,2,1,0:T(8,128)S(1)} %get-tuple-element.36), channel_id=1, source_target_pairs={{0,8},{8,0},{16,24},{24,16},{1,9},{9,1},{17,25},{25,17},{2,10},{10... | collective-permute-start | bytes 98312 | tf_op jit(solution)/shard_map/ppermute | solution.py:301
  8.5 1.4 %collective-permute-start.4 = (f32[1,2,8,512]{3,2,1,0:T(8,128)S(1)}, f32[1,2,8,512]{3,2,1,0:T(8,128)S(1)}, u32[]{:S(2)}, u32[]{:S(2)}) collective-permute-start(f32[1,2,8,512]{3,2,1,0:T(8,128)S(1)} %get-tuple-element.37), channel_id=1, source_target_pairs={{0,8},{8,0},{16,24},{24,16},{1,9},{9,1},{17,25},{25,17},{2,10},{10... | collective-permute-start | bytes 98312 | tf_op jit(solution)/shard_map/ppermute | solution.py:301
  9.3 1.7 %collective-permute-start.7 = (f32[1,4,8,512]{3,2,1,0:T(8,128)S(1)}, f32[1,4,8,512]{3,2,1,0:T(8,128)S(1)}, u32[]{:S(2)}, u32[]{:S(2)}) collective-permute-start(f32[1,4,8,512]{3,2,1,0:T(8,128)S(1)} %shade.8), channel_id=1, source_target_pairs={{0,8},{8,0},{16,24},{24,16},{1,9},{9,1},{17,25},{25,17},{2,10},{10... | collective-permute-start | bytes 196616 | tf_op jit(solution)/shard_map/ppermute | solution.py:301
  9.9 5.0 %collective-permute-start.5 = (f32[1,4,8,512]{3,2,1,0:T(8,128)S(1)}, f32[1,4,8,512]{3,2,1,0:T(8,128)S(1)}, u32[]{:S(2)}, u32[]{:S(2)}) collective-permute-start(f32[1,4,8,512]{3,2,1,0:T(8,128)S(1)} %first_merge.3), channel_id=1, source_target_pairs={{0,16},{8,24},{16,0},{24,8},{1,17},{9,25},{17,1},{25,9},{2,18},{10... | collective-permute-start | bytes 196616 | tf_op jit(solution)/shard_map/ppermute | solution.py:301
  11.1 5.0 %collective-permute-start.12 = (f32[1,4,8,512]{3,2,1,0:T(8,128)S(1)}, f32[1,4,8,512]{3,2,1,0:T(8,128)S(1)}, u32[]{:S(2)}, u32[]{:S(2)}) collective-permute-start(f32[1,4,8,512]{3,2,1,0:T(8,128)S(1)} %first_merge.4), channel_id=1, source_target_pairs={{0,16},{8,24},{16,0},{24,8},{1,17},{9,25},{17,1},{25,9},{2,18},{10... | collective-permute-start | bytes 196616 | tf_op jit(solution)/shard_map/ppermute | solution.py:301
  12.5 2.6 %collective-permute-start.8 = (f32[1,2,8,512]{3,2,1,0:T(8,128)S(1)}, f32[1,2,8,512]{3,2,1,0:T(8,128)S(1)}, u32[]{:S(2)}, u32[]{:S(2)}) collective-permute-start(f32[1,2,8,512]{3,2,1,0:T(8,128)S(1)} %get-tuple-element.46), channel_id=1, source_target_pairs={{0,8},{8,0},{16,24},{24,16},{1,9},{9,1},{17,25},{25,17},{2,10},{10... | collective-permute-start | bytes 98312 | tf_op jit(solution)/shard_map/ppermute | solution.py:301
  12.5 2.6 %collective-permute-start.9 = (f32[1,2,8,512]{3,2,1,0:T(8,128)S(1)}, f32[1,2,8,512]{3,2,1,0:T(8,128)S(1)}, u32[]{:S(2)}, u32[]{:S(2)}) collective-permute-start(f32[1,2,8,512]{3,2,1,0:T(8,128)S(1)} %get-tuple-element.47), channel_id=1, source_target_pairs={{0,8},{8,0},{16,24},{24,16},{1,9},{9,1},{17,25},{25,17},{2,10},{10... | collective-permute-start | bytes 98312 | tf_op jit(solution)/shard_map/ppermute | solution.py:301
  13.0 2.1 %collective-permute-start.10 = (f32[1,2,8,512]{3,2,1,0:T(8,128)S(1)}, f32[1,2,8,512]{3,2,1,0:T(8,128)S(1)}, u32[]{:S(2)}, u32[]{:S(2)}) collective-permute-start(f32[1,2,8,512]{3,2,1,0:T(8,128)S(1)} %get-tuple-element.48), channel_id=1, source_target_pairs={{0,8},{8,0},{16,24},{24,16},{1,9},{9,1},{17,25},{25,17},{2,10},{10... | collective-permute-start | bytes 98312 | tf_op jit(solution)/shard_map/ppermute | solution.py:301
  14.9 1.2 %collective-permute-start.11 = (f32[1,2,8,512]{3,2,1,0:T(8,128)S(1)}, f32[1,2,8,512]{3,2,1,0:T(8,128)S(1)}, u32[]{:S(2)}, u32[]{:S(2)}) collective-permute-start(f32[1,2,8,512]{3,2,1,0:T(8,128)S(1)} %get-tuple-element.49), channel_id=1, source_target_pairs={{0,8},{8,0},{16,24},{24,16},{1,9},{9,1},{17,25},{25,17},{2,10},{10... | collective-permute-start | bytes 98312 | tf_op jit(solution)/shard_map/ppermute | solution.py:301

commit v9 on v8

--- a/solution.py
+++ b/solution.py
@@ -142,7 +142,7 @@
     trades, images = rest[: len(bands)], rest[len(bands) :]
     slices, rows, cols = density.shape
     pieces, _, _, piece = images[0].shape
-    planes = 4 * len(bands) // len(images)
+    planes = [(image, i) for image in images for i in range(image.shape[1])]
     me, tile = lax.axis_index("depth"), lax.axis_index("tile")
     bits = [(me >> i) & 1 if stays[i] else 1 - ((me >> i) & 1) for i in range(2)]
     depth_is_low = me & 1 == 0
@@ -196,8 +196,8 @@
                     for channel in range(3):
                         sums[channel] = sums[channel] + weighted[(channel, k, *at)] * shade
                 for channel, value in enumerate([*sums, passed[at]]):
-                    image, plane = divmod(4 * n + channel, planes)
-                    images[image][i, plane, :, p : p + LANES] = value
+                    image, plane = planes[4 * n + channel]
+                    image[i, plane, :, p : p + LANES] = value
 
 
 def merged(behind, kept, received):
@@ -303,13 +303,12 @@
     *faces, row_even, row_odd = traded
     rows_of = {EVEN: row_even, ODD: row_odd}
 
-    def shaded(stays, bands, count=1):
-        planes = 4 * len(bands) // count
+    def shaded(stays, bands, planes):
         return pl.pallas_call(
             functools.partial(shade_kernel, stays, bands),
-            out_shape=[f32(half // 2, planes, SUBLANES, piece)] * count,
+            out_shape=[f32(half // 2, count, SUBLANES, piece) for count in planes],
             in_specs=[vmem()] * (5 + len(bands)),
-            out_specs=[vmem()] * count,
+            out_specs=[vmem()] * len(planes),
             compiler_params=params(),
             cost_estimate=cost(5 * slices * pixels, 2 * slices * pixels),
             name="shade",
@@ -319,18 +318,18 @@
     bands = (EVEN, ODD)
     sent_far = []
     for band in bands:
-        sent = shaded((False, False), (band,), 2 if band == EVEN else 1)
+        sent = shaded((False, False), (band,), (4,) if band == EVEN else (4,))
         received = [swap(x, 0) for x in sent]
-        (kept,) = shaded((True, False), (band,))
+        (kept,) = shaded((True, False), (band,), (4,))
         _, kept, weighted = lax.optimization_barrier((sent, kept, weighted))
         if sent_far:
             _, kept = lax.optimization_barrier((sent_far[-1], kept))
         sent_far.append(call(first_merge_kernel, "first_merge", f32(*kept.shape), kept, *received))
     received = [swap(x, 1) for x in sent_far]
     _, weighted = lax.optimization_barrier((sent_far[-1], weighted))
-    near = [swap(x, 0) for x in shaded((False, True), bands, 4)]
+    near = [swap(x, 0) for x in shaded((False, True), bands, (3, 3, 2))]
     received[0], weighted = lax.optimization_barrier((received[0], weighted))
-    (kept,) = shaded((True, True), bands)
+    (kept,) = shaded((True, True), bands, (8,))
     kept = call(first_merge_kernel, "first_merge", f32(*kept.shape), kept, *near)
     for level in range(1, levels - 1):
         left = kept.shape[0] // 2

time: 17 us -> 16.3 us (0.959)
  waiting for transfers between devices: 3.96 us -> 3.44 us
    ppermute x9 -> x7, waiting for transfers between devices: 3.07 us -> 2.55 us  [swap(): lax.ppermute(x, 'depth', [(i, i ^ 1 << level) for i in range(slab_count)])]
    ppermute x9 -> x7, starting transfers between devices: 3.52 us -> 3.42 us  [swap(): lax.ppermute(x, 'depth', [(i, i ^ 1 << level) for i in range(slab_count)])]
  transfers between devices with their start and end apart: 13 -> 11, of which waited for: 5 -> 4; matrix products, arithmetic and copies ran while one was open for 0% -> 0% of each run, Pallas kernels for 13% -> 14%
where the time goes in v9:
time: 16.3 us; the launch traced here: 16.2 us
  starting transfers between devices  7.86 us (48%)
  Pallas kernels  4.12 us (25%)
  waiting for transfers between devices  3.44 us (21%)
  between operations  0.76 us (5%)
    ppermute x4, starting transfers between devices, trade(): return lax.ppermute(x, ('depth', 'tile'), pairs)  4.44 us
    ppermute x7, starting transfers between devices, swap(): lax.ppermute(x, 'depth', [(i, i ^ 1 << level) for i in range(slab_count)])  3.42 us
    ppermute x7, waiting for transfers between devices, swap(): lax.ppermute(x, 'depth', [(i, i ^ 1 << level) for i in range(slab_count)])  2.55 us
    pallas_call x1, Pallas kernels, on_device(): pl.pallas_call(load_kernel, out_shape=[f32(*density.shape), jax.ShapeDtyp...  1.25 us
    pallas_call x6, Pallas kernels, shaded(): pl.pallas_call(functools.partial(shade_kernel, stays, bands), out_shape=[...  1.1 us
    pallas_call x1, Pallas kernels, on_device(): pl.pallas_call(weights_kernel, out_shape=[f32(3, slices, rows, cols), f32...  1.02 us
    ppermute x4, waiting for transfers between devices, trade(): return lax.ppermute(x, ('depth', 'tile'), pairs)  0.89 us
    pallas_call x4, Pallas kernels, call(): pl.pallas_call(kernel, out_shape=out_shape, in_specs=[vmem()] * len(args)...  0.75 us
  transfers between devices with their start and end apart: 11, of which 4 were waited for; matrix products, arithmetic and copies ran while one was open for 0% of the time, Pallas kernels for 14%

profile of v9, /device:TPU:0, one launch (start us, length us, event | category | flops | bytes accessed | tf_op | source)
XLA Modules:
  0.0 16.2 jit_solution(8179321913301354435)
XLA Ops:
  0.0 1.3 %load.1 = (f32[4,16,2048]{2,1,0:T(8,128)S(1)}, s32[4,16,2048]{2,1,0:T(8,128)S(1)}, f32[16,2048]{1,0:T(8,128)S(1)}, f32[16,2048]{1,0:T(8,128)S(1)}, f32[4,2048]{1...) custom-call(f32[4,16,2048]{2,1,0:T(8,128)} %density_in.1, s32[4,16,2048]{2,1,0:T(8,128)} %bins_in.1, ...), custom_call_target="tpu_custom_call" | custom-call | tf_op jit(solution)/shard_map/load/pallas_call | solution.py:263
  1.3 0.5 %collective-permute-start = (f32[16,2048]{1,0:T(8,128)S(1)}, f32[16,2048]{1,0:T(8,128)S(1)}, u32[]{:S(2)}, u32[]{:S(2)}) collective-permute-start(f32[16,2048]{1,0:T(8,128)S(1)} %get-tuple-element.26), channel_id=1, source_target_pairs={{0,8},{1,9},{2,10},{3,11},{4,12},{5,13},{6,14},{7,15},{8,0},{9,1},... | collective-permute-start | bytes 393224 | tf_op jit(solution)/shard_map/ppermute | solution.py:89
  1.8 2.6 %collective-permute-start.1 = (f32[16,2048]{1,0:T(8,128)S(1)}, f32[16,2048]{1,0:T(8,128)S(1)}, u32[]{:S(2)}, u32[]{:S(2)}) collective-permute-start(f32[16,2048]{1,0:T(8,128)S(1)} %get-tuple-element.27), channel_id=1, source_target_pairs={{0,1},{1,0},{2,3},{3,2},{4,5},{5,4},{6,7},{7,6},{8,16},{9,17},{10,... | collective-permute-start | bytes 393224 | tf_op jit(solution)/shard_map/ppermute | solution.py:89
  4.3 0.1 collective-permute-start.2
  4.4 1.3 %collective-permute-start.5 = (f32[4,2048]{1,0:T(4,128)S(1)}, f32[4,2048]{1,0:T(4,128)S(1)}, u32[]{:S(2)}, u32[]{:S(2)}) collective-permute-start(f32[4,2048]{1,0:T(4,128)S(1)} %get-tuple-element.35), channel_id=1, source_target_pairs={{0,8},{1,2},{2,1},{3,4},{4,3},{5,6},{6,5},{7,15},{8,0},{9,10},{10,... | collective-permute-start | bytes 98312 | tf_op jit(solution)/shard_map/ppermute | solution.py:89
  6.3 1.0 %weights.1 = (f32[3,4,16,2048]{3,2,1,0:T(8,128)S(1)}, f32[16,2048]{1,0:T(8,128)S(1)}) custom-call(s32[1,1]{1,0:T(1,128)S(6)} %copy.6.count, s32[4,16,2048]{2,1,0:T(8,128)S(1)} %get-tuple-element.28.bins, s32[2,2,8,128]{3,2,1,0:T(8,128)S(1)} %get-tuple-element.29.tables), custom_call_target="tpu_custom_call" | custom-call | flops 8388608 | bytes 2097152 | tf_op jit(solution)/shard_map/weights/pallas_call | solution.py:290
  7.4 0.9 %collective-permute-done.2.rest_0_ = f32[4,2048]{1,0:T(4,128)S(1)} collective-permute-done((f32[4,2048]{1,0:T(4,128)S(1)}, f32[4,2048]{1,0:T(4,128)S(1)}, u32[]{:S(2)}, u32[]{:S(2)}) %collective-permute-start.2) | collective-permute-done | bytes 32800 | tf_op jit(solution)/shard_map/ppermute | solution.py:89
  8.3 0.2 %shade.6 = f32[1,4,8,512]{3,2,1,0:T(8,128)S(1)} custom-call(f32[4,16,2048]{2,1,0:T(8,128)S(1)} %get-tuple-element.25.density, f32[16,2048]{1,0:T(8,128)S(1)} %collective-permute-done.depth_even, f32[16,2048]{1,0:T(8,128)S(1)} %collective-permute-done.1.depth_odd, f32[3,4,16,2048]{3,2,1,0:T(8,128)S(1)} %get-tuple-element.40.weighted, ...), custom_call_target="tpu_custom_call" | custom-call | flops 655360 | bytes 262144 | tf_op jit(solution)/shard_map/shade/pallas_call | solution.py:307
  8.4 0.1 collective-permute-start.3
  8.5 0.2 %shade.7.kept = f32[1,4,8,512]{3,2,1,0:T(8,128)S(1)} custom-call(f32[4,16,2048]{2,1,0:T(8,128)S(1)} %get-tuple-element.25.density, f32[16,2048]{1,0:T(8,128)S(1)} %collective-permute-done.depth_even, f32[16,2048]{1,0:T(8,128)S(1)} %collective-permute-done.1.depth_odd, f32[3,4,16,2048]{3,2,1,0:T(8,128)S(1)} %get-tuple-element.40.weighted, ...), custom_call_target="tpu_custom_call" | custom-call | flops 655360 | bytes 262144 | tf_op jit(solution)/shard_map/shade/pallas_call | solution.py:307
  8.7 0.2 %shade.8 = f32[1,4,8,512]{3,2,1,0:T(8,128)S(1)} custom-call(f32[4,16,2048]{2,1,0:T(8,128)S(1)} %get-tuple-element.25.density, f32[16,2048]{1,0:T(8,128)S(1)} %collective-permute-done.depth_even, f32[16,2048]{1,0:T(8,128)S(1)} %collective-permute-done.1.depth_odd, f32[3,4,16,2048]{3,2,1,0:T(8,128)S(1)} %get-tuple-element.40.weighted, ...), custom_call_target="tpu_custom_call" | custom-call | flops 655360 | bytes 262144 | tf_op jit(solution)/shard_map/shade/pallas_call | solution.py:307
  8.9 0.5 %collective-permute-start.6 = (f32[1,4,8,512]{3,2,1,0:T(8,128)S(1)}, f32[1,4,8,512]{3,2,1,0:T(8,128)S(1)}, u32[]{:S(2)}, u32[]{:S(2)}) collective-permute-start(f32[1,4,8,512]{3,2,1,0:T(8,128)S(1)} %shade.8), channel_id=1, source_target_pairs={{0,8},{8,0},{16,24},{24,16},{1,9},{9,1},{17,25},{25,17},{2,10},{10... | collective-permute-start | bytes 196616 | tf_op jit(solution)/shard_map/ppermute | solution.py:301
  9.4 0.3 %collective-permute-done.3.rest_0_ = f32[1,4,8,512]{3,2,1,0:T(8,128)S(1)} collective-permute-done((f32[1,4,8,512]{3,2,1,0:T(8,128)S(1)}, f32[1,4,8,512]{3,2,1,0:T(8,128)S(1)}, u32[]{:S(2)}, u32[]{:S(2)}) %collective-permute-start.3) | collective-permute-done | bytes 65568 | tf_op jit(solution)/shard_map/ppermute | solution.py:301
  9.8 0.8 %collective-permute-start.4 = (f32[1,4,8,512]{3,2,1,0:T(8,128)S(1)}, f32[1,4,8,512]{3,2,1,0:T(8,128)S(1)}, u32[]{:S(2)}, u32[]{:S(2)}) collective-permute-start(f32[1,4,8,512]{3,2,1,0:T(8,128)S(1)} %first_merge.3), channel_id=1, source_target_pairs={{0,16},{8,24},{16,0},{24,8},{1,17},{9,25},{17,1},{25,9},{2,18},{10... | collective-permute-start | bytes 196616 | tf_op jit(solution)/shard_map/ppermute | solution.py:301
  10.5 0.2 shade.9.kept
  10.7 1.4 %collective-permute-start.10 = (f32[1,4,8,512]{3,2,1,0:T(8,128)S(1)}, f32[1,4,8,512]{3,2,1,0:T(8,128)S(1)}, u32[]{:S(2)}, u32[]{:S(2)}) collective-permute-start(f32[1,4,8,512]{3,2,1,0:T(8,128)S(1)} %first_merge.4), channel_id=1, source_target_pairs={{0,16},{8,24},{16,0},{24,8},{1,17},{9,25},{17,1},{25,9},{2,18},{10... | collective-permute-start | bytes 196616 | tf_op jit(solution)/shard_map/ppermute | solution.py:301
  12.1 0.2 %shade.11 = (f32[1,3,8,512]{3,2,1,0:T(8,128)S(1)}, f32[1,3,8,512]{3,2,1,0:T(8,128)S(1)}, f32[1,2,8,512]{3,2,1,0:T(8,128)S(1)}) custom-call(f32[4,16,2048]{2,1,0:T(8,128)S(1)} %get-tuple-element.25.density, f32[16,2048]{1,0:T(8,128)S(1)} %collective-permute-done.depth_even, f32[16,2048]{1,0:T(8,128)S(1)} %collective-permute-done.1.depth_odd, ...), custom_call_target="tpu_custom_call" | custom-call | flops 655360 | bytes 262144 | tf_op jit(solution)/shard_map/shade/pallas_call | solution.py:307
  12.4 0.1 collective-permute-start.7
  12.4 0.5 %collective-permute-start.8 = (f32[1,3,8,512]{3,2,1,0:T(8,128)S(1)}, f32[1,3,8,512]{3,2,1,0:T(8,128)S(1)}, u32[]{:S(2)}, u32[]{:S(2)}) collective-permute-start(f32[1,3,8,512]{3,2,1,0:T(8,128)S(1)} %get-tuple-element.42), channel_id=1, source_target_pairs={{0,8},{8,0},{16,24},{24,16},{1,9},{9,1},{17,25},{25,17},{2,10},{10... | collective-permute-start | bytes 147464 | tf_op jit(solution)/shard_map/ppermute | solution.py:301
  12.9 0.1 collective-permute-start.9
  13.0 1.7 %collective-permute-done.4.rest_0_ = f32[1,4,8,512]{3,2,1,0:T(8,128)S(1)} collective-permute-done((f32[1,4,8,512]{3,2,1,0:T(8,128)S(1)}, f32[1,4,8,512]{3,2,1,0:T(8,128)S(1)}, u32[]{:S(2)}, u32[]{:S(2)}) %collective-permute-start.4) | collective-permute-done | bytes 65568 | tf_op jit(solution)/shard_map/ppermute | solution.py:301
  14.7 0.2 %shade.10.kept = f32[1,8,8,512]{3,2,1,0:T(8,128)S(1)} custom-call(f32[4,16,2048]{2,1,0:T(8,128)S(1)} %get-tuple-element.25.density, f32[16,2048]{1,0:T(8,128)S(1)} %collective-permute-done.depth_even, f32[16,2048]{1,0:T(8,128)S(1)} %collective-permute-done.1.depth_odd, f32[3,4,16,2048]{3,2,1,0:T(8,128)S(1)} %get-tuple-element.40.weighted, ...), custom_call_target="tpu_custom_call" | custom-call | flops 655360 | bytes 262144 | tf_op jit(solution)/shard_map/shade/pallas_call | solution.py:307
  15.0 0.5 %collective-permute-done.10.rest_1_ = f32[1,4,8,512]{3,2,1,0:T(8,128)S(1)} collective-permute-done((f32[1,4,8,512]{3,2,1,0:T(8,128)S(1)}, f32[1,4,8,512]{3,2,1,0:T(8,128)S(1)}, u32[]{:S(2)}, u32[]{:S(2)}) %collective-permute-start.10) | collective-permute-done | bytes 65568 | tf_op jit(solution)/shard_map/ppermute | solution.py:301
  15.5 0.7 %last_merge.1 = f32[4,16,512]{2,1,0:T(8,128)} custom-call(f32[1,8,8,512]{3,2,1,0:T(8,128)S(1)} %first_merge.5.kept, f32[1,4,8,512]{3,2,1,0:T(8,128)S(1)} %collective-permute-done.4.rest_0_, f32[1,4,8,512]{3,2,1,0:T(8,128)S(1)} %collective-permute-done.10.rest_1_), custom_call_target="tpu_custom_call" | custom-call | tf_op jit(solution)/shard_map/last_merge/pallas_call | solution.py:246
  (10 shorter events, 0.1 us)
Async XLA Ops:
  1.3 7.0 %collective-permute-start = (f32[16,2048]{1,0:T(8,128)S(1)}, f32[16,2048]{1,0:T(8,128)S(1)}, u32[]{:S(2)}, u32[]{:S(2)}) collective-permute-start(f32[16,2048]{1,0:T(8,128)S(1)} %get-tuple-element.26), channel_id=1, source_target_pairs={{0,8},{1,9},{2,10},{3,11},{4,12},{5,13},{6,14},{7,15},{8,0},{9,1},... | collective-permute-start | bytes 393224 | tf_op jit(solution)/shard_map/ppermute | solution.py:89
  1.8 6.5 %collective-permute-start.1 = (f32[16,2048]{1,0:T(8,128)S(1)}, f32[16,2048]{1,0:T(8,128)S(1)}, u32[]{:S(2)}, u32[]{:S(2)}) collective-permute-start(f32[16,2048]{1,0:T(8,128)S(1)} %get-tuple-element.27), channel_id=1, source_target_pairs={{0,1},{1,0},{2,3},{3,2},{4,5},{5,4},{6,7},{7,6},{8,16},{9,17},{10,... | collective-permute-start | bytes 393224 | tf_op jit(solution)/shard_map/ppermute | solution.py:89
  4.3 3.9 %collective-permute-start.2 = (f32[4,2048]{1,0:T(4,128)S(1)}, f32[4,2048]{1,0:T(4,128)S(1)}, u32[]{:S(2)}, u32[]{:S(2)}) collective-permute-start(f32[4,2048]{1,0:T(4,128)S(1)} %get-tuple-element.32), channel_id=1, source_target_pairs={{0,1},{1,0},{2,3},{3,2},{4,5},{5,4},{6,7},{7,6},{8,9},{9,8},{10,11... | collective-permute-start | bytes 98312 | tf_op jit(solution)/shard_map/ppermute | solution.py:89
  4.4 4.3 %collective-permute-start.5 = (f32[4,2048]{1,0:T(4,128)S(1)}, f32[4,2048]{1,0:T(4,128)S(1)}, u32[]{:S(2)}, u32[]{:S(2)}) collective-permute-start(f32[4,2048]{1,0:T(4,128)S(1)} %get-tuple-element.35), channel_id=1, source_target_pairs={{0,8},{1,2},{2,1},{3,4},{4,3},{5,6},{6,5},{7,15},{8,0},{9,10},{10,... | collective-permute-start | bytes 98312 | tf_op jit(solution)/shard_map/ppermute | solution.py:89
  8.4 1.3 %collective-permute-start.3 = (f32[1,4,8,512]{3,2,1,0:T(8,128)S(1)}, f32[1,4,8,512]{3,2,1,0:T(8,128)S(1)}, u32[]{:S(2)}, u32[]{:S(2)}) collective-permute-start(f32[1,4,8,512]{3,2,1,0:T(8,128)S(1)} %shade.6), channel_id=1, source_target_pairs={{0,8},{8,0},{16,24},{24,16},{1,9},{9,1},{17,25},{25,17},{2,10},{10... | collective-permute-start | bytes 196616 | tf_op jit(solution)/shard_map/ppermute | solution.py:301
  8.9 1.8 %collective-permute-start.6 = (f32[1,4,8,512]{3,2,1,0:T(8,128)S(1)}, f32[1,4,8,512]{3,2,1,0:T(8,128)S(1)}, u32[]{:S(2)}, u32[]{:S(2)}) collective-permute-start(f32[1,4,8,512]{3,2,1,0:T(8,128)S(1)} %shade.8), channel_id=1, source_target_pairs={{0,8},{8,0},{16,24},{24,16},{1,9},{9,1},{17,25},{25,17},{2,10},{10... | collective-permute-start | bytes 196616 | tf_op jit(solution)/shard_map/ppermute | solution.py:301
  9.8 5.0 %collective-permute-start.4 = (f32[1,4,8,512]{3,2,1,0:T(8,128)S(1)}, f32[1,4,8,512]{3,2,1,0:T(8,128)S(1)}, u32[]{:S(2)}, u32[]{:S(2)}) collective-permute-start(f32[1,4,8,512]{3,2,1,0:T(8,128)S(1)} %first_merge.3), channel_id=1, source_target_pairs={{0,16},{8,24},{16,0},{24,8},{1,17},{9,25},{17,1},{25,9},{2,18},{10... | collective-permute-start | bytes 196616 | tf_op jit(solution)/shard_map/ppermute | solution.py:301
  10.7 4.8 %collective-permute-start.10 = (f32[1,4,8,512]{3,2,1,0:T(8,128)S(1)}, f32[1,4,8,512]{3,2,1,0:T(8,128)S(1)}, u32[]{:S(2)}, u32[]{:S(2)}) collective-permute-start(f32[1,4,8,512]{3,2,1,0:T(8,128)S(1)} %first_merge.4), channel_id=1, source_target_pairs={{0,16},{8,24},{16,0},{24,8},{1,17},{9,25},{17,1},{25,9},{2,18},{10... | collective-permute-start | bytes 196616 | tf_op jit(solution)/shard_map/ppermute | solution.py:301
  12.4 2.6 %collective-permute-start.7 = (f32[1,3,8,512]{3,2,1,0:T(8,128)S(1)}, f32[1,3,8,512]{3,2,1,0:T(8,128)S(1)}, u32[]{:S(2)}, u32[]{:S(2)}) collective-permute-start(f32[1,3,8,512]{3,2,1,0:T(8,128)S(1)} %get-tuple-element.41), channel_id=1, source_target_pairs={{0,8},{8,0},{16,24},{24,16},{1,9},{9,1},{17,25},{25,17},{2,10},{10... | collective-permute-start | bytes 147464 | tf_op jit(solution)/shard_map/ppermute | solution.py:301
  12.4 2.5 %collective-permute-start.8 = (f32[1,3,8,512]{3,2,1,0:T(8,128)S(1)}, f32[1,3,8,512]{3,2,1,0:T(8,128)S(1)}, u32[]{:S(2)}, u32[]{:S(2)}) collective-permute-start(f32[1,3,8,512]{3,2,1,0:T(8,128)S(1)} %get-tuple-element.42), channel_id=1, source_target_pairs={{0,8},{8,0},{16,24},{24,16},{1,9},{9,1},{17,25},{25,17},{2,10},{10... | collective-permute-start | bytes 147464 | tf_op jit(solution)/shard_map/ppermute | solution.py:301
  12.9 2.0 %collective-permute-start.9 = (f32[1,2,8,512]{3,2,1,0:T(8,128)S(1)}, f32[1,2,8,512]{3,2,1,0:T(8,128)S(1)}, u32[]{:S(2)}, u32[]{:S(2)}) collective-permute-start(f32[1,2,8,512]{3,2,1,0:T(8,128)S(1)} %get-tuple-element.43), channel_id=1, source_target_pairs={{0,8},{8,0},{16,24},{24,16},{1,9},{9,1},{17,25},{25,17},{2,10},{10... | collective-permute-start | bytes 98312 | tf_op jit(solution)/shard_map/ppermute | solution.py:301

commit v10 on v9

--- a/solution.py
+++ b/solution.py
@@ -38,24 +38,13 @@
     return jax.ShapeDtypeStruct(shape, jnp.float32)
 
 
-def load_kernel(
-    density_in, bins_in, colors_in, opacities_in,
-    density, bins, depth_even, depth_odd, row_even, row_odd, tables,
-    colors, opacities, done,
-):
+def load_kernel(density_in, density, depth_even, depth_odd, row_even, row_odd, done):
+    copy = pltpu.make_async_copy(density_in, density, done)
+    copy.start()
     slices, rows, _ = density.shape
-    moves = [
-        (density_in, density),
-        (bins_in, bins),
-        (colors_in, colors),
-        (opacities_in, opacities),
-    ]
-    copies = [pltpu.make_async_copy(a, b, done.at[i]) for i, (a, b) in enumerate(moves)]
-    for copy in copies:
-        copy.start()
     depth_low = lax.axis_index("depth") & 1 == 0
     tile_low = lax.axis_index("tile") & 1 == 0
-    copies[0].wait()
+    copy.wait()
     first, last = density[0], density[slices - 1]
     depth_even[...] = jnp.where(depth_low, last, first)
     depth_odd[...] = jnp.where(depth_low, first, last)
@@ -63,15 +52,6 @@
         top, bottom = density[k, 0:1], density[k, rows - 1 : rows]
         row_even[k : k + 1] = jnp.where(tile_low, bottom, top)
         row_odd[k : k + 1] = jnp.where(tile_low, top, bottom)
-    for copy in copies[1:]:
-        copy.wait()
-    color = whole_number(colors[...], COLOR_ONE)
-    opacity = whole_number(opacities[...].reshape(1, -1), OPACITY_ONE)
-    words = [color[0:1] | (color[1:2] << 16), color[2:3] | (opacity << 16)]
-    for part in range(tables.shape[0]):
-        for j in range(2):
-            table = words[j][:, part * LANES : (part + 1) * LANES]
-            tables[part, j] = jnp.broadcast_to(table, (SUBLANES, LANES))
 
 
 def trade(x, axis, first):
@@ -93,10 +73,28 @@
     return (x.astype(jnp.float32) * one).astype(jnp.int32)
 
 
-def weights_kernel(count, bins, tables, weighted, passed):
+def weights_kernel(
+    count, bins_in, colors_in, opacities_in, weighted, passed, bins, colors, opacities, done
+):
+    moves = [(colors_in, colors), (opacities_in, opacities), (bins_in, bins)]
+    copies = [pltpu.make_async_copy(a, b, done.at[i]) for i, (a, b) in enumerate(moves)]
+    for copy in copies:
+        copy.start()
     slices, rows, cols = bins.shape
-    parts = tables.shape[0]
-    table = [[tables[part, j] for j in range(2)] for part in range(parts)]
+    parts = colors.shape[1] // LANES
+    copies[0].wait()
+    copies[1].wait()
+    color = whole_number(colors[...], COLOR_ONE)
+    opacity = whole_number(opacities[...].reshape(1, -1), OPACITY_ONE)
+    words = [color[0:1] | (color[1:2] << 16), color[2:3] | (opacity << 16)]
+    table = [
+        [
+            jnp.broadcast_to(word[:, part * LANES : (part + 1) * LANES], (SUBLANES, LANES))
+            for word in words
+        ]
+        for part in range(parts)
+    ]
+    copies[2].wait()
     occupied = count[0, 0]
     unit = [flag(k < occupied) * (1.0 / OPACITY_ONE) for k in range(slices)]
     for r in range(0, rows, SUBLANES):
@@ -258,29 +256,22 @@
     slab_count = lax.axis_size("depth")
     half, piece = slab_count // 2, cols // slab_count
     pixels = rows * cols
-    parts = opacities.shape[0] // LANES
     here = pl.BlockSpec(memory_space=pltpu.HBM)
-    density, bins, *faces, tables = pl.pallas_call(
+    density, *faces = pl.pallas_call(
         load_kernel,
         out_shape=[
             f32(*density.shape),
-            jax.ShapeDtypeStruct(bins.shape, jnp.int32),
             f32(rows, cols),
             f32(rows, cols),
             f32(slices, cols),
             f32(slices, cols),
-            jax.ShapeDtypeStruct((parts, 2, SUBLANES, LANES), jnp.int32),
         ],
-        in_specs=[here] * 4,
-        out_specs=[vmem()] * 7,
-        scratch_shapes=[
-            pltpu.VMEM(colors.shape, colors.dtype),
-            pltpu.VMEM(opacities.shape, opacities.dtype),
-            pltpu.SemaphoreType.DMA((4,)),
-        ],
+        in_specs=[here],
+        out_specs=[vmem()] * 5,
+        scratch_shapes=[pltpu.SemaphoreType.DMA],
         compiler_params=params(),
         name="load",
-    )(*(stay(x) for x in (density, bins, colors, opacities)))
+    )(stay(density))
     traded = [
         trade(faces[0], "depth", 0),
         trade(faces[1], "depth", 1),
@@ -290,12 +281,18 @@
     weighted, passed = pl.pallas_call(
         weights_kernel,
         out_shape=[f32(3, slices, rows, cols), f32(rows, cols)],
-        in_specs=[smem(), vmem(), vmem()],
+        in_specs=[smem()] + [here] * 3,
         out_specs=[vmem()] * 2,
+        scratch_shapes=[
+            pltpu.VMEM(bins.shape, jnp.int32),
+            pltpu.VMEM(colors.shape, colors.dtype),
+            pltpu.VMEM(opacities.shape, opacities.dtype),
+            pltpu.SemaphoreType.DMA((3,)),
+        ],
         compiler_params=params(),
         cost_estimate=cost(64 * slices * pixels, 16 * slices * pixels),
         name="weights",
-    )(counts, bins, tables)
+    )(counts, stay(bins), stay(colors), stay(opacities))
 
     def swap(x, level):
         return lax.ppermute(x, "depth", [(i, i ^ 1 << level) for i in range(slab_count)])

time: 16.3 us -> 16.5 us (1.012)
  Pallas kernels: 4.12 us -> 5.06 us
  waiting for transfers between devices: 3.44 us -> 2.56 us
    pallas_call x1, Pallas kernels: 1.02 us -> 2.13 us  [on_device(): pl.pallas_call(weights_kernel, out_shape=[f32(3, slices, rows, cols), f32...]
    ppermute x4, waiting for transfers between devices: 0.89 us -> 0.01 us  [trade(): return lax.ppermute(x, ('depth', 'tile'), pairs)]
    pallas_call x1, Pallas kernels: 1.25 us -> 1.08 us  [on_device(): pl.pallas_call(load_kernel, out_shape=[f32(*density.shape), f32(rows, col...]
  transfers between devices with their start and end apart: 11 -> 11, of which waited for: 4 -> 3; matrix products, arithmetic and copies ran while one was open for 0% -> 0% of each run, Pallas kernels for 14% -> 20%
where the time goes in v10:
time: 16.5 us; the launch traced here: 16.3 us
  starting transfers between devices  7.86 us (48%)
  Pallas kernels  5.06 us (31%)
  waiting for transfers between devices  2.56 us (16%)
  between operations  0.79 us (5%)
    ppermute x4, starting transfers between devices, trade(): return lax.ppermute(x, ('depth', 'tile'), pairs)  4.44 us
    ppermute x7, starting transfers between devices, swap(): lax.ppermute(x, 'depth', [(i, i ^ 1 << level) for i in range(slab_count)])  3.42 us
    ppermute x7, waiting for transfers between devices, swap(): lax.ppermute(x, 'depth', [(i, i ^ 1 << level) for i in range(slab_count)])  2.55 us
    pallas_call x1, Pallas kernels, on_device(): pl.pallas_call(weights_kernel, out_shape=[f32(3, slices, rows, cols), f32...  2.13 us
    pallas_call x6, Pallas kernels, shaded(): pl.pallas_call(functools.partial(shade_kernel, stays, bands), out_shape=[...  1.11 us
    pallas_call x1, Pallas kernels, on_device(): pl.pallas_call(load_kernel, out_shape=[f32(*density.shape), f32(rows, col...  1.08 us
    pallas_call x4, Pallas kernels, call(): pl.pallas_call(kernel, out_shape=out_shape, in_specs=[vmem()] * len(args)...  0.75 us
  transfers between devices with their start and end apart: 11, of which 3 were waited for; matrix products, arithmetic and copies ran while one was open for 0% of the time, Pallas kernels for 20%

profile of v10, /device:TPU:0, one launch (start us, length us, event | category | flops | bytes accessed | tf_op | source)
XLA Modules:
  0.0 16.3 jit_solution(7115158780614222826)
XLA Ops:
  0.0 1.1 %load.1 = (f32[4,16,2048]{2,1,0:T(8,128)S(1)}, f32[16,2048]{1,0:T(8,128)S(1)}, f32[16,2048]{1,0:T(8,128)S(1)}, f32[4,2048]{1,0:T(4,128)S(1)}, f32[4,2048]{1,0:T(4,128)S(1)}) custom-call(f32[4,16,2048]{2,1,0:T(8,128)} %density_in.1), custom_call_target="tpu_custom_call" | custom-call | tf_op jit(solution)/shard_map/load/pallas_call | solution.py:260
  1.1 0.5 %collective-permute-start = (f32[16,2048]{1,0:T(8,128)S(1)}, f32[16,2048]{1,0:T(8,128)S(1)}, u32[]{:S(2)}, u32[]{:S(2)}) collective-permute-start(f32[16,2048]{1,0:T(8,128)S(1)} %get-tuple-element.24), channel_id=1, source_target_pairs={{0,8},{1,9},{2,10},{3,11},{4,12},{5,13},{6,14},{7,15},{8,0},{9,1},... | collective-permute-start | bytes 393224 | tf_op jit(solution)/shard_map/ppermute | solution.py:69
  1.6 2.6 %collective-permute-start.1 = (f32[16,2048]{1,0:T(8,128)S(1)}, f32[16,2048]{1,0:T(8,128)S(1)}, u32[]{:S(2)}, u32[]{:S(2)}) collective-permute-start(f32[16,2048]{1,0:T(8,128)S(1)} %get-tuple-element.25), channel_id=1, source_target_pairs={{0,1},{1,0},{2,3},{3,2},{4,5},{5,4},{6,7},{7,6},{8,16},{9,17},{10,... | collective-permute-start | bytes 393224 | tf_op jit(solution)/shard_map/ppermute | solution.py:69
  4.2 0.1 collective-permute-start.2
  4.2 1.3 %collective-permute-start.5 = (f32[4,2048]{1,0:T(4,128)S(1)}, f32[4,2048]{1,0:T(4,128)S(1)}, u32[]{:S(2)}, u32[]{:S(2)}) collective-permute-start(f32[4,2048]{1,0:T(4,128)S(1)} %get-tuple-element.31), channel_id=1, source_target_pairs={{0,8},{1,2},{2,1},{3,4},{4,3},{5,6},{6,5},{7,15},{8,0},{9,10},{10,... | collective-permute-start | bytes 98312 | tf_op jit(solution)/shard_map/ppermute | solution.py:69
  6.2 2.1 %weights.1 = (f32[3,4,16,2048]{3,2,1,0:T(8,128)S(1)}, f32[16,2048]{1,0:T(8,128)S(1)}) custom-call(s32[1,1]{1,0:T(1,128)S(6)} %copy.6.count, s32[4,16,2048]{2,1,0:T(8,128)} %bins_in.1, bf16[3,256]{1,0:T(4,128)(2,1)} %colors_in.1, bf16[256]{0:T(256)(128)(2,1)} %opacities_in.1), custom_call_target="tpu_custom_call" | custom-call | flops 8388608 | bytes 2097152 | tf_op jit(solution)/shard_map/weights/pallas_call | solution.py:281
  8.3 0.0 collective-permute-done.2.rest_0_
  8.3 0.2 %shade.6 = f32[1,4,8,512]{3,2,1,0:T(8,128)S(1)} custom-call(f32[4,16,2048]{2,1,0:T(8,128)S(1)} %get-tuple-element.23.density, f32[16,2048]{1,0:T(8,128)S(1)} %collective-permute-done.depth_even, f32[16,2048]{1,0:T(8,128)S(1)} %collective-permute-done.1.depth_odd, f32[3,4,16,2048]{3,2,1,0:T(8,128)S(1)} %get-tuple-element.36.weighted, ...), custom_call_target="tpu_custom_call" | custom-call | flops 655360 | bytes 262144 | tf_op jit(solution)/shard_map/shade/pallas_call | solution.py:304
  8.5 0.1 collective-permute-start.3
  8.6 0.2 %shade.7.kept = f32[1,4,8,512]{3,2,1,0:T(8,128)S(1)} custom-call(f32[4,16,2048]{2,1,0:T(8,128)S(1)} %get-tuple-element.23.density, f32[16,2048]{1,0:T(8,128)S(1)} %collective-permute-done.depth_even, f32[16,2048]{1,0:T(8,128)S(1)} %collective-permute-done.1.depth_odd, f32[3,4,16,2048]{3,2,1,0:T(8,128)S(1)} %get-tuple-element.36.weighted, ...), custom_call_target="tpu_custom_call" | custom-call | flops 655360 | bytes 262144 | tf_op jit(solution)/shard_map/shade/pallas_call | solution.py:304
  8.8 0.2 %shade.8 = f32[1,4,8,512]{3,2,1,0:T(8,128)S(1)} custom-call(f32[4,16,2048]{2,1,0:T(8,128)S(1)} %get-tuple-element.23.density, f32[16,2048]{1,0:T(8,128)S(1)} %collective-permute-done.depth_even, f32[16,2048]{1,0:T(8,128)S(1)} %collective-permute-done.1.depth_odd, f32[3,4,16,2048]{3,2,1,0:T(8,128)S(1)} %get-tuple-element.36.weighted, ...), custom_call_target="tpu_custom_call" | custom-call | flops 655360 | bytes 262144 | tf_op jit(solution)/shard_map/shade/pallas_call | solution.py:304
  9.0 0.5 %collective-permute-start.6 = (f32[1,4,8,512]{3,2,1,0:T(8,128)S(1)}, f32[1,4,8,512]{3,2,1,0:T(8,128)S(1)}, u32[]{:S(2)}, u32[]{:S(2)}) collective-permute-start(f32[1,4,8,512]{3,2,1,0:T(8,128)S(1)} %shade.8), channel_id=1, source_target_pairs={{0,8},{8,0},{16,24},{24,16},{1,9},{9,1},{17,25},{25,17},{2,10},{10... | collective-permute-start | bytes 196616 | tf_op jit(solution)/shard_map/ppermute | solution.py:298
  9.5 0.3 %collective-permute-done.3.rest_0_ = f32[1,4,8,512]{3,2,1,0:T(8,128)S(1)} collective-permute-done((f32[1,4,8,512]{3,2,1,0:T(8,128)S(1)}, f32[1,4,8,512]{3,2,1,0:T(8,128)S(1)}, u32[]{:S(2)}, u32[]{:S(2)}) %collective-permute-start.3) | collective-permute-done | bytes 65568 | tf_op jit(solution)/shard_map/ppermute | solution.py:298
  9.9 0.9 %collective-permute-start.4 = (f32[1,4,8,512]{3,2,1,0:T(8,128)S(1)}, f32[1,4,8,512]{3,2,1,0:T(8,128)S(1)}, u32[]{:S(2)}, u32[]{:S(2)}) collective-permute-start(f32[1,4,8,512]{3,2,1,0:T(8,128)S(1)} %first_merge.3), channel_id=1, source_target_pairs={{0,16},{8,24},{16,0},{24,8},{1,17},{9,25},{17,1},{25,9},{2,18},{10... | collective-permute-start | bytes 196616 | tf_op jit(solution)/shard_map/ppermute | solution.py:298
  10.8 0.2 shade.9.kept
  11.0 1.2 %collective-permute-start.10 = (f32[1,4,8,512]{3,2,1,0:T(8,128)S(1)}, f32[1,4,8,512]{3,2,1,0:T(8,128)S(1)}, u32[]{:S(2)}, u32[]{:S(2)}) collective-permute-start(f32[1,4,8,512]{3,2,1,0:T(8,128)S(1)} %first_merge.4), channel_id=1, source_target_pairs={{0,16},{8,24},{16,0},{24,8},{1,17},{9,25},{17,1},{25,9},{2,18},{10... | collective-permute-start | bytes 196616 | tf_op jit(solution)/shard_map/ppermute | solution.py:298
  12.2 0.2 %shade.11 = (f32[1,3,8,512]{3,2,1,0:T(8,128)S(1)}, f32[1,3,8,512]{3,2,1,0:T(8,128)S(1)}, f32[1,2,8,512]{3,2,1,0:T(8,128)S(1)}) custom-call(f32[4,16,2048]{2,1,0:T(8,128)S(1)} %get-tuple-element.23.density, f32[16,2048]{1,0:T(8,128)S(1)} %collective-permute-done.depth_even, f32[16,2048]{1,0:T(8,128)S(1)} %collective-permute-done.1.depth_odd, ...), custom_call_target="tpu_custom_call" | custom-call | flops 655360 | bytes 262144 | tf_op jit(solution)/shard_map/shade/pallas_call | solution.py:304
  12.4 0.1 collective-permute-start.7
  12.5 0.5 %collective-permute-start.8 = (f32[1,3,8,512]{3,2,1,0:T(8,128)S(1)}, f32[1,3,8,512]{3,2,1,0:T(8,128)S(1)}, u32[]{:S(2)}, u32[]{:S(2)}) collective-permute-start(f32[1,3,8,512]{3,2,1,0:T(8,128)S(1)} %get-tuple-element.38), channel_id=1, source_target_pairs={{0,8},{8,0},{16,24},{24,16},{1,9},{9,1},{17,25},{25,17},{2,10},{10... | collective-permute-start | bytes 147464 | tf_op jit(solution)/shard_map/ppermute | solution.py:298
  13.0 0.1 collective-permute-start.9
  13.1 1.6 %collective-permute-done.4.rest_0_ = f32[1,4,8,512]{3,2,1,0:T(8,128)S(1)} collective-permute-done((f32[1,4,8,512]{3,2,1,0:T(8,128)S(1)}, f32[1,4,8,512]{3,2,1,0:T(8,128)S(1)}, u32[]{:S(2)}, u32[]{:S(2)}) %collective-permute-start.4) | collective-permute-done | bytes 65568 | tf_op jit(solution)/shard_map/ppermute | solution.py:298
  14.7 0.2 %shade.10.kept = f32[1,8,8,512]{3,2,1,0:T(8,128)S(1)} custom-call(f32[4,16,2048]{2,1,0:T(8,128)S(1)} %get-tuple-element.23.density, f32[16,2048]{1,0:T(8,128)S(1)} %collective-permute-done.depth_even, f32[16,2048]{1,0:T(8,128)S(1)} %collective-permute-done.1.depth_odd, f32[3,4,16,2048]{3,2,1,0:T(8,128)S(1)} %get-tuple-element.36.weighted, ...), custom_call_target="tpu_custom_call" | custom-call | flops 655360 | bytes 262144 | tf_op jit(solution)/shard_map/shade/pallas_call | solution.py:304
  15.0 0.6 %collective-permute-done.10.rest_1_ = f32[1,4,8,512]{3,2,1,0:T(8,128)S(1)} collective-permute-done((f32[1,4,8,512]{3,2,1,0:T(8,128)S(1)}, f32[1,4,8,512]{3,2,1,0:T(8,128)S(1)}, u32[]{:S(2)}, u32[]{:S(2)}) %collective-permute-start.10) | collective-permute-done | bytes 65568 | tf_op jit(solution)/shard_map/ppermute | solution.py:298
  15.6 0.7 %last_merge.1 = f32[4,16,512]{2,1,0:T(8,128)} custom-call(f32[1,8,8,512]{3,2,1,0:T(8,128)S(1)} %first_merge.5.kept, f32[1,4,8,512]{3,2,1,0:T(8,128)S(1)} %collective-permute-done.4.rest_0_, f32[1,4,8,512]{3,2,1,0:T(8,128)S(1)} %collective-permute-done.10.rest_1_), custom_call_target="tpu_custom_call" | custom-call | tf_op jit(solution)/shard_map/last_merge/pallas_call | solution.py:244
  (10 shorter events, 0.1 us)
Async XLA Ops:
  1.1 7.2 %collective-permute-start = (f32[16,2048]{1,0:T(8,128)S(1)}, f32[16,2048]{1,0:T(8,128)S(1)}, u32[]{:S(2)}, u32[]{:S(2)}) collective-permute-start(f32[16,2048]{1,0:T(8,128)S(1)} %get-tuple-element.24), channel_id=1, source_target_pairs={{0,8},{1,9},{2,10},{3,11},{4,12},{5,13},{6,14},{7,15},{8,0},{9,1},... | collective-permute-start | bytes 393224 | tf_op jit(solution)/shard_map/ppermute | solution.py:69
  1.6 6.7 %collective-permute-start.1 = (f32[16,2048]{1,0:T(8,128)S(1)}, f32[16,2048]{1,0:T(8,128)S(1)}, u32[]{:S(2)}, u32[]{:S(2)}) collective-permute-start(f32[16,2048]{1,0:T(8,128)S(1)} %get-tuple-element.25), channel_id=1, source_target_pairs={{0,1},{1,0},{2,3},{3,2},{4,5},{5,4},{6,7},{7,6},{8,16},{9,17},{10,... | collective-permute-start | bytes 393224 | tf_op jit(solution)/shard_map/ppermute | solution.py:69
  4.2 4.1 %collective-permute-start.2 = (f32[4,2048]{1,0:T(4,128)S(1)}, f32[4,2048]{1,0:T(4,128)S(1)}, u32[]{:S(2)}, u32[]{:S(2)}) collective-permute-start(f32[4,2048]{1,0:T(4,128)S(1)} %get-tuple-element.28), channel_id=1, source_target_pairs={{0,1},{1,0},{2,3},{3,2},{4,5},{5,4},{6,7},{7,6},{8,9},{9,8},{10,11... | collective-permute-start | bytes 98312 | tf_op jit(solution)/shard_map/ppermute | solution.py:69
  4.2 4.5 %collective-permute-start.5 = (f32[4,2048]{1,0:T(4,128)S(1)}, f32[4,2048]{1,0:T(4,128)S(1)}, u32[]{:S(2)}, u32[]{:S(2)}) collective-permute-start(f32[4,2048]{1,0:T(4,128)S(1)} %get-tuple-element.31), channel_id=1, source_target_pairs={{0,8},{1,2},{2,1},{3,4},{4,3},{5,6},{6,5},{7,15},{8,0},{9,10},{10,... | collective-permute-start | bytes 98312 | tf_op jit(solution)/shard_map/ppermute | solution.py:69
  8.5 1.3 %collective-permute-start.3 = (f32[1,4,8,512]{3,2,1,0:T(8,128)S(1)}, f32[1,4,8,512]{3,2,1,0:T(8,128)S(1)}, u32[]{:S(2)}, u32[]{:S(2)}) collective-permute-start(f32[1,4,8,512]{3,2,1,0:T(8,128)S(1)} %shade.6), channel_id=1, source_target_pairs={{0,8},{8,0},{16,24},{24,16},{1,9},{9,1},{17,25},{25,17},{2,10},{10... | collective-permute-start | bytes 196616 | tf_op jit(solution)/shard_map/ppermute | solution.py:298
  9.0 2.0 %collective-permute-start.6 = (f32[1,4,8,512]{3,2,1,0:T(8,128)S(1)}, f32[1,4,8,512]{3,2,1,0:T(8,128)S(1)}, u32[]{:S(2)}, u32[]{:S(2)}) collective-permute-start(f32[1,4,8,512]{3,2,1,0:T(8,128)S(1)} %shade.8), channel_id=1, source_target_pairs={{0,8},{8,0},{16,24},{24,16},{1,9},{9,1},{17,25},{25,17},{2,10},{10... | collective-permute-start | bytes 196616 | tf_op jit(solution)/shard_map/ppermute | solution.py:298
  9.9 4.8 %collective-permute-start.4 = (f32[1,4,8,512]{3,2,1,0:T(8,128)S(1)}, f32[1,4,8,512]{3,2,1,0:T(8,128)S(1)}, u32[]{:S(2)}, u32[]{:S(2)}) collective-permute-start(f32[1,4,8,512]{3,2,1,0:T(8,128)S(1)} %first_merge.3), channel_id=1, source_target_pairs={{0,16},{8,24},{16,0},{24,8},{1,17},{9,25},{17,1},{25,9},{2,18},{10... | collective-permute-start | bytes 196616 | tf_op jit(solution)/shard_map/ppermute | solution.py:298
  11.0 4.6 %collective-permute-start.10 = (f32[1,4,8,512]{3,2,1,0:T(8,128)S(1)}, f32[1,4,8,512]{3,2,1,0:T(8,128)S(1)}, u32[]{:S(2)}, u32[]{:S(2)}) collective-permute-start(f32[1,4,8,512]{3,2,1,0:T(8,128)S(1)} %first_merge.4), channel_id=1, source_target_pairs={{0,16},{8,24},{16,0},{24,8},{1,17},{9,25},{17,1},{25,9},{2,18},{10... | collective-permute-start | bytes 196616 | tf_op jit(solution)/shard_map/ppermute | solution.py:298
  12.4 2.5 %collective-permute-start.7 = (f32[1,3,8,512]{3,2,1,0:T(8,128)S(1)}, f32[1,3,8,512]{3,2,1,0:T(8,128)S(1)}, u32[]{:S(2)}, u32[]{:S(2)}) collective-permute-start(f32[1,3,8,512]{3,2,1,0:T(8,128)S(1)} %get-tuple-element.37), channel_id=1, source_target_pairs={{0,8},{8,0},{16,24},{24,16},{1,9},{9,1},{17,25},{25,17},{2,10},{10... | collective-permute-start | bytes 147464 | tf_op jit(solution)/shard_map/ppermute | solution.py:298
  12.5 2.4 %collective-permute-start.8 = (f32[1,3,8,512]{3,2,1,0:T(8,128)S(1)}, f32[1,3,8,512]{3,2,1,0:T(8,128)S(1)}, u32[]{:S(2)}, u32[]{:S(2)}) collective-permute-start(f32[1,3,8,512]{3,2,1,0:T(8,128)S(1)} %get-tuple-element.38), channel_id=1, source_target_pairs={{0,8},{8,0},{16,24},{24,16},{1,9},{9,1},{17,25},{25,17},{2,10},{10... | collective-permute-start | bytes 147464 | tf_op jit(solution)/shard_map/ppermute | solution.py:298
  13.0 1.9 %collective-permute-start.9 = (f32[1,2,8,512]{3,2,1,0:T(8,128)S(1)}, f32[1,2,8,512]{3,2,1,0:T(8,128)S(1)}, u32[]{:S(2)}, u32[]{:S(2)}) collective-permute-start(f32[1,2,8,512]{3,2,1,0:T(8,128)S(1)} %get-tuple-element.39), channel_id=1, source_target_pairs={{0,8},{8,0},{16,24},{24,16},{1,9},{9,1},{17,25},{25,17},{2,10},{10... | collective-permute-start | bytes 98312 | tf_op jit(solution)/shard_map/ppermute | solution.py:298

commit v11 on v9

--- a/solution.py
+++ b/solution.py
@@ -138,7 +138,7 @@
     return tile_is_low if band == EVEN else 1 - tile_is_low
 
 
-def shade_kernel(stays, bands, density, depth_even, depth_odd, weighted, passed, *rest):
+def shade_kernel(stays, bands, density, depth_odd, depth_even, weighted, passed, *rest):
     trades, images = rest[: len(bands)], rest[len(bands) :]
     slices, rows, cols = density.shape
     pieces, _, _, piece = images[0].shape
@@ -312,7 +312,7 @@
             compiler_params=params(),
             cost_estimate=cost(5 * slices * pixels, 2 * slices * pixels),
             name="shade",
-        )(density, *faces, weighted, passed, *(rows_of[band] for band in bands))
+        )(density, *faces[::-1], weighted, passed, *(rows_of[band] for band in bands))
 
     levels = slab_count.bit_length() - 1
     bands = (EVEN, ODD)

time: 16.3 us -> 16.4 us (level)
  starting transfers between devices: 7.86 us -> 8.06 us
    ppermute x4, starting transfers between devices: 4.44 us -> 4.64 us  [trade(): return lax.ppermute(x, ('depth', 'tile'), pairs)]
  transfers between devices with their start and end apart: 11 -> 11, of which waited for: 4 -> 4; matrix products, arithmetic and copies ran while one was open for 0% -> 0% of each run, Pallas kernels for 14% -> 13%
where the time goes in v11:
time: 16.4 us; the launch traced here: 16.3 us
  starting transfers between devices  8.06 us (49%)
  Pallas kernels  4.12 us (25%)
  waiting for transfers between devices  3.31 us (20%)
  between operations  0.77 us (5%)
    ppermute x4, starting transfers between devices, trade(): return lax.ppermute(x, ('depth', 'tile'), pairs)  4.64 us
    ppermute x7, starting transfers between devices, swap(): lax.ppermute(x, 'depth', [(i, i ^ 1 << level) for i in range(slab_count)])  3.42 us
    ppermute x7, waiting for transfers between devices, swap(): lax.ppermute(x, 'depth', [(i, i ^ 1 << level) for i in range(slab_count)])  2.55 us
    pallas_call x1, Pallas kernels, on_device(): pl.pallas_call(load_kernel, out_shape=[f32(*density.shape), jax.ShapeDtyp...  1.25 us
    pallas_call x6, Pallas kernels, shaded(): pl.pallas_call(functools.partial(shade_kernel, stays, bands), out_shape=[...  1.1 us
    pallas_call x1, Pallas kernels, on_device(): pl.pallas_call(weights_kernel, out_shape=[f32(3, slices, rows, cols), f32...  1.02 us
    ppermute x4, waiting for transfers between devices, trade(): return lax.ppermute(x, ('depth', 'tile'), pairs)  0.76 us
    pallas_call x4, Pallas kernels, call(): pl.pallas_call(kernel, out_shape=out_shape, in_specs=[vmem()] * len(args)...  0.75 us
  transfers between devices with their start and end apart: 11, of which 4 were waited for; matrix products, arithmetic and copies ran while one was open for 0% of the time, Pallas kernels for 13%

profile of v11, /device:TPU:0, one launch (start us, length us, event | category | flops | bytes accessed | tf_op | source)
XLA Modules:
  0.0 16.3 jit_solution(14848041196431764073)
XLA Ops:
  0.0 1.3 %load.1 = (f32[4,16,2048]{2,1,0:T(8,128)S(1)}, s32[4,16,2048]{2,1,0:T(8,128)S(1)}, f32[16,2048]{1,0:T(8,128)S(1)}, f32[16,2048]{1,0:T(8,128)S(1)}, f32[4,2048]{1...) custom-call(f32[4,16,2048]{2,1,0:T(8,128)} %density_in.1, s32[4,16,2048]{2,1,0:T(8,128)} %bins_in.1, ...), custom_call_target="tpu_custom_call" | custom-call | tf_op jit(solution)/shard_map/load/pallas_call | solution.py:263
  1.3 3.0 %collective-permute-start = (f32[16,2048]{1,0:T(8,128)S(1)}, f32[16,2048]{1,0:T(8,128)S(1)}, u32[]{:S(2)}, u32[]{:S(2)}) collective-permute-start(f32[16,2048]{1,0:T(8,128)S(1)} %get-tuple-element.26), channel_id=1, source_target_pairs={{0,1},{1,0},{2,3},{3,2},{4,5},{5,4},{6,7},{7,6},{8,16},{9,17},{10,... | collective-permute-start | bytes 393224 | tf_op jit(solution)/shard_map/ppermute | solution.py:89
  4.3 0.1 collective-permute-start.1
  4.4 1.5 %collective-permute-start.2 = (f32[4,2048]{1,0:T(4,128)S(1)}, f32[4,2048]{1,0:T(4,128)S(1)}, u32[]{:S(2)}, u32[]{:S(2)}) collective-permute-start(f32[4,2048]{1,0:T(4,128)S(1)} %get-tuple-element.32), channel_id=1, source_target_pairs={{0,1},{1,0},{2,3},{3,2},{4,5},{5,4},{6,7},{7,6},{8,9},{9,8},{10,11... | collective-permute-start | bytes 98312 | tf_op jit(solution)/shard_map/ppermute | solution.py:89
  6.6 1.0 %weights.1 = (f32[3,4,16,2048]{3,2,1,0:T(8,128)S(1)}, f32[16,2048]{1,0:T(8,128)S(1)}) custom-call(s32[1,1]{1,0:T(1,128)S(6)} %copy.6.count, s32[4,16,2048]{2,1,0:T(8,128)S(1)} %get-tuple-element.28.bins, s32[2,2,8,128]{3,2,1,0:T(8,128)S(1)} %get-tuple-element.29.tables), custom_call_target="tpu_custom_call" | custom-call | flops 8388608 | bytes 2097152 | tf_op jit(solution)/shard_map/weights/pallas_call | solution.py:290
  7.6 0.8 %collective-permute-done.2.rest_0_ = f32[4,2048]{1,0:T(4,128)S(1)} collective-permute-done((f32[4,2048]{1,0:T(4,128)S(1)}, f32[4,2048]{1,0:T(4,128)S(1)}, u32[]{:S(2)}, u32[]{:S(2)}) %collective-permute-start.2) | collective-permute-done | bytes 32800 | tf_op jit(solution)/shard_map/ppermute | solution.py:89
  8.3 0.0 collective-permute-done.depth_odd
  8.3 0.2 shade.6
  8.5 0.1 collective-permute-start.3
  8.6 0.2 %shade.7.kept = f32[1,4,8,512]{3,2,1,0:T(8,128)S(1)} custom-call(f32[4,16,2048]{2,1,0:T(8,128)S(1)} %get-tuple-element.25.density, f32[16,2048]{1,0:T(8,128)S(1)} %collective-permute-done.depth_odd, f32[16,2048]{1,0:T(8,128)S(1)} %collective-permute-done.1.depth_even, f32[3,4,16,2048]{3,2,1,0:T(8,128)S(1)} %get-tuple-element.40.weighted, ...), custom_call_target="tpu_custom_call" | custom-call | flops 655360 | bytes 262144 | tf_op jit(solution)/shard_map/shade/pallas_call | solution.py:307
  8.8 0.2 %shade.8 = f32[1,4,8,512]{3,2,1,0:T(8,128)S(1)} custom-call(f32[4,16,2048]{2,1,0:T(8,128)S(1)} %get-tuple-element.25.density, f32[16,2048]{1,0:T(8,128)S(1)} %collective-permute-done.depth_odd, f32[16,2048]{1,0:T(8,128)S(1)} %collective-permute-done.1.depth_even, f32[3,4,16,2048]{3,2,1,0:T(8,128)S(1)} %get-tuple-element.40.weighted, ...), custom_call_target="tpu_custom_call" | custom-call | flops 655360 | bytes 262144 | tf_op jit(solution)/shard_map/shade/pallas_call | solution.py:307
  8.9 0.5 %collective-permute-start.6 = (f32[1,4,8,512]{3,2,1,0:T(8,128)S(1)}, f32[1,4,8,512]{3,2,1,0:T(8,128)S(1)}, u32[]{:S(2)}, u32[]{:S(2)}) collective-permute-start(f32[1,4,8,512]{3,2,1,0:T(8,128)S(1)} %shade.8), channel_id=1, source_target_pairs={{0,8},{8,0},{16,24},{24,16},{1,9},{9,1},{17,25},{25,17},{2,10},{10... | collective-permute-start | bytes 196616 | tf_op jit(solution)/shard_map/ppermute | solution.py:301
  9.5 0.3 %collective-permute-done.3.rest_0_ = f32[1,4,8,512]{3,2,1,0:T(8,128)S(1)} collective-permute-done((f32[1,4,8,512]{3,2,1,0:T(8,128)S(1)}, f32[1,4,8,512]{3,2,1,0:T(8,128)S(1)}, u32[]{:S(2)}, u32[]{:S(2)}) %collective-permute-start.3) | collective-permute-done | bytes 65568 | tf_op jit(solution)/shard_map/ppermute | solution.py:301
  9.8 1.0 %collective-permute-start.4 = (f32[1,4,8,512]{3,2,1,0:T(8,128)S(1)}, f32[1,4,8,512]{3,2,1,0:T(8,128)S(1)}, u32[]{:S(2)}, u32[]{:S(2)}) collective-permute-start(f32[1,4,8,512]{3,2,1,0:T(8,128)S(1)} %first_merge.3), channel_id=1, source_target_pairs={{0,16},{8,24},{16,0},{24,8},{1,17},{9,25},{17,1},{25,9},{2,18},{10... | collective-permute-start | bytes 196616 | tf_op jit(solution)/shard_map/ppermute | solution.py:301
  10.8 0.2 shade.9.kept
  11.0 1.2 %collective-permute-start.10 = (f32[1,4,8,512]{3,2,1,0:T(8,128)S(1)}, f32[1,4,8,512]{3,2,1,0:T(8,128)S(1)}, u32[]{:S(2)}, u32[]{:S(2)}) collective-permute-start(f32[1,4,8,512]{3,2,1,0:T(8,128)S(1)} %first_merge.4), channel_id=1, source_target_pairs={{0,16},{8,24},{16,0},{24,8},{1,17},{9,25},{17,1},{25,9},{2,18},{10... | collective-permute-start | bytes 196616 | tf_op jit(solution)/shard_map/ppermute | solution.py:301
  12.2 0.2 %shade.11 = (f32[1,3,8,512]{3,2,1,0:T(8,128)S(1)}, f32[1,3,8,512]{3,2,1,0:T(8,128)S(1)}, f32[1,2,8,512]{3,2,1,0:T(8,128)S(1)}) custom-call(f32[4,16,2048]{2,1,0:T(8,128)S(1)} %get-tuple-element.25.density, f32[16,2048]{1,0:T(8,128)S(1)} %collective-permute-done.depth_odd, f32[16,2048]{1,0:T(8,128)S(1)} %collective-permute-done.1.depth_even, ...), custom_call_target="tpu_custom_call" | custom-call | flops 655360 | bytes 262144 | tf_op jit(solution)/shard_map/shade/pallas_call | solution.py:307
  12.4 0.1 collective-permute-start.7
  12.5 0.5 %collective-permute-start.8 = (f32[1,3,8,512]{3,2,1,0:T(8,128)S(1)}, f32[1,3,8,512]{3,2,1,0:T(8,128)S(1)}, u32[]{:S(2)}, u32[]{:S(2)}) collective-permute-start(f32[1,3,8,512]{3,2,1,0:T(8,128)S(1)} %get-tuple-element.42), channel_id=1, source_target_pairs={{0,8},{8,0},{16,24},{24,16},{1,9},{9,1},{17,25},{25,17},{2,10},{10... | collective-permute-start | bytes 147464 | tf_op jit(solution)/shard_map/ppermute | solution.py:301
  13.0 0.1 collective-permute-start.9
  13.1 1.7 %collective-permute-done.4.rest_0_ = f32[1,4,8,512]{3,2,1,0:T(8,128)S(1)} collective-permute-done((f32[1,4,8,512]{3,2,1,0:T(8,128)S(1)}, f32[1,4,8,512]{3,2,1,0:T(8,128)S(1)}, u32[]{:S(2)}, u32[]{:S(2)}) %collective-permute-start.4) | collective-permute-done | bytes 65568 | tf_op jit(solution)/shard_map/ppermute | solution.py:301
  14.8 0.2 %shade.10.kept = f32[1,8,8,512]{3,2,1,0:T(8,128)S(1)} custom-call(f32[4,16,2048]{2,1,0:T(8,128)S(1)} %get-tuple-element.25.density, f32[16,2048]{1,0:T(8,128)S(1)} %collective-permute-done.depth_odd, f32[16,2048]{1,0:T(8,128)S(1)} %collective-permute-done.1.depth_even, f32[3,4,16,2048]{3,2,1,0:T(8,128)S(1)} %get-tuple-element.40.weighted, ...), custom_call_target="tpu_custom_call" | custom-call | flops 655360 | bytes 262144 | tf_op jit(solution)/shard_map/shade/pallas_call | solution.py:307
  15.1 0.5 %collective-permute-done.10.rest_1_ = f32[1,4,8,512]{3,2,1,0:T(8,128)S(1)} collective-permute-done((f32[1,4,8,512]{3,2,1,0:T(8,128)S(1)}, f32[1,4,8,512]{3,2,1,0:T(8,128)S(1)}, u32[]{:S(2)}, u32[]{:S(2)}) %collective-permute-start.10) | collective-permute-done | bytes 65568 | tf_op jit(solution)/shard_map/ppermute | solution.py:301
  15.6 0.7 %last_merge.1 = f32[4,16,512]{2,1,0:T(8,128)} custom-call(f32[1,8,8,512]{3,2,1,0:T(8,128)S(1)} %first_merge.5.kept, f32[1,4,8,512]{3,2,1,0:T(8,128)S(1)} %collective-permute-done.4.rest_0_, f32[1,4,8,512]{3,2,1,0:T(8,128)S(1)} %collective-permute-done.10.rest_1_), custom_call_target="tpu_custom_call" | custom-call | tf_op jit(solution)/shard_map/last_merge/pallas_call | solution.py:246
  (10 shorter events, 0.1 us)
Async XLA Ops:
  1.3 7.1 %collective-permute-start = (f32[16,2048]{1,0:T(8,128)S(1)}, f32[16,2048]{1,0:T(8,128)S(1)}, u32[]{:S(2)}, u32[]{:S(2)}) collective-permute-start(f32[16,2048]{1,0:T(8,128)S(1)} %get-tuple-element.26), channel_id=1, source_target_pairs={{0,1},{1,0},{2,3},{3,2},{4,5},{5,4},{6,7},{7,6},{8,16},{9,17},{10,... | collective-permute-start | bytes 393224 | tf_op jit(solution)/shard_map/ppermute | solution.py:89
  4.3 4.1 %collective-permute-start.1 = (f32[16,2048]{1,0:T(8,128)S(1)}, f32[16,2048]{1,0:T(8,128)S(1)}, u32[]{:S(2)}, u32[]{:S(2)}) collective-permute-start(f32[16,2048]{1,0:T(8,128)S(1)} %get-tuple-element.27), channel_id=1, source_target_pairs={{0,8},{1,9},{2,10},{3,11},{4,12},{5,13},{6,14},{7,15},{8,0},{9,1},... | collective-permute-start | bytes 393224 | tf_op jit(solution)/shard_map/ppermute | solution.py:89
  4.4 3.9 %collective-permute-start.2 = (f32[4,2048]{1,0:T(4,128)S(1)}, f32[4,2048]{1,0:T(4,128)S(1)}, u32[]{:S(2)}, u32[]{:S(2)}) collective-permute-start(f32[4,2048]{1,0:T(4,128)S(1)} %get-tuple-element.32), channel_id=1, source_target_pairs={{0,1},{1,0},{2,3},{3,2},{4,5},{5,4},{6,7},{7,6},{8,9},{9,8},{10,11... | collective-permute-start | bytes 98312 | tf_op jit(solution)/shard_map/ppermute | solution.py:89
  5.9 2.9 %collective-permute-start.5 = (f32[4,2048]{1,0:T(4,128)S(1)}, f32[4,2048]{1,0:T(4,128)S(1)}, u32[]{:S(2)}, u32[]{:S(2)}) collective-permute-start(f32[4,2048]{1,0:T(4,128)S(1)} %get-tuple-element.35), channel_id=1, source_target_pairs={{0,8},{1,2},{2,1},{3,4},{4,3},{5,6},{6,5},{7,15},{8,0},{9,10},{10,... | collective-permute-start | bytes 98312 | tf_op jit(solution)/shard_map/ppermute | solution.py:89
  8.5 1.3 %collective-permute-start.3 = (f32[1,4,8,512]{3,2,1,0:T(8,128)S(1)}, f32[1,4,8,512]{3,2,1,0:T(8,128)S(1)}, u32[]{:S(2)}, u32[]{:S(2)}) collective-permute-start(f32[1,4,8,512]{3,2,1,0:T(8,128)S(1)} %shade.6), channel_id=1, source_target_pairs={{0,8},{8,0},{16,24},{24,16},{1,9},{9,1},{17,25},{25,17},{2,10},{10... | collective-permute-start | bytes 196616 | tf_op jit(solution)/shard_map/ppermute | solution.py:301
  8.9 2.1 %collective-permute-start.6 = (f32[1,4,8,512]{3,2,1,0:T(8,128)S(1)}, f32[1,4,8,512]{3,2,1,0:T(8,128)S(1)}, u32[]{:S(2)}, u32[]{:S(2)}) collective-permute-start(f32[1,4,8,512]{3,2,1,0:T(8,128)S(1)} %shade.8), channel_id=1, source_target_pairs={{0,8},{8,0},{16,24},{24,16},{1,9},{9,1},{17,25},{25,17},{2,10},{10... | collective-permute-start | bytes 196616 | tf_op jit(solution)/shard_map/ppermute | solution.py:301
  9.8 4.9 %collective-permute-start.4 = (f32[1,4,8,512]{3,2,1,0:T(8,128)S(1)}, f32[1,4,8,512]{3,2,1,0:T(8,128)S(1)}, u32[]{:S(2)}, u32[]{:S(2)}) collective-permute-start(f32[1,4,8,512]{3,2,1,0:T(8,128)S(1)} %first_merge.3), channel_id=1, source_target_pairs={{0,16},{8,24},{16,0},{24,8},{1,17},{9,25},{17,1},{25,9},{2,18},{10... | collective-permute-start | bytes 196616 | tf_op jit(solution)/shard_map/ppermute | solution.py:301
  11.0 4.6 %collective-permute-start.10 = (f32[1,4,8,512]{3,2,1,0:T(8,128)S(1)}, f32[1,4,8,512]{3,2,1,0:T(8,128)S(1)}, u32[]{:S(2)}, u32[]{:S(2)}) collective-permute-start(f32[1,4,8,512]{3,2,1,0:T(8,128)S(1)} %first_merge.4), channel_id=1, source_target_pairs={{0,16},{8,24},{16,0},{24,8},{1,17},{9,25},{17,1},{25,9},{2,18},{10... | collective-permute-start | bytes 196616 | tf_op jit(solution)/shard_map/ppermute | solution.py:301
  12.4 2.6 %collective-permute-start.7 = (f32[1,3,8,512]{3,2,1,0:T(8,128)S(1)}, f32[1,3,8,512]{3,2,1,0:T(8,128)S(1)}, u32[]{:S(2)}, u32[]{:S(2)}) collective-permute-start(f32[1,3,8,512]{3,2,1,0:T(8,128)S(1)} %get-tuple-element.41), channel_id=1, source_target_pairs={{0,8},{8,0},{16,24},{24,16},{1,9},{9,1},{17,25},{25,17},{2,10},{10... | collective-permute-start | bytes 147464 | tf_op jit(solution)/shard_map/ppermute | solution.py:301
  12.5 2.5 %collective-permute-start.8 = (f32[1,3,8,512]{3,2,1,0:T(8,128)S(1)}, f32[1,3,8,512]{3,2,1,0:T(8,128)S(1)}, u32[]{:S(2)}, u32[]{:S(2)}) collective-permute-start(f32[1,3,8,512]{3,2,1,0:T(8,128)S(1)} %get-tuple-element.42), channel_id=1, source_target_pairs={{0,8},{8,0},{16,24},{24,16},{1,9},{9,1},{17,25},{25,17},{2,10},{10... | collective-permute-start | bytes 147464 | tf_op jit(solution)/shard_map/ppermute | solution.py:301
  13.0 2.0 %collective-permute-start.9 = (f32[1,2,8,512]{3,2,1,0:T(8,128)S(1)}, f32[1,2,8,512]{3,2,1,0:T(8,128)S(1)}, u32[]{:S(2)}, u32[]{:S(2)}) collective-permute-start(f32[1,2,8,512]{3,2,1,0:T(8,128)S(1)} %get-tuple-element.43), channel_id=1, source_target_pairs={{0,8},{8,0},{16,24},{24,16},{1,9},{9,1},{17,25},{25,17},{2,10},{10... | collective-permute-start | bytes 98312 | tf_op jit(solution)/shard_map/ppermute | solution.py:301
